TPU v7x, 256 devices: a whole 4x4x8 slice. The times are simulated.
256 devices in a mesh: dom: 32 (over x, y, core), tm: 8 (over z).
Axes of the slice: x: 4, y: 4, z: 8, core: 2. Of those that a mesh axis runs over, the one named last changes fastest.
Arguments:
- features: bfloat16 [8, 8192, 512], P('tm', 'dom'), may hold values from -6 to 6
- tile_rows: int32 [8, 768], P('tm', 'dom'), may hold values from 0 to 63, as said below
- tile_cols: int32 [8, 768], P('tm', 'dom'), may hold values from 0 to 63, as said below
- tile_vals: bfloat16 [8, 768, 128, 128], P('tm', 'dom'), may hold values from 0 to 0.0625
- tile_used: int32 [8, 32], P('tm', 'dom'), may hold values from 12 to 24, as said below
- pool_weight: bfloat16 [512, 512], replicated, may hold values from -0.25 to 0.25
- w_in: bfloat16 [3, 512, 512], replicated, may hold values from -0.25 to 0.25
- w_state: bfloat16 [3, 512, 512], replicated, may hold values from -0.25 to 0.25
- gate_offset: float32 [512], replicated, may hold values from 0 to 5
- start_weight: float32 [512, 512], replicated, may hold values from -3 to 3
Outputs:
- hidden_out: bfloat16 [8, 8192, 512], P('tm', 'dom')
- weights_out: float32 [8, 512, 512], P('tm')
Inputs may be any that keep to these rules, and one draw needn't show every extreme that they name: `tile_rows`: every slot of row partition d names a row block of that partition, d * 2 to (d + 1) * 2 - 1. `tile_cols`: within one snapshot and one row partition, all slots whose column blocks lie on the same dom index name the same column block. `tile_used`: in every snapshot some row partition has all 24 slots live.
All inputs are finite; a program needn't handle non-finite values.
Results may differ from a plain program's by a relative error of at most 0.017.
Values may be sent and summed in bfloat16 or wider, within the bound.
No kernel may reach another device: no remote copies, remote signals or barrier semaphores. Data moves between devices by JAX's collectives and lax.ppermute only.
A program may use at most 64 MiB of HBM per device.

v0:
```python
import jax
import jax.numpy as jnp
from jax import lax
from jax.experimental import pallas as pl
from jax.experimental.pallas import tpu as pltpu
from jax.sharding import Mesh, PartitionSpec as P


BLOCK = 128
X, Y, C = 4, 4, 2
CHIPS = X * Y
F32 = jnp.float32
BF16 = jnp.bfloat16
VM = pltpu.MemorySpace.VMEM
SM = pltpu.MemorySpace.SMEM
NN = (((1,), (0,)), ((), ()))
NT = (((1,), (1,)), ((), ()))
TN = (((0,), (0,)), ((), ()))


def mm(a, b, dims):
    return lax.dot_general(a, b, dims, preferred_element_type=F32)


def vspec():
    return pl.BlockSpec(memory_space=VM)


def sspec():
    return pl.BlockSpec(memory_space=SM)


def call(kernel, out_shape, in_specs, scratch=(), flops=10**8, bytes_accessed=10**6, vmem_mib=8):
    many = isinstance(out_shape, (tuple, list))
    return pl.pallas_call(
        kernel,
        out_shape=out_shape,
        in_specs=in_specs,
        out_specs=tuple(vspec() for _ in out_shape) if many else vspec(),
        scratch_shapes=list(scratch),
        cost_estimate=pl.CostEstimate(flops=flops, bytes_accessed=bytes_accessed, transcendentals=0),
        compiler_params=pltpu.CompilerParams(vmem_limit_bytes=vmem_mib * 2**20),
    )


def pool_send_kernel(core_ref, feat_ref, pool_ref, send_ref):
    half = send_ref.shape[0]
    other = pl.multiple_of((1 - core_ref[0]) * half, half)
    gates = jax.nn.sigmoid(mm(feat_ref[...], pool_ref[:, pl.ds(other, half)], NN)).astype(BF16)
    send_ref[...] = mm(gates, feat_ref[...], TN).astype(BF16)


def pool_keep_kernel(core_ref, feat_ref, pool_ref, keep_ref):
    half = keep_ref.shape[0]
    own = pl.multiple_of(core_ref[0] * half, half)
    gates = jax.nn.sigmoid(mm(feat_ref[...], pool_ref[:, pl.ds(own, half)], NN)).astype(BF16)
    keep_ref[...] = mm(gates, feat_ref[...], TN)


def chain_kernel(meta_ref, summ_ref, w_in_ref, w_state_ref, offset_ref, start_ref, out_ref, side_ref, startt_ref):
    n_t, cols, width = summ_ref.shape
    summ = summ_ref[...].reshape(n_t * cols, width)
    for g in range(3):
        side = mm(summ, w_in_ref[g], NT)
        if g == 0:
            side = side - offset_ref[...]
        side_ref[g] = side.reshape(n_t, cols, width)
    startt_ref[...] = start_ref[...].T
    col0 = pl.multiple_of(meta_ref[1], cols)
    state = startt_ref[pl.ds(col0, cols), :]
    last = meta_ref[0]

    def step(t, state):
        state_b = state.astype(BF16)
        update = jax.nn.sigmoid(side_ref[0, t] + mm(state_b, w_state_ref[0], NT))
        reset = jax.nn.sigmoid(side_ref[1, t] + mm(state_b, w_state_ref[1], NT))
        cand = jnp.tanh(side_ref[2, t] + mm((reset * state).astype(BF16), w_state_ref[2], NT))
        return (1.0 - update) * state + update * cand

    state = lax.fori_loop(0, last + 1, step, state)
    out_ref[...] = jnp.broadcast_to(state.astype(BF16)[None], out_ref.shape)


def agg_kernel(own_idx, oth_idx, tiles_own, tiles_oth, feat_own, feat_oth, *refs):
    pieces, (agg_own, agg_oth, blocks, rhs, lhs, sems) = refs[:-6], refs[-6:]
    slots = tiles_own.shape[0]
    copies = []
    first = 0
    for n, piece in enumerate(pieces):
        cp = pltpu.make_async_copy(piece, blocks.at[pl.ds(first, piece.shape[0])], sems.at[n])
        cp.start()
        copies.append(cp)
        first += piece.shape[0]
    for p, (idx, tiles, feat, out) in enumerate(
        ((own_idx, tiles_own, feat_own, agg_own), (oth_idx, tiles_oth, feat_oth, agg_oth))
    ):
        for j in range(slots):
            tile = tiles[j]
            for r in range(2):
                on = idx[1, j] == r
                lhs[p, r * BLOCK : (r + 1) * BLOCK, j * BLOCK : (j + 1) * BLOCK] = jnp.where(
                    on, tile, jnp.zeros_like(tile)
                )
    for cp in copies:
        cp.wait()
    for p, (idx, feat, out) in enumerate(((own_idx, feat_own, agg_own), (oth_idx, feat_oth, agg_oth))):
        for j in range(slots):
            rhs[p, j * BLOCK : (j + 1) * BLOCK, :] = blocks[idx[0, j]]
        total = mm(lhs[p], rhs[p], NN)
        out[...] = (feat[...].astype(F32) + total).astype(BF16)


def final_kernel(core_ref, wt_own, wt_oth, agg_own, agg_oth, hid_ref, w_ref, wt, agg):
    half = wt_own.shape[0]
    own = pl.multiple_of(core_ref[0] * half, half)
    oth = pl.multiple_of((1 - core_ref[0]) * half, half)
    wt[pl.ds(own, half), :] = wt_own[...]
    wt[pl.ds(oth, half), :] = wt_oth[...]
    agg[:, pl.ds(own, half)] = agg_own[...]
    agg[:, pl.ds(oth, half)] = agg_oth[...]
    width = wt.shape[0]
    mixed = mm(agg[...], wt[...], NT)
    hid_ref[...] = jnp.maximum(mixed * width ** (-0.5), 0.0).astype(BF16)
    w_ref[...] = wt[...].astype(F32).T


def swap(x):
    return lax.ppermute(x, "c", [(0, 1), (1, 0)])


def trade(x, axes):
    return lax.all_to_all(x, axes, split_axis=0, concat_axis=0, tiled=True)


def shift(x, axis, distance):
    size = lax.axis_size(axis)
    return lax.ppermute(x, axis, [(i, (i + distance) % size) for i in range(size)])


def spread(x, axis):
    below = shift(x, axis, 1)
    above = shift(x, axis, -1)
    part = x.shape[0] // 2
    low = shift(below[:part], axis, 1)
    high = shift(above[part:], axis, -1)
    return [x, below, above, low, high]


def slot_of(there, here):
    step = (there - here) % 4
    return jnp.where(step == 0, 0, jnp.where(step == 3, 1, step + 1))


def layer(
    features,
    tile_rows,
    tile_cols,
    tile_vals,
    tile_used,
    pool_weight,
    w_in,
    w_state,
    gate_offset,
    start_weight,
):
    rows_dev, width = features.shape[1:]
    slots = tile_rows.shape[1]
    half = width // 2
    n_tm = lax.axis_size("z")
    core = lax.axis_index("c").astype(jnp.int32)
    chip = (lax.axis_index("x") * Y + lax.axis_index("y")).astype(jnp.int32)
    dom = chip * C + core
    t_index = lax.axis_index("z").astype(jnp.int32)
    core_s = core.reshape(1)
    feat = features[0]
    blocks_dev = rows_dev // BLOCK

    bf_half = jax.ShapeDtypeStruct((half, width), BF16)
    send = call(pool_send_kernel, bf_half, [sspec(), vspec(), vspec()])(core_s, feat, pool_weight)
    keep = call(
        pool_keep_kernel, jax.ShapeDtypeStruct((half, width), F32), [sspec(), vspec(), vspec()]
    )(core_s, feat, pool_weight)
    partial = (keep + swap(send).astype(F32)).astype(BF16)
    cols = half // CHIPS
    parts = trade(partial.reshape(CHIPS, cols, width), ("x", "y"))
    summ = (jnp.sum(parts.astype(F32), axis=0) * (rows_dev * CHIPS * C) ** (-0.5)).astype(BF16)
    summ = trade(jnp.broadcast_to(summ[None], (n_tm, cols, width)), "z")

    feat_mine = lax.dynamic_slice_in_dim(feat, core * half, half, 1)
    feat_send = lax.dynamic_slice_in_dim(feat, (1 - core) * half, half, 1)
    feat_oth = swap(feat_send)
    blocks_a = spread(feat_mine.reshape(blocks_dev, BLOCK, half), "x")
    blocks_b = spread(feat_oth.reshape(blocks_dev, BLOCK, half), "y")
    blocks_a = spread(jnp.concatenate(blocks_a), "y")
    blocks_b = spread(jnp.concatenate(blocks_b), "x")
    gathered = blocks_a + blocks_b

    live = jnp.arange(slots, dtype=jnp.int32) < tile_used[0, 0]
    where_to = jnp.where(live, tile_rows[0] - dom * blocks_dev, blocks_dev)
    own_idx = jnp.stack([tile_cols[0], where_to])
    oth_idx = swap(own_idx)

    def place(idx):
        owner, block = idx[0] // blocks_dev, idx[0] % blocks_dev
        in_x = slot_of(owner // (Y * C), lax.axis_index("x"))
        in_y = slot_of((owner // C) % Y, lax.axis_index("y"))
        in_a = (in_y * 4 + in_x) * blocks_dev + block
        in_b = (in_x * 4 + in_y) * blocks_dev + block + CHIPS * blocks_dev
        return jnp.stack([jnp.where(owner % C == core, in_a, in_b), idx[1]])

    tiles_own = tile_vals[0]
    tiles_oth = swap(tiles_own)
    agg_shape = jax.ShapeDtypeStruct((rows_dev, half), BF16)
    agg_own, agg_send = call(
        agg_kernel,
        (agg_shape, agg_shape),
        [sspec(), sspec(), vspec(), vspec(), vspec(), vspec()] + [pl.BlockSpec(memory_space=pl.ANY)] * len(gathered),
        scratch=[
            pltpu.VMEM((CHIPS * C * blocks_dev, BLOCK, half), BF16),
            pltpu.VMEM((2, slots * BLOCK, half), BF16),
            pltpu.VMEM((2, rows_dev, slots * BLOCK), BF16),
            pltpu.SemaphoreType.DMA((len(gathered),)),
        ],
        vmem_mib=20,
    )(place(own_idx), place(oth_idx), tiles_own, tiles_oth, feat_mine, feat_oth, *gathered)
    agg_oth = swap(agg_send)

    col0 = core * half + chip * cols
    lane0 = col0 // BLOCK
    start_cols = lax.dynamic_slice_in_dim(start_weight, lane0 * BLOCK, BLOCK, 1)
    meta = jnp.stack([t_index, col0 % BLOCK])
    evolved = call(
        chain_kernel,
        jax.ShapeDtypeStruct((CHIPS, cols, width), BF16),
        [sspec(), vspec(), vspec(), vspec(), vspec(), vspec()],
        scratch=[pltpu.VMEM((3, n_tm, cols, width), F32), pltpu.VMEM((BLOCK, width), F32)],
        vmem_mib=12,
    )(meta, summ, w_in, w_state, gate_offset[None, :], start_cols)
    wt_own = trade(evolved, ("x", "y")).reshape(half, width)
    wt_oth = swap(wt_own)
    hidden, weights = call(
        final_kernel,
        (jax.ShapeDtypeStruct((rows_dev, width), BF16), jax.ShapeDtypeStruct((width, width), F32)),
        [sspec(), vspec(), vspec(), vspec(), vspec()],
        scratch=[pltpu.VMEM((width, width), BF16), pltpu.VMEM((rows_dev, width), BF16)],
    )(core_s, wt_own, wt_oth, agg_own, agg_oth)
    return hidden[None], weights[None]


def solution(mesh):
    n_tm = mesh.shape["tm"]
    fine = Mesh(mesh.devices.reshape(X, Y, C, n_tm), ("x", "y", "c", "z"))
    dom = ("x", "y", "c")
    in_specs = (
        P("z", dom, None),
        P("z", dom),
        P("z", dom),
        P("z", dom, None, None),
        P("z", dom),
        P(),
        P(),
        P(),
        P(),
        P(),
    )
    out_specs = (P("z", dom, None), P("z", None, None))
    return jax.shard_map(layer, mesh=fine, in_specs=in_specs, out_specs=out_specs, check_vma=False)
```

profile of v0, /device:TPU:1, one launch (start us, length us, event | category | flops | bytes accessed | tf_op | source)
XLA Modules:
  0.0 103.7 jit_solution(4491845817396277408)
XLA Ops:
  1.8 2.1 %collective-permute-start.5 = (bf16[2,128,256]{2,1,0:T(8,128)(2,1)S(1)}, bf16[2,128,256]{2,1,0:T(8,128)(2,1)S(1)}, u32[]{:S(2)}, u32[]{:S(2)}) collective-permute-start(bf16[2,128,256]{2,1,0:T(8,128)(2,1)S(1)} %bitcast.19), channel_id=1, source_target_pairs={{0,64},{64,128},{128,192},{192,0},{1,65},{65,129},{129,193},{193,1... | collective-permute-start | bytes 393224 | tf_op jit(solution)/shard_map/ppermute | solution.py:137
  5.2 3.0 %collective-permute-start.4 = (bf16[256,256]{1,0:T(8,128)(2,1)S(1)}, bf16[256,256]{1,0:T(8,128)(2,1)S(1)}, u32[]{:S(2)}, u32[]{:S(2)}) collective-permute-start(bf16[256,256]{1,0:T(8,128)(2,1)S(1)} %get-tuple-element.10), channel_id=1, source_target_pairs={{0,8},{8,0},{1,9},{9,1},{2,10},{10,2},{3,11},{11,3},{4,12},{12,4},... | collective-permute-start | bytes 393224 | tf_op jit(solution)/shard_map/ppermute | solution.py:128
  14.9 2.7 %collective-permute-start.14 = (bf16[2,128,256]{2,1,0:T(8,128)(2,1)S(1)}, bf16[2,128,256]{2,1,0:T(8,128)(2,1)S(1)}, u32[]{:S(2)}, u32[]{:S(2)}) collective-permute-start(bf16[2,128,256]{2,1,0:T(8,128)(2,1)S(1)} %bitcast.29), channel_id=1, source_target_pairs={{0,48},{16,0},{32,16},{48,32},{1,49},{17,1},{33,17},{49,33},{2,50}... | collective-permute-start | bytes 393224 | tf_op jit(solution)/shard_map/ppermute | solution.py:137
  18.9 3.7 %collective-permute-done.7 = bf16[1,128,256]{2,1,0:T(8,128)(2,1)S(1)} collective-permute-done((bf16[1,128,256]{2,1,0:T(8,128)(2,1)S(1)}, bf16[1,128,256]{2,1,0:T(8,128)(2,1)S(1)}, u32[]{:S(2)}, u32[]{:S(2)}) %collective-permute-start.7) | collective-permute-done | bytes 65568 | tf_op jit(solution)/shard_map/ppermute | solution.py:137
  23.2 2.5 %collective-permute-done.8 = bf16[1,128,256]{2,1,0:T(8,128)(2,1)S(1)} collective-permute-done((bf16[1,128,256]{2,1,0:T(8,128)(2,1)S(1)}, bf16[1,128,256]{2,1,0:T(8,128)(2,1)S(1)}, u32[]{:S(2)}, u32[]{:S(2)}) %collective-permute-start.8) | collective-permute-done | bytes 65568 | tf_op jit(solution)/shard_map/ppermute | solution.py:137
  26.3 2.7 %collective-permute-start.10 = (bf16[8,128,256]{2,1,0:T(8,128)(2,1)}, bf16[8,128,256]{2,1,0:T(8,128)(2,1)}, u32[]{:S(2)}, u32[]{:S(2)}) collective-permute-start(bf16[8,128,256]{2,1,0:T(8,128)(2,1)} %constant_dynamic-update-slice_fusion.refs_0_), channel_id=1, source_target_pairs={{0,48},{16,0},{32,16},{48,32},{1,49},{17,1},{33,17},{49,33},{2,50}... | collective-permute-start | bytes 1572872 | tf_op jit(solution)/shard_map/ppermute | solution.py:137
  30.9 2.1 %collective-permute-start.16 = (bf16[1,128,256]{2,1,0:T(8,128)(2,1)}, bf16[1,128,256]{2,1,0:T(8,128)(2,1)}, u32[]{:S(2)}, u32[]{:S(2)}) collective-permute-start(bf16[1,128,256]{2,1,0:T(8,128)(2,1)} %slice.46), channel_id=1, source_target_pairs={{0,48},{16,0},{32,16},{48,32},{1,49},{17,1},{33,17},{49,33},{2,50}... | collective-permute-start | bytes 196616 | tf_op jit(solution)/shard_map/ppermute | solution.py:137
  33.0 1.7 %add_convert_fusion = bf16[256,512]{1,0:T(8,128)(2,1)} fusion(f32[256,512]{1,0:T(8,128)S(1)} %shard_map.113, bf16[256,512]{1,0:T(8,128)(2,1)} %collective-permute-done), kind=kLoop, calls=%fused_computation.1 | loop fusion | flops 393216 | bytes 1048576 | tf_op jit(solution)/shard_map/convert_element_type | solution.py:183
  34.8 4.2 %all-to-all-start = ((bf16[16,16,512]{2,1,0:T(8,128)(2,1)}), bf16[16,16,512]{2,1,0:T(8,128)(2,1)}, u32[]{:S(2)}, u32[]{:S(2)}) async-start(bf16[16,16,512]{2,1,0:T(8,128)(2,1)} %bitcast.31), calls=%async_computation | async-start | bytes 524288 | tf_op jit(solution)/shard_map/all_to_all | solution.py:132
  40.5 1.6 %constant_dynamic-update-slice_fusion.7 = bf16[8,128,256]{2,1,0:T(8,128)(2,1)} fusion(bf16[8,128,256]{2,1,0:T(8,128)(2,1)} %constant_dynamic-update-slice_fusion.8, bf16[2,128,256]{2,1,0:T(8,128)(2,1)} %copy-done.14), kind=kLoop, calls=%fused_computation.11 | loop fusion | bytes 262144
  43.6 2.7 %all-to-all-done = bf16[16,16,512]{2,1,0:T(8,128)(2,1)} async-done(((bf16[16,16,512]{2,1,0:T(8,128)(2,1)}), bf16[16,16,512]{2,1,0:T(8,128)(2,1)}, u32[]{:S(2)}, u32[]{:S(2)}) %all-to-all-start) | async-done | bytes 262176 | tf_op jit(solution)/shard_map/all_to_all | solution.py:132
  48.0 6.5 %all-to-all-start.1 = ((bf16[8,16,512]{2,1,0:T(8,128)(2,1)}), bf16[8,16,512]{2,1,0:T(8,128)(2,1)}, u32[]{:S(2)}, u32[]{:S(2)}) async-start(bf16[8,16,512]{2,1,0:T(8,128)(2,1)} %broadcast_in_dim.26), calls=%async_computation.1 | async-start | bytes 262144 | tf_op jit(solution)/shard_map/all_to_all | solution.py:132
  56.0 2.7 %collective-permute-start.18 = (bf16[8,128,256]{2,1,0:T(8,128)(2,1)}, bf16[8,128,256]{2,1,0:T(8,128)(2,1)}, u32[]{:S(2)}, u32[]{:S(2)}) collective-permute-start(bf16[8,128,256]{2,1,0:T(8,128)(2,1)} %constant_dynamic-update-slice_fusion.5.refs_5_), channel_id=1, source_target_pairs={{0,192},{64,0},{128,64},{192,128},{1,193},{65,1},{129,65},{193,129... | collective-permute-start | bytes 1572872 | tf_op jit(solution)/shard_map/ppermute | solution.py:137
  58.7 3.8 %all-to-all-done.1.summ_ref = bf16[8,16,512]{2,1,0:T(8,128)(2,1)} async-done(((bf16[8,16,512]{2,1,0:T(8,128)(2,1)}), bf16[8,16,512]{2,1,0:T(8,128)(2,1)}, u32[]{:S(2)}, u32[]{:S(2)}) %all-to-all-start.1) | async-done | bytes 131104 | tf_op jit(solution)/shard_map/all_to_all | solution.py:132
  64.0 2.2 %shard_map.115 = bf16[16,16,512]{2,1,0:T(8,128)(2,1)S(1)} custom-call(s32[2]{0:T(128)S(1)} %pad_add_fusion.3.meta_ref, bf16[8,16,512]{2,1,0:T(8,128)(2,1)} %all-to-all-done.1.summ_ref, bf16[3,512,512]{2,1,0:T(8,128)(2,1)S(1)} %copy-done.5, bf16[3,512,512]{2,1,0:T(8,128)(2,1)S(1)} %copy-done.6, f32[1,512]{1,0:T(1,128)S(1)} %bitcast.30, ...), custom_call_target="tpu_custom_call" | custom-call | flops 100000000 | bytes 1000000 | tf_op jit(solution)/shard_map/pallas_call | solution.py:232
  66.9 3.9 %all-to-all-start.2 = ((bf16[16,16,512]{2,1,0:T(8,128)(2,1)}), bf16[16,16,512]{2,1,0:T(8,128)(2,1)S(1)}, u32[]{:S(2)}, u32[]{:S(2)}) async-start(bf16[16,16,512]{2,1,0:T(8,128)(2,1)} %copy-done.7), calls=%async_computation.2 | async-start | bytes 524288 | tf_op jit(solution)/shard_map/all_to_all | solution.py:132
  71.5 6.4 %collective-permute-start.2 = (s32[2,24]{1,0:T(2,128)S(1)}, s32[2,24]{1,0:T(2,128)S(1)}, u32[]{:S(2)}, u32[]{:S(2)}) collective-permute-start(s32[2,24]{1,0:T(2,128)S(1)} %get-tuple-element.14), channel_id=1, source_target_pairs={{0,8},{8,0},{1,9},{9,1},{2,10},{10,2},{3,11},{11,3},{4,12},{12,4},... | collective-permute-start | bytes 584 | tf_op jit(solution)/shard_map/ppermute | solution.py:128
  78.7 1.6 %collective-permute-start.11 = (bf16[4,128,256]{2,1,0:T(8,128)(2,1)}, bf16[4,128,256]{2,1,0:T(8,128)(2,1)}, u32[]{:S(2)}, u32[]{:S(2)}) collective-permute-start(bf16[4,128,256]{2,1,0:T(8,128)(2,1)} %slice.43), channel_id=1, source_target_pairs={{0,16},{16,32},{32,48},{48,0},{1,17},{17,33},{33,49},{49,1},{2,18}... | collective-permute-start | bytes 786440 | tf_op jit(solution)/shard_map/ppermute | solution.py:137
  80.3 1.7 %slice.44 = bf16[4,128,256]{2,1,0:T(8,128)(2,1)} slice(bf16[8,128,256]{2,1,0:T(8,128)(2,1)} %collective-permute-done.10.refs_2_), slice={[4:8], [0:128], [0:256]} | slice | bytes 524288 | tf_op jit(solution)/shard_map/slice | solution.py:145
  83.2 1.7 %slice.47 = bf16[4,128,256]{2,1,0:T(8,128)(2,1)} slice(bf16[8,128,256]{2,1,0:T(8,128)(2,1)} %collective-permute-done.17.refs_6_), slice={[0:4], [0:128], [0:256]} | slice | bytes 524288 | tf_op jit(solution)/shard_map/slice | solution.py:144
  86.4 1.7 %slice.48 = bf16[4,128,256]{2,1,0:T(8,128)(2,1)} slice(bf16[8,128,256]{2,1,0:T(8,128)(2,1)} %collective-permute-done.18.refs_7_), slice={[4:8], [0:128], [0:256]} | slice | bytes 524288 | tf_op jit(solution)/shard_map/slice | solution.py:145
  90.3 3.6 %collective-permute-done.19.refs_8_ = bf16[4,128,256]{2,1,0:T(8,128)(2,1)} collective-permute-done((bf16[4,128,256]{2,1,0:T(8,128)(2,1)}, bf16[4,128,256]{2,1,0:T(8,128)(2,1)}, u32[]{:S(2)}, u32[]{:S(2)}) %collective-permute-start.19) | collective-permute-done | bytes 262176 | tf_op jit(solution)/shard_map/ppermute | solution.py:137
  95.4 4.1 %shard_map.116 = (bf16[256,256]{1,0:T(8,128)(2,1)S(1)}, bf16[256,256]{1,0:T(8,128)(2,1)S(1)}) custom-call(s32[2,24]{1,0:T(2,128)S(1)} %get-tuple-element.15.own_idx, s32[2,24]{1,0:T(2,128)S(1)} %pad_add_fusion.2.oth_idx, bf16[24,128,128]{2,1,0:T(8,128)(2,1)S(1)} %bitcast.26, bf16[24,128,128]{2,1,0:T(8,128)(2,1)} %collective-permute-done.3.tiles_oth, ...), custom_call_target="tpu_custom_call" | custom-call | flops 100000000 | bytes 1000000 | tf_op jit(solution)/shard_map/pallas_call | solution.py:214
  99.5 1.8 %collective-permute-start.21 = (bf16[256,256]{1,0:T(8,128)(2,1)S(1)}, bf16[256,256]{1,0:T(8,128)(2,1)S(1)}, u32[]{:S(2)}, u32[]{:S(2)}) collective-permute-start(bf16[256,256]{1,0:T(8,128)(2,1)S(1)} %get-tuple-element.7), channel_id=1, source_target_pairs={{0,8},{8,0},{1,9},{9,1},{2,10},{10,2},{3,11},{11,3},{4,12},{12,4},... | collective-permute-start | bytes 393224 | tf_op jit(solution)/shard_map/ppermute | solution.py:128
  (93 shorter events, 31.4 us)
Async XLA Ops:
  1.8 13.1 %collective-permute-start.5 = (bf16[2,128,256]{2,1,0:T(8,128)(2,1)S(1)}, bf16[2,128,256]{2,1,0:T(8,128)(2,1)S(1)}, u32[]{:S(2)}, u32[]{:S(2)}) collective-permute-start(bf16[2,128,256]{2,1,0:T(8,128)(2,1)S(1)} %bitcast.19), channel_id=1, source_target_pairs={{0,64},{64,128},{128,192},{192,0},{1,65},{65,129},{129,193},{193,1... | collective-permute-start | bytes 393224 | tf_op jit(solution)/shard_map/ppermute | solution.py:137
  3.9 14.4 %collective-permute-start.6 = (bf16[2,128,256]{2,1,0:T(8,128)(2,1)S(1)}, bf16[2,128,256]{2,1,0:T(8,128)(2,1)S(1)}, u32[]{:S(2)}, u32[]{:S(2)}) collective-permute-start(bf16[2,128,256]{2,1,0:T(8,128)(2,1)S(1)} %bitcast.20), channel_id=1, source_target_pairs={{0,192},{64,0},{128,64},{192,128},{1,193},{65,1},{129,65},{193,129... | collective-permute-start | bytes 393224 | tf_op jit(solution)/shard_map/ppermute | solution.py:137
  5.2 8.9 %collective-permute-start.4 = (bf16[256,256]{1,0:T(8,128)(2,1)S(1)}, bf16[256,256]{1,0:T(8,128)(2,1)S(1)}, u32[]{:S(2)}, u32[]{:S(2)}) collective-permute-start(bf16[256,256]{1,0:T(8,128)(2,1)S(1)} %get-tuple-element.10), channel_id=1, source_target_pairs={{0,8},{8,0},{1,9},{9,1},{2,10},{10,2},{3,11},{11,3},{4,12},{12,4},... | collective-permute-start | bytes 393224 | tf_op jit(solution)/shard_map/ppermute | solution.py:128
  8.3 81.0 %collective-permute-start.3 = (bf16[24,128,128]{2,1,0:T(8,128)(2,1)}, bf16[24,128,128]{2,1,0:T(8,128)(2,1)}, u32[]{:S(2)}, u32[]{:S(2)}) collective-permute-start(bf16[24,128,128]{2,1,0:T(8,128)(2,1)} %bitcast.25), channel_id=1, source_target_pairs={{0,8},{8,0},{1,9},{9,1},{2,10},{10,2},{3,11},{11,3},{4,12},{12,4},... | collective-permute-start | bytes 2359304 | tf_op jit(solution)/shard_map/ppermute | solution.py:128
  11.6 19.4 %collective-permute-start = (bf16[256,512]{1,0:T(8,128)(2,1)}, bf16[256,512]{1,0:T(8,128)(2,1)}, u32[]{:S(2)}, u32[]{:S(2)}) collective-permute-start(bf16[256,512]{1,0:T(8,128)(2,1)} %shard_map.114), channel_id=1, source_target_pairs={{0,8},{8,0},{1,9},{9,1},{2,10},{10,2},{3,11},{11,3},{4,12},{12,4},... | collective-permute-start | bytes 786440 | tf_op jit(solution)/shard_map/ppermute | solution.py:128
  14.1 12.2 %collective-permute-start.13 = (bf16[2,128,256]{2,1,0:T(8,128)(2,1)S(1)}, bf16[2,128,256]{2,1,0:T(8,128)(2,1)S(1)}, u32[]{:S(2)}, u32[]{:S(2)}) collective-permute-start(bf16[2,128,256]{2,1,0:T(8,128)(2,1)S(1)} %bitcast.27), channel_id=1, source_target_pairs={{0,16},{16,32},{32,48},{48,0},{1,17},{17,33},{33,49},{49,1},{2,18}... | collective-permute-start | bytes 393224 | tf_op jit(solution)/shard_map/ppermute | solution.py:137
  14.9 14.7 %collective-permute-start.14 = (bf16[2,128,256]{2,1,0:T(8,128)(2,1)S(1)}, bf16[2,128,256]{2,1,0:T(8,128)(2,1)S(1)}, u32[]{:S(2)}, u32[]{:S(2)}) collective-permute-start(bf16[2,128,256]{2,1,0:T(8,128)(2,1)S(1)} %bitcast.29), channel_id=1, source_target_pairs={{0,48},{16,0},{32,16},{48,32},{1,49},{17,1},{33,17},{49,33},{2,50}... | collective-permute-start | bytes 393224 | tf_op jit(solution)/shard_map/ppermute | solution.py:137
  18.2 4.3 %collective-permute-start.7 = (bf16[1,128,256]{2,1,0:T(8,128)(2,1)S(1)}, bf16[1,128,256]{2,1,0:T(8,128)(2,1)S(1)}, u32[]{:S(2)}, u32[]{:S(2)}) collective-permute-start(bf16[1,128,256]{2,1,0:T(8,128)(2,1)S(1)} %slice.41), channel_id=1, source_target_pairs={{0,64},{64,128},{128,192},{192,0},{1,65},{65,129},{129,193},{193,1... | collective-permute-start | bytes 196616 | tf_op jit(solution)/shard_map/ppermute | solution.py:137
  22.5 3.1 %collective-permute-start.8 = (bf16[1,128,256]{2,1,0:T(8,128)(2,1)S(1)}, bf16[1,128,256]{2,1,0:T(8,128)(2,1)S(1)}, u32[]{:S(2)}, u32[]{:S(2)}) collective-permute-start(bf16[1,128,256]{2,1,0:T(8,128)(2,1)S(1)} %slice.42), channel_id=1, source_target_pairs={{0,192},{64,0},{128,64},{192,128},{1,193},{65,1},{129,65},{193,129... | collective-permute-start | bytes 196616 | tf_op jit(solution)/shard_map/ppermute | solution.py:137
  26.3 45.2 %collective-permute-start.9 = (bf16[8,128,256]{2,1,0:T(8,128)(2,1)}, bf16[8,128,256]{2,1,0:T(8,128)(2,1)S(1)}, u32[]{:S(2)}, u32[]{:S(2)}) collective-permute-start(bf16[8,128,256]{2,1,0:T(8,128)(2,1)} %constant_dynamic-update-slice_fusion.refs_0_), channel_id=1, source_target_pairs={{0,16},{16,32},{32,48},{48,0},{1,17},{17,33},{33,49},{49,1},{2,18}... | collective-permute-start | bytes 1572872 | tf_op jit(solution)/shard_map/ppermute | solution.py:137
  26.3 52.4 %collective-permute-start.10 = (bf16[8,128,256]{2,1,0:T(8,128)(2,1)}, bf16[8,128,256]{2,1,0:T(8,128)(2,1)}, u32[]{:S(2)}, u32[]{:S(2)}) collective-permute-start(bf16[8,128,256]{2,1,0:T(8,128)(2,1)} %constant_dynamic-update-slice_fusion.refs_0_), channel_id=1, source_target_pairs={{0,48},{16,0},{32,16},{48,32},{1,49},{17,1},{33,17},{49,33},{2,50}... | collective-permute-start | bytes 1572872 | tf_op jit(solution)/shard_map/ppermute | solution.py:137
  29.6 12.5 %collective-permute-start.15 = (bf16[1,128,256]{2,1,0:T(8,128)(2,1)}, bf16[1,128,256]{2,1,0:T(8,128)(2,1)}, u32[]{:S(2)}, u32[]{:S(2)}) collective-permute-start(bf16[1,128,256]{2,1,0:T(8,128)(2,1)} %slice.45), channel_id=1, source_target_pairs={{0,16},{16,32},{32,48},{48,0},{1,17},{17,33},{33,49},{49,1},{2,18}... | collective-permute-start | bytes 196616 | tf_op jit(solution)/shard_map/ppermute | solution.py:137
  30.9 23.6 %collective-permute-start.16 = (bf16[1,128,256]{2,1,0:T(8,128)(2,1)}, bf16[1,128,256]{2,1,0:T(8,128)(2,1)}, u32[]{:S(2)}, u32[]{:S(2)}) collective-permute-start(bf16[1,128,256]{2,1,0:T(8,128)(2,1)} %slice.46), channel_id=1, source_target_pairs={{0,48},{16,0},{32,16},{48,32},{1,49},{17,1},{33,17},{49,33},{2,50}... | collective-permute-start | bytes 196616 | tf_op jit(solution)/shard_map/ppermute | solution.py:137
  34.8 11.5 %all-to-all-start = ((bf16[16,16,512]{2,1,0:T(8,128)(2,1)}), bf16[16,16,512]{2,1,0:T(8,128)(2,1)}, u32[]{:S(2)}, u32[]{:S(2)}) async-start(bf16[16,16,512]{2,1,0:T(8,128)(2,1)} %bitcast.31), calls=%async_computation | async-start | bytes 524288 | tf_op jit(solution)/shard_map/all_to_all | solution.py:132
  48.0 14.6 %all-to-all-start.1 = ((bf16[8,16,512]{2,1,0:T(8,128)(2,1)}), bf16[8,16,512]{2,1,0:T(8,128)(2,1)}, u32[]{:S(2)}, u32[]{:S(2)}) async-start(bf16[8,16,512]{2,1,0:T(8,128)(2,1)} %broadcast_in_dim.26), calls=%async_computation.1 | async-start | bytes 262144 | tf_op jit(solution)/shard_map/all_to_all | solution.py:132
  56.0 26.0 %collective-permute-start.17 = (bf16[8,128,256]{2,1,0:T(8,128)(2,1)}, bf16[8,128,256]{2,1,0:T(8,128)(2,1)}, u32[]{:S(2)}, u32[]{:S(2)}) collective-permute-start(bf16[8,128,256]{2,1,0:T(8,128)(2,1)} %constant_dynamic-update-slice_fusion.5.refs_5_), channel_id=1, source_target_pairs={{0,64},{64,128},{128,192},{192,0},{1,65},{65,129},{129,193},{193,1... | collective-permute-start | bytes 1572872 | tf_op jit(solution)/shard_map/ppermute | solution.py:137
  56.0 28.9 %collective-permute-start.18 = (bf16[8,128,256]{2,1,0:T(8,128)(2,1)}, bf16[8,128,256]{2,1,0:T(8,128)(2,1)}, u32[]{:S(2)}, u32[]{:S(2)}) collective-permute-start(bf16[8,128,256]{2,1,0:T(8,128)(2,1)} %constant_dynamic-update-slice_fusion.5.refs_5_), channel_id=1, source_target_pairs={{0,192},{64,0},{128,64},{192,128},{1,193},{65,1},{129,65},{193,129... | collective-permute-start | bytes 1572872 | tf_op jit(solution)/shard_map/ppermute | solution.py:137
  66.9 22.4 %all-to-all-start.2 = ((bf16[16,16,512]{2,1,0:T(8,128)(2,1)}), bf16[16,16,512]{2,1,0:T(8,128)(2,1)S(1)}, u32[]{:S(2)}, u32[]{:S(2)}) async-start(bf16[16,16,512]{2,1,0:T(8,128)(2,1)} %copy-done.7), calls=%async_computation.2 | async-start | bytes 524288 | tf_op jit(solution)/shard_map/all_to_all | solution.py:132
  71.5 16.6 %collective-permute-start.2 = (s32[2,24]{1,0:T(2,128)S(1)}, s32[2,24]{1,0:T(2,128)S(1)}, u32[]{:S(2)}, u32[]{:S(2)}) collective-permute-start(s32[2,24]{1,0:T(2,128)S(1)} %get-tuple-element.14), channel_id=1, source_target_pairs={{0,8},{8,0},{1,9},{9,1},{2,10},{10,2},{3,11},{11,3},{4,12},{12,4},... | collective-permute-start | bytes 584 | tf_op jit(solution)/shard_map/ppermute | solution.py:128
  78.7 11.6 %collective-permute-start.11 = (bf16[4,128,256]{2,1,0:T(8,128)(2,1)}, bf16[4,128,256]{2,1,0:T(8,128)(2,1)}, u32[]{:S(2)}, u32[]{:S(2)}) collective-permute-start(bf16[4,128,256]{2,1,0:T(8,128)(2,1)} %slice.43), channel_id=1, source_target_pairs={{0,16},{16,32},{32,48},{48,0},{1,17},{17,33},{33,49},{49,1},{2,18}... | collective-permute-start | bytes 786440 | tf_op jit(solution)/shard_map/ppermute | solution.py:137
  82.0 8.3 %collective-permute-start.12 = (bf16[4,128,256]{2,1,0:T(8,128)(2,1)}, bf16[4,128,256]{2,1,0:T(8,128)(2,1)}, u32[]{:S(2)}, u32[]{:S(2)}) collective-permute-start(bf16[4,128,256]{2,1,0:T(8,128)(2,1)} %slice.44), channel_id=1, source_target_pairs={{0,48},{16,0},{32,16},{48,32},{1,49},{17,1},{33,17},{49,33},{2,50}... | collective-permute-start | bytes 786440 | tf_op jit(solution)/shard_map/ppermute | solution.py:137
  84.9 9.0 %collective-permute-start.19 = (bf16[4,128,256]{2,1,0:T(8,128)(2,1)}, bf16[4,128,256]{2,1,0:T(8,128)(2,1)}, u32[]{:S(2)}, u32[]{:S(2)}) collective-permute-start(bf16[4,128,256]{2,1,0:T(8,128)(2,1)} %slice.47), channel_id=1, source_target_pairs={{0,64},{64,128},{128,192},{192,0},{1,65},{65,129},{129,193},{193,1... | collective-permute-start | bytes 786440 | tf_op jit(solution)/shard_map/ppermute | solution.py:137
  88.1 7.3 %collective-permute-start.20 = (bf16[4,128,256]{2,1,0:T(8,128)(2,1)}, bf16[4,128,256]{2,1,0:T(8,128)(2,1)}, u32[]{:S(2)}, u32[]{:S(2)}) collective-permute-start(bf16[4,128,256]{2,1,0:T(8,128)(2,1)} %slice.48), channel_id=1, source_target_pairs={{0,192},{64,0},{128,64},{192,128},{1,193},{65,1},{129,65},{193,129... | collective-permute-start | bytes 786440 | tf_op jit(solution)/shard_map/ppermute | solution.py:137
  89.3 13.0 %collective-permute-start.1 = (bf16[256,512]{1,0:T(8,128)(2,1)S(1)}, bf16[256,512]{1,0:T(8,128)(2,1)S(1)}, u32[]{:S(2)}, u32[]{:S(2)}) collective-permute-start(bf16[256,512]{1,0:T(8,128)(2,1)S(1)} %bitcast.23), channel_id=1, source_target_pairs={{0,8},{8,0},{1,9},{9,1},{2,10},{10,2},{3,11},{11,3},{4,12},{12,4},... | collective-permute-start | bytes 786440 | tf_op jit(solution)/shard_map/ppermute | solution.py:128
  (17 other events, 230.6 us)
where the time goes:
time: 105 us; the launch traced here: 104 us
  starting transfers between devices  46.7 us (44%)
  local copies, waits for them, and re-layouts  23.6 us (22%)
  waiting for transfers between devices  18.8 us (18%)
  Pallas kernels  9.5 us (9%)
  other arithmetic  3.57 us (3%)
  between operations  1.51 us (1%)
    ppermute x16, starting transfers between devices, shift(): lax.ppermute(x, axis, [(i, (i + distance) % size) for i in range(size)])  19.2 us
    all_to_all x3, starting transfers between devices, trade(): return lax.all_to_all(x, axes, split_axis=0, concat_axis=0, tiled=True)  14.7 us
    ppermute x6, starting transfers between devices, swap(): return lax.ppermute(x, 'c', [(0, 1), (1, 0)])  12.8 us
    unnamed x40, local copies, waits for them, and re-layouts  12.7 us
    ppermute x16, waiting for transfers between devices, shift(): lax.ppermute(x, axis, [(i, (i + distance) % size) for i in range(size)])  11.2 us
    all_to_all x3, waiting for transfers between devices, trade(): return lax.all_to_all(x, axes, split_axis=0, concat_axis=0, tiled=True)  6.58 us
    pallas_call x1, Pallas kernels, layer(): call(agg_kernel, (agg_shape, agg_shape), [sspec(), sspec(), vspec(), vspe...  4.06 us
    slice x4, local copies, waits for them, and re-layouts, spread(): high = shift(above[part:], axis, -1)  4.02 us
  transfers between devices with their start and end apart: 25, of which 7 were waited for; matrix products, arithmetic and copies ran while one was open for 21% of the time, Pallas kernels for 8%

commit v1 on v0

v1 whole, which is shorter than its diff:
```python
import jax
import jax.numpy as jnp
from jax import lax
from jax.experimental import pallas as pl
from jax.experimental.pallas import tpu as pltpu
from jax.sharding import Mesh, PartitionSpec as P


BLOCK = 128
X, Y, C = 4, 4, 2
CHIPS = X * Y
F32 = jnp.float32
BF16 = jnp.bfloat16
VM = pltpu.MemorySpace.VMEM
SM = pltpu.MemorySpace.SMEM
HB = pltpu.MemorySpace.HBM
NN = (((1,), (0,)), ((), ()))
NT = (((1,), (1,)), ((), ()))
TN = (((0,), (0,)), ((), ()))


def mm(a, b, dims):
    return lax.dot_general(a, b, dims, preferred_element_type=F32)


def vspec():
    return pl.BlockSpec(memory_space=VM)


def hspec():
    return pl.BlockSpec(memory_space=HB)


def sspec():
    return pl.BlockSpec(memory_space=SM)


def call(kernel, out_shape, in_specs, scratch=(), flops=10**8, bytes_accessed=10**6, vmem_mib=8, out=None):
    many = isinstance(out_shape, (tuple, list))
    return pl.pallas_call(
        kernel,
        out_shape=out_shape,
        in_specs=in_specs,
        out_specs=out or (tuple(vspec() for _ in out_shape) if many else vspec()),
        scratch_shapes=list(scratch),
        cost_estimate=pl.CostEstimate(flops=flops, bytes_accessed=bytes_accessed, transcendentals=0),
        compiler_params=pltpu.CompilerParams(vmem_limit_bytes=vmem_mib * 2**20),
    )


def pool_kernel(core_ref, feat_hbm, pool_hbm, send_ref, keep_ref, mine_ref, give_ref, feat_ref, pool_ref, sems):
    fetch = [pltpu.make_async_copy(feat_hbm, feat_ref, sems.at[0]), pltpu.make_async_copy(pool_hbm, pool_ref, sems.at[1])]
    for cp in fetch:
        cp.start()
    for cp in fetch:
        cp.wait()
    half = send_ref.shape[0]
    own = pl.multiple_of(core_ref[0] * half, half)
    other = pl.multiple_of((1 - core_ref[0]) * half, half)
    feat = feat_ref[...]
    gates = jax.nn.sigmoid(mm(feat, pool_ref[:, pl.ds(other, half)], NN)).astype(BF16)
    send_ref[...] = mm(gates, feat, TN).astype(BF16)
    gates = jax.nn.sigmoid(mm(feat, pool_ref[:, pl.ds(own, half)], NN)).astype(BF16)
    keep_ref[...] = mm(gates, feat, TN)
    mine_ref[...] = feat_ref[:, pl.ds(own, half)]
    give_ref[...] = feat_ref[:, pl.ds(other, half)]


def join_kernel(a_ref, b_ref, out_ref):
    n = a_ref.shape[0]
    out_ref[:n] = a_ref[...]
    out_ref[n:] = b_ref[...]


def join(a, b):
    shape = jax.ShapeDtypeStruct((a.shape[0] + b.shape[0],) + a.shape[1:], a.dtype)
    return call(join_kernel, shape, [vspec(), vspec()], flops=0)(a, b)


def chain_kernel(meta_ref, summ_ref, w_in_ref, w_state_ref, offset_ref, start_ref, out_hbm, side_ref, startt_ref, w_ref, out_ref, sems):
    fetch = pltpu.make_async_copy(w_state_ref, w_ref, sems.at[0])
    fetch.start()
    n_t, cols, width = summ_ref.shape
    summ = summ_ref[...].reshape(n_t * cols, width)
    for g in range(3):
        side = mm(summ, w_in_ref[g], NT)
        if g == 0:
            side = side - offset_ref[...]
        side_ref[g] = side.reshape(n_t, cols, width)
    startt_ref[...] = start_ref[...].T
    col0 = pl.multiple_of(meta_ref[1], cols)
    state = startt_ref[pl.ds(col0, cols), :]
    last = meta_ref[0]
    fetch.wait()

    def step(t, state):
        state_b = state.astype(BF16)
        update = jax.nn.sigmoid(side_ref[0, t] + mm(state_b, w_ref[0], NT))
        reset = jax.nn.sigmoid(side_ref[1, t] + mm(state_b, w_ref[1], NT))
        cand = jnp.tanh(side_ref[2, t] + mm((reset * state).astype(BF16), w_ref[2], NT))
        return (1.0 - update) * state + update * cand

    state = lax.fori_loop(0, last + 1, step, state)
    out_ref[...] = jnp.broadcast_to(state.astype(BF16)[None], out_ref.shape)
    store = pltpu.make_async_copy(out_ref, out_hbm, sems.at[1])
    store.start()
    store.wait()


def masked(idx, tiles, lhs):
    for j in range(tiles.shape[0]):
        tile = tiles[j]
        for r in range(2):
            lhs[r * BLOCK : (r + 1) * BLOCK, j * BLOCK : (j + 1) * BLOCK] = jnp.where(
                idx[1, j] == r, tile, jnp.zeros_like(tile)
            )


def slot_of(step):
    return jnp.where(step == 0, 0, jnp.where(step == 3, 1, step + 1))


def agg_oth_kernel(here, own_idx, oth_idx, tiles, feat, *refs):
    pieces, (agg, rhs_own, blocks, rhs, lhs, sems) = refs[:-6], refs[-6:]
    copies = []
    first = 0
    for n, piece in enumerate(pieces):
        cp = pltpu.make_async_copy(piece, blocks.at[pl.ds(first, piece.shape[0])], sems.at[n])
        cp.start()
        copies.append(cp)
        first += piece.shape[0]
    masked(oth_idx, tiles, lhs)
    for cp in copies:
        cp.wait()
    per_dev = first // (CHIPS * C)
    for idx, out in ((oth_idx, rhs), (own_idx, rhs_own)):
        for j in range(tiles.shape[0]):
            col = idx[0, j]
            owner = lax.div(col, per_dev)
            in_x = slot_of((lax.div(owner, Y * C) - here[0]) & 3)
            in_y = slot_of((lax.div(owner, C) - here[1]) & 3)
            same = (owner & 1) == here[2]
            place = jnp.where(same, in_y * 4 + in_x, in_x * 4 + in_y + CHIPS)
            out[j * BLOCK : (j + 1) * BLOCK, :] = blocks[place * per_dev + lax.rem(col, per_dev)]
    agg[...] = (feat[...].astype(F32) + mm(lhs[...], rhs[...], NN)).astype(BF16)


def agg_own_kernel(own_idx, tiles, feat, rhs, agg, lhs):
    masked(own_idx, tiles, lhs)
    agg[...] = (feat[...].astype(F32) + mm(lhs[...], rhs[...], NN)).astype(BF16)


def final_kernel(core_ref, wt_own, wt_oth, agg_own, agg_oth, hid_ref, w_ref, wt, agg):
    half = wt_own.shape[0]
    own = pl.multiple_of(core_ref[0] * half, half)
    oth = pl.multiple_of((1 - core_ref[0]) * half, half)
    wt[pl.ds(own, half), :] = wt_own[...]
    wt[pl.ds(oth, half), :] = wt_oth[...]
    agg[:, pl.ds(own, half)] = agg_own[...]
    agg[:, pl.ds(oth, half)] = agg_oth[...]
    width = wt.shape[0]
    mixed = mm(agg[...], wt[...], NT)
    hid_ref[...] = jnp.maximum(mixed * width ** (-0.5), 0.0).astype(BF16)
    w_ref[...] = wt[...].astype(F32).T


def swap(x):
    return lax.ppermute(x, "c", [(0, 1), (1, 0)])


def trade(x, axes):
    return lax.all_to_all(x, axes, split_axis=0, concat_axis=0, tiled=True)


def shift(x, axis, distance):
    size = lax.axis_size(axis)
    return lax.ppermute(x, axis, [(i, (i + distance) % size) for i in range(size)])


def spread(x, axis):
    below = shift(x, axis, 1)
    above = shift(x, axis, -1)
    return [x, below, above, shift(below, axis, 1)]


def spread2(low, high, axis):
    below = [shift(low, axis, 1), shift(high, axis, 1)]
    above = [shift(low, axis, -1), shift(high, axis, -1)]
    opposite = [shift(below[0], axis, 1), shift(above[1], axis, -1)]
    return [low, high] + below + above + opposite


def layer(
    features,
    tile_rows,
    tile_cols,
    tile_vals,
    tile_used,
    pool_weight,
    w_in,
    w_state,
    gate_offset,
    start_weight,
):
    rows_dev, width = features.shape[1:]
    slots = tile_rows.shape[1]
    half = width // 2
    n_tm = lax.axis_size("z")
    core = lax.axis_index("c").astype(jnp.int32)
    chip = (lax.axis_index("x") * Y + lax.axis_index("y")).astype(jnp.int32)
    dom = chip * C + core
    t_index = lax.axis_index("z").astype(jnp.int32)
    core_s = core.reshape(1)
    feat = features[0]
    blocks_dev = rows_dev // BLOCK

    bf_half = jax.ShapeDtypeStruct((half, width), BF16)
    feat_half = jax.ShapeDtypeStruct((rows_dev, half), BF16)
    send, keep, feat_mine, feat_give = call(
        pool_kernel,
        (bf_half, jax.ShapeDtypeStruct((half, width), F32), feat_half, feat_half),
        [sspec(), hspec(), hspec()],
        scratch=[pltpu.VMEM(feat.shape, BF16), pltpu.VMEM(pool_weight.shape, BF16), pltpu.SemaphoreType.DMA((2,))],
    )(core_s, feat, pool_weight)
    partial = (keep + swap(send).astype(F32)).astype(BF16)
    cols = half // CHIPS
    parts = trade(partial.reshape(CHIPS, cols, width), ("x", "y"))
    summ = (jnp.sum(parts.astype(F32), axis=0) * (rows_dev * CHIPS * C) ** (-0.5)).astype(BF16)
    summ = trade(jnp.broadcast_to(summ[None], (n_tm, cols, width)), "z")

    feat_oth = swap(feat_give)
    four = (blocks_dev, BLOCK, half)
    blocks_a = spread(feat_mine.reshape(four), "x")
    blocks_b = spread(feat_oth.reshape(four), "y")
    low_a, low_b = join(*blocks_a[:2]), join(*blocks_b[:2])
    high_a, high_b = join(*blocks_a[2:]), join(*blocks_b[2:])
    gathered = spread2(low_a, high_a, "y") + spread2(low_b, high_b, "x")

    live = jnp.arange(slots, dtype=jnp.int32) < tile_used[0, 0]
    where_to = jnp.where(live, tile_rows[0] - dom * blocks_dev, blocks_dev)
    own_idx = jnp.stack([tile_cols[0], where_to])
    oth_idx = swap(own_idx)

    tiles_own = tile_vals[0]
    tiles_oth = swap(tiles_own)
    here = jnp.stack([lax.axis_index("x"), lax.axis_index("y"), core]).astype(jnp.int32)
    depth = slots * BLOCK
    lhs = pltpu.VMEM((rows_dev, depth), BF16)
    agg_give, rhs_own = call(
        agg_oth_kernel,
        (feat_half, jax.ShapeDtypeStruct((depth, half), BF16)),
        [sspec()] * 3 + [vspec()] * 2 + [pl.BlockSpec(memory_space=pl.ANY)] * len(gathered),
        scratch=[
            pltpu.VMEM((CHIPS * C * blocks_dev, BLOCK, half), BF16),
            pltpu.VMEM((depth, half), BF16),
            lhs,
            pltpu.SemaphoreType.DMA((len(gathered),)),
        ],
        vmem_mib=16,
    )(here, own_idx, oth_idx, tiles_oth, feat_oth, *gathered)
    agg_oth = swap(agg_give)
    agg_own = call(
        agg_own_kernel, feat_half, [sspec()] + [vspec()] * 3, scratch=[lhs], vmem_mib=8
    )(own_idx, tiles_own, feat_mine, rhs_own)

    col0 = core * half + chip * cols
    lane0 = col0 // BLOCK
    start_cols = lax.dynamic_slice_in_dim(start_weight, lane0 * BLOCK, BLOCK, 1)
    meta = jnp.stack([t_index, col0 % BLOCK])
    evolved = call(
        chain_kernel,
        jax.ShapeDtypeStruct((CHIPS, cols, width), BF16),
        [sspec(), vspec(), vspec(), hspec(), vspec(), vspec()],
        scratch=[
            pltpu.VMEM((3, n_tm, cols, width), F32),
            pltpu.VMEM((BLOCK, width), F32),
            pltpu.VMEM(w_state.shape, BF16),
            pltpu.VMEM((CHIPS, cols, width), BF16),
            pltpu.SemaphoreType.DMA((2,)),
        ],
        out=hspec(),
        vmem_mib=12,
    )(meta, summ, w_in, w_state, gate_offset[None, :], start_cols)
    wt_own = trade(evolved, ("x", "y")).reshape(half, width)
    wt_oth = swap(wt_own)
    hidden, weights = call(
        final_kernel,
        (jax.ShapeDtypeStruct((rows_dev, width), BF16), jax.ShapeDtypeStruct((width, width), F32)),
        [sspec(), vspec(), vspec(), vspec(), vspec()],
        scratch=[pltpu.VMEM((width, width), BF16), pltpu.VMEM((rows_dev, width), BF16)],
    )(core_s, wt_own, wt_oth, agg_own, agg_oth)
    return hidden[None], weights[None]


def solution(mesh):
    n_tm = mesh.shape["tm"]
    fine = Mesh(mesh.devices.reshape(X, Y, C, n_tm), ("x", "y", "c", "z"))
    dom = ("x", "y", "c")
    in_specs = (
        P("z", dom, None),
        P("z", dom),
        P("z", dom),
        P("z", dom, None, None),
        P("z", dom),
        P(),
        P(),
        P(),
        P(),
        P(),
    )
    out_specs = (P("z", dom, None), P("z", None, None))
    return jax.shard_map(layer, mesh=fine, in_specs=in_specs, out_specs=out_specs, check_vma=False)
```

time: 105 us -> 89.9 us (0.86)
  waiting for transfers between devices: 18.8 us -> 6.8 us
  local copies, waits for them, and re-layouts: 23.6 us -> 13.3 us
  starting transfers between devices: 46.7 us -> 52.5 us
  Pallas kernels: 9.5 us -> 13 us
  other arithmetic: 3.57 us -> 1.94 us
    ppermute x16 -> x18, waiting for transfers between devices: 11.2 us -> 0.05 us  [shift(): lax.ppermute(x, axis, [(i, (i + distance) % size) for i in range(size)])]
    slice x8 -> x0, local copies, waits for them, and re-layouts: 7.06 us -> none  [the longest x4 4.02 us: spread(): high = shift(above[part:], axis, -1)]
    pallas_call x3 -> x7, Pallas kernels: 5.92 us -> 9.63 us  [the longest x1 3.87 us: layer(): call(agg_oth_kernel, (feat_half, jax.ShapeDtypeStruct((depth, half), BF16...]
    all_to_all x3, starting transfers between devices: 14.7 us -> 17.6 us  [trade(): return lax.all_to_all(x, axes, split_axis=0, concat_axis=0, tiled=True)]
    concatenate x2 -> x0, local copies, waits for them, and re-layouts: 2.1 us -> none  [the longest x1 1.46 us: layer(): blocks_b = spread(jnp.concatenate(blocks_b), 'x')]
    ppermute x16 -> x18, starting transfers between devices: 19.2 us -> 20.8 us  [shift(): lax.ppermute(x, axis, [(i, (i + distance) % size) for i in range(size)])]
    ppermute x6, starting transfers between devices: 12.8 us -> 14.1 us  [swap(): return lax.ppermute(x, 'c', [(0, 1), (1, 0)])]
    dynamic_slice x1 -> x0, local copies, waits for them, and re-layouts: 1.09 us -> none  [layer(): feat_send = lax.dynamic_slice_in_dim(feat, (1 - core) * half, half, 1)]
  transfers between devices with their start and end apart: 25 -> 27, of which waited for: 7 -> 2; matrix products, arithmetic and copies ran while one was open for 21% -> 3% of each run, Pallas kernels for 8% -> 12%
where the time goes in v1:
time: 89.9 us; the launch traced here: 89.2 us
  starting transfers between devices  52.5 us (58%)
  local copies, waits for them, and re-layouts  13.3 us (15%)
  Pallas kernels  13 us (14%)
  waiting for transfers between devices  6.8 us (8%)
  other arithmetic  1.94 us (2%)
  between operations  1.64 us (2%)
    ppermute x18, starting transfers between devices, shift(): lax.ppermute(x, axis, [(i, (i + distance) % size) for i in range(size)])  20.8 us
    all_to_all x3, starting transfers between devices, trade(): return lax.all_to_all(x, axes, split_axis=0, concat_axis=0, tiled=True)  17.6 us
    ppermute x6, starting transfers between devices, swap(): return lax.ppermute(x, 'c', [(0, 1), (1, 0)])  14.1 us
    unnamed x48, local copies, waits for them, and re-layouts  12.6 us
    all_to_all x3, waiting for transfers between devices, trade(): return lax.all_to_all(x, axes, split_axis=0, concat_axis=0, tiled=True)  6.74 us
    pallas_call x1, Pallas kernels, layer(): call(agg_oth_kernel, (feat_half, jax.ShapeDtypeStruct((depth, half), BF16...  3.87 us
    pallas_call x4, Pallas kernels, join(): return call(join_kernel, shape, [vspec(), vspec()], flops=0)(a, b)  3.75 us
    pallas_call x1, Pallas kernels, layer(): call(chain_kernel, jax.ShapeDtypeStruct((CHIPS, cols, width), BF16), [ssp...  1.95 us
  transfers between devices with their start and end apart: 27, of which 2 were waited for; matrix products, arithmetic and copies ran while one was open for 3% of the time, Pallas kernels for 12%

profile of v1, /device:TPU:1, one launch (start us, length us, event | category | flops | bytes accessed | tf_op | source)
XLA Modules:
  0.0 89.2 jit_solution(11936357881802521377)
XLA Ops:
  3.6 3.3 %collective-permute-start = (bf16[256,512]{1,0:T(8,128)(2,1)S(1)}, bf16[256,512]{1,0:T(8,128)(2,1)S(1)}, u32[]{:S(2)}, u32[]{:S(2)}) collective-permute-start(bf16[256,512]{1,0:T(8,128)(2,1)S(1)} %get-tuple-element.11), channel_id=1, source_target_pairs={{0,8},{8,0},{1,9},{9,1},{2,10},{10,2},{3,11},{11,3},{4,12},{12,4},... | collective-permute-start | bytes 786440 | tf_op jit(solution)/shard_map/ppermute | solution.py:168
  7.0 2.7 %collective-permute-start.6 = (bf16[2,128,256]{2,1,0:T(8,128)(2,1)S(1)}, bf16[2,128,256]{2,1,0:T(8,128)(2,1)S(1)}, u32[]{:S(2)}, u32[]{:S(2)}) collective-permute-start(bf16[2,128,256]{2,1,0:T(8,128)(2,1)S(1)} %bitcast.21), channel_id=1, source_target_pairs={{0,192},{64,0},{128,64},{192,128},{1,193},{65,1},{129,65},{193,129... | collective-permute-start | bytes 393224 | tf_op jit(solution)/shard_map/ppermute | solution.py:177
  10.4 2.7 %collective-permute-start.15 = (bf16[2,128,256]{2,1,0:T(8,128)(2,1)S(1)}, bf16[2,128,256]{2,1,0:T(8,128)(2,1)}, u32[]{:S(2)}, u32[]{:S(2)}) collective-permute-start(bf16[2,128,256]{2,1,0:T(8,128)(2,1)S(1)} %bitcast.24), channel_id=1, source_target_pairs={{0,48},{16,0},{32,16},{48,32},{1,49},{17,1},{33,17},{49,33},{2,50}... | collective-permute-start | bytes 393224 | tf_op jit(solution)/shard_map/ppermute | solution.py:177
  15.0 6.5 %all-to-all-start = ((bf16[16,16,512]{2,1,0:T(8,128)(2,1)}), bf16[16,16,512]{2,1,0:T(8,128)(2,1)}, u32[]{:S(2)}, u32[]{:S(2)}) async-start(bf16[16,16,512]{2,1,0:T(8,128)(2,1)} %bitcast.4), calls=%async_computation | async-start | bytes 524288 | tf_op jit(solution)/shard_map/all_to_all | solution.py:172
  21.5 1.4 %collective-permute-start.16 = (bf16[2,128,256]{2,1,0:T(8,128)(2,1)}, bf16[2,128,256]{2,1,0:T(8,128)(2,1)}, u32[]{:S(2)}, u32[]{:S(2)}) collective-permute-start(bf16[2,128,256]{2,1,0:T(8,128)(2,1)} %collective-permute-done.14.b_ref), channel_id=1, source_target_pairs={{0,16},{16,32},{32,48},{48,0},{1,17},{17,33},{33,49},{49,1},{2,18}... | collective-permute-start | bytes 393224 | tf_op jit(solution)/shard_map/ppermute | solution.py:177
  24.5 2.9 %collective-permute-start.2 = (s32[2,24]{1,0:T(2,128)S(1)}, s32[2,24]{1,0:T(2,128)S(1)}, u32[]{:S(2)}, u32[]{:S(2)}) collective-permute-start(s32[2,24]{1,0:T(2,128)S(1)} %pad_add_fusion.own_idx), channel_id=1, source_target_pairs={{0,8},{8,0},{1,9},{9,1},{2,10},{10,2},{3,11},{11,3},{4,12},{12,4},... | collective-permute-start | bytes 584 | tf_op jit(solution)/shard_map/ppermute | solution.py:168
  27.5 1.2 %collective-permute-start.10 = (bf16[4,128,256]{2,1,0:T(8,128)(2,1)S(1)}, bf16[4,128,256]{2,1,0:T(8,128)(2,1)}, u32[]{:S(2)}, u32[]{:S(2)}) collective-permute-start(bf16[4,128,256]{2,1,0:T(8,128)(2,1)S(1)} %shard_map.115.refs_0_), channel_id=1, source_target_pairs={{0,48},{16,0},{32,16},{48,32},{1,49},{17,1},{33,17},{49,33},{2,50}... | collective-permute-start | bytes 786440 | tf_op jit(solution)/shard_map/ppermute | solution.py:177
  30.9 2.4 %collective-permute-start.11 = (bf16[4,128,256]{2,1,0:T(8,128)(2,1)S(1)}, bf16[4,128,256]{2,1,0:T(8,128)(2,1)}, u32[]{:S(2)}, u32[]{:S(2)}) collective-permute-start(bf16[4,128,256]{2,1,0:T(8,128)(2,1)S(1)} %shard_map.116.refs_1_), channel_id=1, source_target_pairs={{0,48},{16,0},{32,16},{48,32},{1,49},{17,1},{33,17},{49,33},{2,50}... | collective-permute-start | bytes 786440 | tf_op jit(solution)/shard_map/ppermute | solution.py:177
  37.0 1.5 %collective-permute-start.17 = (bf16[4,128,256]{2,1,0:T(8,128)(2,1)S(1)}, bf16[4,128,256]{2,1,0:T(8,128)(2,1)}, u32[]{:S(2)}, u32[]{:S(2)}) collective-permute-start(bf16[4,128,256]{2,1,0:T(8,128)(2,1)S(1)} %shard_map.117.refs_8_), channel_id=1, source_target_pairs={{0,64},{64,128},{128,192},{192,0},{1,65},{65,129},{129,193},{193,1... | collective-permute-start | bytes 786440 | tf_op jit(solution)/shard_map/ppermute | solution.py:177
  39.1 7.3 %all-to-all-start.1 = ((bf16[8,16,512]{2,1,0:T(8,128)(2,1)}), bf16[8,16,512]{2,1,0:T(8,128)(2,1)S(1)}, u32[]{:S(2)}, u32[]{:S(2)}) async-start(bf16[8,16,512]{2,1,0:T(8,128)(2,1)} %broadcast_in_dim.19), calls=%async_computation.1 | async-start | bytes 262144 | tf_op jit(solution)/shard_map/all_to_all | solution.py:172
  46.5 1.5 %collective-permute-start.19 = (bf16[4,128,256]{2,1,0:T(8,128)(2,1)S(1)}, bf16[4,128,256]{2,1,0:T(8,128)(2,1)}, u32[]{:S(2)}, u32[]{:S(2)}) collective-permute-start(bf16[4,128,256]{2,1,0:T(8,128)(2,1)S(1)} %shard_map.117.refs_8_), channel_id=1, source_target_pairs={{0,192},{64,0},{128,64},{192,128},{1,193},{65,1},{129,65},{193,129... | collective-permute-start | bytes 786440 | tf_op jit(solution)/shard_map/ppermute | solution.py:177
  47.9 1.5 %collective-permute-start.20 = (bf16[4,128,256]{2,1,0:T(8,128)(2,1)}, bf16[4,128,256]{2,1,0:T(8,128)(2,1)}, u32[]{:S(2)}, u32[]{:S(2)}) collective-permute-start(bf16[4,128,256]{2,1,0:T(8,128)(2,1)} %copy-done.5), channel_id=1, source_target_pairs={{0,192},{64,0},{128,64},{192,128},{1,193},{65,1},{129,65},{193,129... | collective-permute-start | bytes 786440 | tf_op jit(solution)/shard_map/ppermute | solution.py:177
  49.7 4.7 %all-to-all-done.1.summ_ref = bf16[8,16,512]{2,1,0:T(8,128)(2,1)S(1)} async-done(((bf16[8,16,512]{2,1,0:T(8,128)(2,1)}), bf16[8,16,512]{2,1,0:T(8,128)(2,1)S(1)}, u32[]{:S(2)}, u32[]{:S(2)}) %all-to-all-start.1) | async-done | bytes 131104 | tf_op jit(solution)/shard_map/all_to_all | solution.py:172
  54.3 1.4 %copy-done.2 = bf16[3,512,512]{2,1,0:T(8,128)(2,1)S(1)} copy-done((bf16[3,512,512]{2,1,0:T(8,128)(2,1)S(1)}, bf16[3,512,512]{2,1,0:T(8,128)(2,1)}, u32[]{:S(2)}) %copy-start.2) | copy-done | bytes 1572888
  55.7 1.9 %shard_map.114 = bf16[16,16,512]{2,1,0:T(8,128)(2,1)S(1)} custom-call(s32[2]{0:T(128)S(1)} %pad_add_fusion.1.meta_ref, bf16[8,16,512]{2,1,0:T(8,128)(2,1)S(1)} %all-to-all-done.1.summ_ref, bf16[3,512,512]{2,1,0:T(8,128)(2,1)S(1)} %copy-done.1, bf16[3,512,512]{2,1,0:T(8,128)(2,1)S(1)} %copy-done.2, f32[1,512]{1,0:T(1,128)S(1)} %bitcast.27, ...), custom_call_target="tpu_custom_call" | custom-call | flops 100000000 | bytes 1000000 | tf_op jit(solution)/shard_map/pallas_call | solution.py:270
  58.4 3.8 %all-to-all-start.2 = ((bf16[16,16,512]{2,1,0:T(8,128)(2,1)}), bf16[16,16,512]{2,1,0:T(8,128)(2,1)S(1)}, u32[]{:S(2)}, u32[]{:S(2)}) async-start(bf16[16,16,512]{2,1,0:T(8,128)(2,1)} %copy-done.7), calls=%async_computation.2 | async-start | bytes 524288 | tf_op jit(solution)/shard_map/all_to_all | solution.py:172
  62.2 2.6 %collective-permute-start.13 = (bf16[4,128,256]{2,1,0:T(8,128)(2,1)}, bf16[4,128,256]{2,1,0:T(8,128)(2,1)S(1)}, u32[]{:S(2)}, u32[]{:S(2)}) collective-permute-start(bf16[4,128,256]{2,1,0:T(8,128)(2,1)} %collective-permute-done.11.refs_5_), channel_id=1, source_target_pairs={{0,48},{16,0},{32,16},{48,32},{1,49},{17,1},{33,17},{49,33},{2,50}... | collective-permute-start | bytes 786440 | tf_op jit(solution)/shard_map/ppermute | solution.py:177
  66.1 1.5 %collective-permute-start.22 = (bf16[4,128,256]{2,1,0:T(8,128)(2,1)}, bf16[4,128,256]{2,1,0:T(8,128)(2,1)S(1)}, u32[]{:S(2)}, u32[]{:S(2)}) collective-permute-start(bf16[4,128,256]{2,1,0:T(8,128)(2,1)} %collective-permute-done.20.refs_13_), channel_id=1, source_target_pairs={{0,192},{64,0},{128,64},{192,128},{1,193},{65,1},{129,65},{193,129... | collective-permute-start | bytes 786440 | tf_op jit(solution)/shard_map/ppermute | solution.py:177
  67.6 2.1 %all-to-all-done.2 = bf16[16,16,512]{2,1,0:T(8,128)(2,1)S(1)} async-done(((bf16[16,16,512]{2,1,0:T(8,128)(2,1)}), bf16[16,16,512]{2,1,0:T(8,128)(2,1)S(1)}, u32[]{:S(2)}, u32[]{:S(2)}) %all-to-all-start.2) | async-done | bytes 262176 | tf_op jit(solution)/shard_map/all_to_all | solution.py:172
  69.6 4.4 %collective-permute-start.1 = (bf16[256,512]{1,0:T(8,128)(2,1)S(1)}, bf16[256,512]{1,0:T(8,128)(2,1)S(1)}, u32[]{:S(2)}, u32[]{:S(2)}) collective-permute-start(bf16[256,512]{1,0:T(8,128)(2,1)S(1)} %bitcast.16), channel_id=1, source_target_pairs={{0,8},{8,0},{1,9},{9,1},{2,10},{10,2},{3,11},{11,3},{4,12},{12,4},... | collective-permute-start | bytes 786440 | tf_op jit(solution)/shard_map/ppermute | solution.py:168
  80.2 3.9 %shard_map.119 = (bf16[256,256]{1,0:T(8,128)(2,1)S(1)}, bf16[3072,256]{1,0:T(8,128)(2,1)S(1)}) custom-call(s32[3]{0:T(128)S(1)} %pad_add_fusion.2.here, s32[2,24]{1,0:T(2,128)S(1)} %pad_add_fusion.own_idx, s32[2,24]{1,0:T(2,128)S(1)} %collective-permute-done.2.oth_idx, bf16[24,128,128]{2,1,0:T(8,128)(2,1)} %collective-permute-done.3.tiles, ...), custom_call_target="tpu_custom_call" | custom-call | flops 100000000 | bytes 1000000 | tf_op jit(solution)/shard_map/pallas_call | solution.py:249
  84.1 2.4 %collective-permute-start.23 = (bf16[256,256]{1,0:T(8,128)(2,1)S(1)}, bf16[256,256]{1,0:T(8,128)(2,1)S(1)}, u32[]{:S(2)}, u32[]{:S(2)}) collective-permute-start(bf16[256,256]{1,0:T(8,128)(2,1)S(1)} %get-tuple-element.15), channel_id=1, source_target_pairs={{0,8},{8,0},{1,9},{9,1},{2,10},{10,2},{3,11},{11,3},{4,12},{12,4},... | collective-permute-start | bytes 393224 | tf_op jit(solution)/shard_map/ppermute | solution.py:168
  86.5 1.2 %shard_map.120.agg_own = bf16[256,256]{1,0:T(8,128)(2,1)S(1)} custom-call(s32[2,24]{1,0:T(2,128)S(1)} %pad_add_fusion.own_idx, bf16[24,128,128]{2,1,0:T(8,128)(2,1)S(1)} %bitcast.19, bf16[256,256]{1,0:T(8,128)(2,1)S(1)} %copy-done.11, bf16[3072,256]{1,0:T(8,128)(2,1)S(1)} %get-tuple-element.14.rhs), custom_call_target="tpu_custom_call" | custom-call | flops 100000000 | bytes 1000000 | tf_op jit(solution)/shard_map/pallas_call | solution.py:262
  87.7 1.4 %shard_map.121 = (bf16[256,512]{1,0:T(8,128)(2,1)}, f32[512,512]{1,0:T(8,128)}) custom-call(s32[1]{0:T(128)} %bitcast.core_ref, bf16[256,512]{1,0:T(8,128)(2,1)S(1)} %bitcast.17, bf16[256,512]{1,0:T(8,128)(2,1)S(1)} %collective-permute-done.1.wt_oth, bf16[256,256]{1,0:T(8,128)(2,1)S(1)} %shard_map.120.agg_own, ...), custom_call_target="tpu_custom_call" | custom-call | flops 100000000 | bytes 1000000 | tf_op jit(solution)/shard_map/pallas_call | solution.py:286
  (96 shorter events, 21.4 us)
Async XLA Ops:
  3.6 10.5 %collective-permute-start = (bf16[256,512]{1,0:T(8,128)(2,1)S(1)}, bf16[256,512]{1,0:T(8,128)(2,1)S(1)}, u32[]{:S(2)}, u32[]{:S(2)}) collective-permute-start(bf16[256,512]{1,0:T(8,128)(2,1)S(1)} %get-tuple-element.11), channel_id=1, source_target_pairs={{0,8},{8,0},{1,9},{9,1},{2,10},{10,2},{3,11},{11,3},{4,12},{12,4},... | collective-permute-start | bytes 786440 | tf_op jit(solution)/shard_map/ppermute | solution.py:168
  7.0 16.9 %collective-permute-start.6 = (bf16[2,128,256]{2,1,0:T(8,128)(2,1)S(1)}, bf16[2,128,256]{2,1,0:T(8,128)(2,1)S(1)}, u32[]{:S(2)}, u32[]{:S(2)}) collective-permute-start(bf16[2,128,256]{2,1,0:T(8,128)(2,1)S(1)} %bitcast.21), channel_id=1, source_target_pairs={{0,192},{64,0},{128,64},{192,128},{1,193},{65,1},{129,65},{193,129... | collective-permute-start | bytes 393224 | tf_op jit(solution)/shard_map/ppermute | solution.py:177
  10.3 11.2 %collective-permute-start.14 = (bf16[2,128,256]{2,1,0:T(8,128)(2,1)S(1)}, bf16[2,128,256]{2,1,0:T(8,128)(2,1)}, u32[]{:S(2)}, u32[]{:S(2)}) collective-permute-start(bf16[2,128,256]{2,1,0:T(8,128)(2,1)S(1)} %bitcast.23), channel_id=1, source_target_pairs={{0,16},{16,32},{32,48},{48,0},{1,17},{17,33},{33,49},{49,1},{2,18}... | collective-permute-start | bytes 393224 | tf_op jit(solution)/shard_map/ppermute | solution.py:177
  10.4 20.1 %collective-permute-start.15 = (bf16[2,128,256]{2,1,0:T(8,128)(2,1)S(1)}, bf16[2,128,256]{2,1,0:T(8,128)(2,1)}, u32[]{:S(2)}, u32[]{:S(2)}) collective-permute-start(bf16[2,128,256]{2,1,0:T(8,128)(2,1)S(1)} %bitcast.24), channel_id=1, source_target_pairs={{0,48},{16,0},{32,16},{48,32},{1,49},{17,1},{33,17},{49,33},{2,50}... | collective-permute-start | bytes 393224 | tf_op jit(solution)/shard_map/ppermute | solution.py:177
  14.0 23.0 %collective-permute-start.8 = (bf16[4,128,256]{2,1,0:T(8,128)(2,1)S(1)}, bf16[4,128,256]{2,1,0:T(8,128)(2,1)}, u32[]{:S(2)}, u32[]{:S(2)}) collective-permute-start(bf16[4,128,256]{2,1,0:T(8,128)(2,1)S(1)} %shard_map.115.refs_0_), channel_id=1, source_target_pairs={{0,16},{16,32},{32,48},{48,0},{1,17},{17,33},{33,49},{49,1},{2,18}... | collective-permute-start | bytes 786440 | tf_op jit(solution)/shard_map/ppermute | solution.py:177
  14.1 13.4 %collective-permute-start.7 = (bf16[2,128,256]{2,1,0:T(8,128)(2,1)}, bf16[2,128,256]{2,1,0:T(8,128)(2,1)}, u32[]{:S(2)}, u32[]{:S(2)}) collective-permute-start(bf16[2,128,256]{2,1,0:T(8,128)(2,1)} %collective-permute-done.5.b_ref), channel_id=1, source_target_pairs={{0,64},{64,128},{128,192},{192,0},{1,65},{65,129},{129,193},{193,1... | collective-permute-start | bytes 393224 | tf_op jit(solution)/shard_map/ppermute | solution.py:177
  15.0 20.0 %all-to-all-start = ((bf16[16,16,512]{2,1,0:T(8,128)(2,1)}), bf16[16,16,512]{2,1,0:T(8,128)(2,1)}, u32[]{:S(2)}, u32[]{:S(2)}) async-start(bf16[16,16,512]{2,1,0:T(8,128)(2,1)} %bitcast.4), calls=%async_computation | async-start | bytes 524288 | tf_op jit(solution)/shard_map/all_to_all | solution.py:172
  21.5 9.4 %collective-permute-start.16 = (bf16[2,128,256]{2,1,0:T(8,128)(2,1)}, bf16[2,128,256]{2,1,0:T(8,128)(2,1)}, u32[]{:S(2)}, u32[]{:S(2)}) collective-permute-start(bf16[2,128,256]{2,1,0:T(8,128)(2,1)} %collective-permute-done.14.b_ref), channel_id=1, source_target_pairs={{0,16},{16,32},{32,48},{48,0},{1,17},{17,33},{33,49},{49,1},{2,18}... | collective-permute-start | bytes 393224 | tf_op jit(solution)/shard_map/ppermute | solution.py:177
  24.5 11.5 %collective-permute-start.2 = (s32[2,24]{1,0:T(2,128)S(1)}, s32[2,24]{1,0:T(2,128)S(1)}, u32[]{:S(2)}, u32[]{:S(2)}) collective-permute-start(s32[2,24]{1,0:T(2,128)S(1)} %pad_add_fusion.own_idx), channel_id=1, source_target_pairs={{0,8},{8,0},{1,9},{9,1},{2,10},{10,2},{3,11},{11,3},{4,12},{12,4},... | collective-permute-start | bytes 584 | tf_op jit(solution)/shard_map/ppermute | solution.py:168
  27.5 19.0 %collective-permute-start.10 = (bf16[4,128,256]{2,1,0:T(8,128)(2,1)S(1)}, bf16[4,128,256]{2,1,0:T(8,128)(2,1)}, u32[]{:S(2)}, u32[]{:S(2)}) collective-permute-start(bf16[4,128,256]{2,1,0:T(8,128)(2,1)S(1)} %shard_map.115.refs_0_), channel_id=1, source_target_pairs={{0,48},{16,0},{32,16},{48,32},{1,49},{17,1},{33,17},{49,33},{2,50}... | collective-permute-start | bytes 786440 | tf_op jit(solution)/shard_map/ppermute | solution.py:177
  30.5 17.4 %collective-permute-start.9 = (bf16[4,128,256]{2,1,0:T(8,128)(2,1)S(1)}, bf16[4,128,256]{2,1,0:T(8,128)(2,1)}, u32[]{:S(2)}, u32[]{:S(2)}) collective-permute-start(bf16[4,128,256]{2,1,0:T(8,128)(2,1)S(1)} %shard_map.116.refs_1_), channel_id=1, source_target_pairs={{0,16},{16,32},{32,48},{48,0},{1,17},{17,33},{33,49},{49,1},{2,18}... | collective-permute-start | bytes 786440 | tf_op jit(solution)/shard_map/ppermute | solution.py:177
  30.9 18.5 %collective-permute-start.11 = (bf16[4,128,256]{2,1,0:T(8,128)(2,1)S(1)}, bf16[4,128,256]{2,1,0:T(8,128)(2,1)}, u32[]{:S(2)}, u32[]{:S(2)}) collective-permute-start(bf16[4,128,256]{2,1,0:T(8,128)(2,1)S(1)} %shard_map.116.refs_1_), channel_id=1, source_target_pairs={{0,48},{16,0},{32,16},{48,32},{1,49},{17,1},{33,17},{49,33},{2,50}... | collective-permute-start | bytes 786440 | tf_op jit(solution)/shard_map/ppermute | solution.py:177
  36.0 38.8 %collective-permute-start.3 = (bf16[24,128,128]{2,1,0:T(8,128)(2,1)}, bf16[24,128,128]{2,1,0:T(8,128)(2,1)}, u32[]{:S(2)}, u32[]{:S(2)}) collective-permute-start(bf16[24,128,128]{2,1,0:T(8,128)(2,1)} %bitcast.18), channel_id=1, source_target_pairs={{0,8},{8,0},{1,9},{9,1},{2,10},{10,2},{3,11},{11,3},{4,12},{12,4},... | collective-permute-start | bytes 2359304 | tf_op jit(solution)/shard_map/ppermute | solution.py:168
  37.0 12.5 %collective-permute-start.17 = (bf16[4,128,256]{2,1,0:T(8,128)(2,1)S(1)}, bf16[4,128,256]{2,1,0:T(8,128)(2,1)}, u32[]{:S(2)}, u32[]{:S(2)}) collective-permute-start(bf16[4,128,256]{2,1,0:T(8,128)(2,1)S(1)} %shard_map.117.refs_8_), channel_id=1, source_target_pairs={{0,64},{64,128},{128,192},{192,0},{1,65},{65,129},{129,193},{193,1... | collective-permute-start | bytes 786440 | tf_op jit(solution)/shard_map/ppermute | solution.py:177
  39.1 15.2 %all-to-all-start.1 = ((bf16[8,16,512]{2,1,0:T(8,128)(2,1)}), bf16[8,16,512]{2,1,0:T(8,128)(2,1)S(1)}, u32[]{:S(2)}, u32[]{:S(2)}) async-start(bf16[8,16,512]{2,1,0:T(8,128)(2,1)} %broadcast_in_dim.19), calls=%async_computation.1 | async-start | bytes 262144 | tf_op jit(solution)/shard_map/all_to_all | solution.py:172
  46.5 15.8 %collective-permute-start.19 = (bf16[4,128,256]{2,1,0:T(8,128)(2,1)S(1)}, bf16[4,128,256]{2,1,0:T(8,128)(2,1)}, u32[]{:S(2)}, u32[]{:S(2)}) collective-permute-start(bf16[4,128,256]{2,1,0:T(8,128)(2,1)S(1)} %shard_map.117.refs_8_), channel_id=1, source_target_pairs={{0,192},{64,0},{128,64},{192,128},{1,193},{65,1},{129,65},{193,129... | collective-permute-start | bytes 786440 | tf_op jit(solution)/shard_map/ppermute | solution.py:177
  47.9 18.1 %collective-permute-start.20 = (bf16[4,128,256]{2,1,0:T(8,128)(2,1)}, bf16[4,128,256]{2,1,0:T(8,128)(2,1)}, u32[]{:S(2)}, u32[]{:S(2)}) collective-permute-start(bf16[4,128,256]{2,1,0:T(8,128)(2,1)} %copy-done.5), channel_id=1, source_target_pairs={{0,192},{64,0},{128,64},{192,128},{1,193},{65,1},{129,65},{193,129... | collective-permute-start | bytes 786440 | tf_op jit(solution)/shard_map/ppermute | solution.py:177
  49.4 15.5 %collective-permute-start.12 = (bf16[4,128,256]{2,1,0:T(8,128)(2,1)}, bf16[4,128,256]{2,1,0:T(8,128)(2,1)}, u32[]{:S(2)}, u32[]{:S(2)}) collective-permute-start(bf16[4,128,256]{2,1,0:T(8,128)(2,1)} %collective-permute-done.8.refs_2_), channel_id=1, source_target_pairs={{0,16},{16,32},{32,48},{48,0},{1,17},{17,33},{33,49},{49,1},{2,18}... | collective-permute-start | bytes 786440 | tf_op jit(solution)/shard_map/ppermute | solution.py:177
  49.5 18.1 %collective-permute-start.18 = (bf16[4,128,256]{2,1,0:T(8,128)(2,1)}, bf16[4,128,256]{2,1,0:T(8,128)(2,1)}, u32[]{:S(2)}, u32[]{:S(2)}) collective-permute-start(bf16[4,128,256]{2,1,0:T(8,128)(2,1)} %copy-done.5), channel_id=1, source_target_pairs={{0,64},{64,128},{128,192},{192,0},{1,65},{65,129},{129,193},{193,1... | collective-permute-start | bytes 786440 | tf_op jit(solution)/shard_map/ppermute | solution.py:177
  58.4 11.2 %all-to-all-start.2 = ((bf16[16,16,512]{2,1,0:T(8,128)(2,1)}), bf16[16,16,512]{2,1,0:T(8,128)(2,1)S(1)}, u32[]{:S(2)}, u32[]{:S(2)}) async-start(bf16[16,16,512]{2,1,0:T(8,128)(2,1)} %copy-done.7), calls=%async_computation.2 | async-start | bytes 524288 | tf_op jit(solution)/shard_map/all_to_all | solution.py:172
  62.2 11.9 %collective-permute-start.13 = (bf16[4,128,256]{2,1,0:T(8,128)(2,1)}, bf16[4,128,256]{2,1,0:T(8,128)(2,1)S(1)}, u32[]{:S(2)}, u32[]{:S(2)}) collective-permute-start(bf16[4,128,256]{2,1,0:T(8,128)(2,1)} %collective-permute-done.11.refs_5_), channel_id=1, source_target_pairs={{0,48},{16,0},{32,16},{48,32},{1,49},{17,1},{33,17},{49,33},{2,50}... | collective-permute-start | bytes 786440 | tf_op jit(solution)/shard_map/ppermute | solution.py:177
  64.9 9.2 %collective-permute-start.21 = (bf16[4,128,256]{2,1,0:T(8,128)(2,1)}, bf16[4,128,256]{2,1,0:T(8,128)(2,1)S(1)}, u32[]{:S(2)}, u32[]{:S(2)}) collective-permute-start(bf16[4,128,256]{2,1,0:T(8,128)(2,1)} %collective-permute-done.17.refs_10_), channel_id=1, source_target_pairs={{0,64},{64,128},{128,192},{192,0},{1,65},{65,129},{129,193},{193,1... | collective-permute-start | bytes 786440 | tf_op jit(solution)/shard_map/ppermute | solution.py:177
  66.1 8.7 %collective-permute-start.22 = (bf16[4,128,256]{2,1,0:T(8,128)(2,1)}, bf16[4,128,256]{2,1,0:T(8,128)(2,1)S(1)}, u32[]{:S(2)}, u32[]{:S(2)}) collective-permute-start(bf16[4,128,256]{2,1,0:T(8,128)(2,1)} %collective-permute-done.20.refs_13_), channel_id=1, source_target_pairs={{0,192},{64,0},{128,64},{192,128},{1,193},{65,1},{129,65},{193,129... | collective-permute-start | bytes 786440 | tf_op jit(solution)/shard_map/ppermute | solution.py:177
  69.6 18.1 %collective-permute-start.1 = (bf16[256,512]{1,0:T(8,128)(2,1)S(1)}, bf16[256,512]{1,0:T(8,128)(2,1)S(1)}, u32[]{:S(2)}, u32[]{:S(2)}) collective-permute-start(bf16[256,512]{1,0:T(8,128)(2,1)S(1)} %bitcast.16), channel_id=1, source_target_pairs={{0,8},{8,0},{1,9},{9,1},{2,10},{10,2},{3,11},{11,3},{4,12},{12,4},... | collective-permute-start | bytes 786440 | tf_op jit(solution)/shard_map/ppermute | solution.py:168
  (27 other events, 266.8 us)

commit v2 on v1

--- a/solution.py
+++ b/solution.py
@@ -1,3 +1,5 @@
+import functools
+
 import jax
 import jax.numpy as jnp
 from jax import lax
@@ -8,6 +10,7 @@
 
 BLOCK = 128
 X, Y, C = 4, 4, 2
+WHOLE = 60
 CHIPS = X * Y
 F32 = jnp.float32
 BF16 = jnp.bfloat16
@@ -66,28 +69,54 @@
     give_ref[...] = feat_ref[:, pl.ds(other, half)]
 
 
-def join_kernel(a_ref, b_ref, out_ref):
-    n = a_ref.shape[0]
-    out_ref[:n] = a_ref[...]
-    out_ref[n:] = b_ref[...]
+def join_kernel(*refs):
+    pieces, (low, high, sems) = refs[:-3], refs[-3:]
+    half = len(pieces) // 2
+    copies = []
+    for n, piece in enumerate(pieces):
+        out = low if n < half else high
+        size = piece.shape[0]
+        cp = pltpu.make_async_copy(piece, out.at[pl.ds((n % half) * size, size)], sems.at[n])
+        cp.start()
+        copies.append(cp)
+    for cp in copies:
+        cp.wait()
 
 
 def join(a, b):
-    shape = jax.ShapeDtypeStruct((a.shape[0] + b.shape[0],) + a.shape[1:], a.dtype)
-    return call(join_kernel, shape, [vspec(), vspec()], flops=0)(a, b)
-
-
-def chain_kernel(meta_ref, summ_ref, w_in_ref, w_state_ref, offset_ref, start_ref, out_hbm, side_ref, startt_ref, w_ref, out_ref, sems):
-    fetch = pltpu.make_async_copy(w_state_ref, w_ref, sems.at[0])
+    shape = jax.ShapeDtypeStruct((len(a) * a[0].shape[0],) + a[0].shape[1:], a[0].dtype)
+    pieces = a + b
+    return call(
+        join_kernel,
+        (shape, shape),
+        [pl.BlockSpec(memory_space=pl.ANY)] * len(pieces),
+        scratch=[pltpu.SemaphoreType.DMA((len(pieces),))],
+        flops=0,
+        vmem_mib=WHOLE,
+    )(*pieces)
+
+
+def sum_kernel(scale, parts_ref, out_ref):
+    total = jnp.sum(parts_ref[...].astype(F32), axis=0) * scale
+    out_ref[...] = jnp.broadcast_to(total.astype(BF16)[None], out_ref.shape)
+
+
+def chain_kernel(
+    meta_ref, summ_ref, w_in_hbm, w_state_hbm, offset_ref, start_ref, out_hbm, side_ref, startt_ref, w_in_ref, w_ref, out_ref, sems
+):
+    fetch_in = pltpu.make_async_copy(w_in_hbm, w_in_ref, sems.at[2])
+    fetch_in.start()
+    fetch = pltpu.make_async_copy(w_state_hbm, w_ref, sems.at[0])
     fetch.start()
     n_t, cols, width = summ_ref.shape
     summ = summ_ref[...].reshape(n_t * cols, width)
+    startt_ref[...] = start_ref[...].T
+    fetch_in.wait()
     for g in range(3):
         side = mm(summ, w_in_ref[g], NT)
         if g == 0:
             side = side - offset_ref[...]
         side_ref[g] = side.reshape(n_t, cols, width)
-    startt_ref[...] = start_ref[...].T
     col0 = pl.multiple_of(meta_ref[1], cols)
     state = startt_ref[pl.ds(col0, cols), :]
     last = meta_ref[0]
@@ -178,16 +207,7 @@
 
 
 def spread(x, axis):
-    below = shift(x, axis, 1)
-    above = shift(x, axis, -1)
-    return [x, below, above, shift(below, axis, 1)]
-
-
-def spread2(low, high, axis):
-    below = [shift(low, axis, 1), shift(high, axis, 1)]
-    above = [shift(low, axis, -1), shift(high, axis, -1)]
-    opposite = [shift(below[0], axis, 1), shift(above[1], axis, -1)]
-    return [low, high] + below + above + opposite
+    return [x] + [shift(x, axis, step) for step in (1, -1, 2)]
 
 
 def layer(
@@ -225,16 +245,17 @@
     partial = (keep + swap(send).astype(F32)).astype(BF16)
     cols = half // CHIPS
     parts = trade(partial.reshape(CHIPS, cols, width), ("x", "y"))
-    summ = (jnp.sum(parts.astype(F32), axis=0) * (rows_dev * CHIPS * C) ** (-0.5)).astype(BF16)
-    summ = trade(jnp.broadcast_to(summ[None], (n_tm, cols, width)), "z")
+    snaps = jax.ShapeDtypeStruct((n_tm, cols, width), BF16)
+    scale = (rows_dev * CHIPS * C) ** (-0.5)
+    summ = call(functools.partial(sum_kernel, scale), snaps, [vspec()], flops=10**7, vmem_mib=WHOLE)(parts)
+    summ = trade(summ, "z")
 
     feat_oth = swap(feat_give)
     four = (blocks_dev, BLOCK, half)
     blocks_a = spread(feat_mine.reshape(four), "x")
     blocks_b = spread(feat_oth.reshape(four), "y")
-    low_a, low_b = join(*blocks_a[:2]), join(*blocks_b[:2])
-    high_a, high_b = join(*blocks_a[2:]), join(*blocks_b[2:])
-    gathered = spread2(low_a, high_a, "y") + spread2(low_b, high_b, "x")
+    joined_a, joined_b = join(blocks_a, blocks_b)
+    gathered = spread(joined_a, "y") + spread(joined_b, "x")
 
     live = jnp.arange(slots, dtype=jnp.int32) < tile_used[0, 0]
     where_to = jnp.where(live, tile_rows[0] - dom * blocks_dev, blocks_dev)
@@ -256,7 +277,7 @@
             lhs,
             pltpu.SemaphoreType.DMA((len(gathered),)),
         ],
-        vmem_mib=16,
+        vmem_mib=WHOLE,
     )(here, own_idx, oth_idx, tiles_oth, feat_oth, *gathered)
     agg_oth = swap(agg_give)
     agg_own = call(
@@ -270,16 +291,17 @@
     evolved = call(
         chain_kernel,
         jax.ShapeDtypeStruct((CHIPS, cols, width), BF16),
-        [sspec(), vspec(), vspec(), hspec(), vspec(), vspec()],
+        [sspec(), vspec(), hspec(), hspec(), vspec(), vspec()],
         scratch=[
             pltpu.VMEM((3, n_tm, cols, width), F32),
             pltpu.VMEM((BLOCK, width), F32),
+            pltpu.VMEM(w_in.shape, BF16),
             pltpu.VMEM(w_state.shape, BF16),
             pltpu.VMEM((CHIPS, cols, width), BF16),
-            pltpu.SemaphoreType.DMA((2,)),
+            pltpu.SemaphoreType.DMA((3,)),
         ],
         out=hspec(),
-        vmem_mib=12,
+        vmem_mib=WHOLE,
     )(meta, summ, w_in, w_state, gate_offset[None, :], start_cols)
     wt_own = trade(evolved, ("x", "y")).reshape(half, width)
     wt_oth = swap(wt_own)

time: 89.9 us -> 107 us (1.19)
  waiting for transfers between devices: 6.8 us -> 30.8 us
  local copies, waits for them, and re-layouts: 13.3 us -> 7.29 us
  starting transfers between devices: 52.5 us -> 46.6 us
  Pallas kernels: 13 us -> 17.2 us
    all_to_all x3, waiting for transfers between devices: 6.74 us -> 28.4 us  [trade(): return lax.all_to_all(x, axes, split_axis=0, concat_axis=0, tiled=True)]
    unnamed x48 -> x44, local copies, waits for them, and re-layouts: 12.6 us -> 6.55 us
    ppermute x6, starting transfers between devices: 14.1 us -> 9.88 us  [swap(): return lax.ppermute(x, 'c', [(0, 1), (1, 0)])]
    ppermute x18 -> x12, starting transfers between devices: 20.8 us -> 16.9 us  [shift(): lax.ppermute(x, axis, [(i, (i + distance) % size) for i in range(size)])]
    pallas_call x1, Pallas kernels: 1.95 us -> 4.43 us  [layer(): call(chain_kernel, jax.ShapeDtypeStruct((CHIPS, cols, width), BF16), [ssp...]
    ppermute x18 -> x12, waiting for transfers between devices: 0.05 us -> 2.45 us  [shift(): lax.ppermute(x, axis, [(i, (i + distance) % size) for i in range(size)])]
    all_to_all x3, starting transfers between devices: 17.6 us -> 19.8 us  [trade(): return lax.all_to_all(x, axes, split_axis=0, concat_axis=0, tiled=True)]
    pallas_call x1, Pallas kernels: 3.87 us -> 5.36 us  [layer(): call(agg_oth_kernel, (feat_half, jax.ShapeDtypeStruct((depth, half), BF16...]
  transfers between devices with their start and end apart: 27 -> 21, of which waited for: 2 -> 7; matrix products, arithmetic and copies ran while one was open for 3% -> 3% of each run, Pallas kernels for 12% -> 14%
where the time goes in v2:
time: 107 us; the launch traced here: 106 us
  starting transfers between devices  46.6 us (44%)
  waiting for transfers between devices  30.8 us (29%)
  Pallas kernels  17.2 us (16%)
  local copies, waits for them, and re-layouts  7.29 us (7%)
  other arithmetic  2.94 us (3%)
  between operations  1.6 us (1%)
    all_to_all x3, waiting for transfers between devices, trade(): return lax.all_to_all(x, axes, split_axis=0, concat_axis=0, tiled=True)  28.4 us
    all_to_all x3, starting transfers between devices, trade(): return lax.all_to_all(x, axes, split_axis=0, concat_axis=0, tiled=True)  19.8 us
    ppermute x12, starting transfers between devices, shift(): lax.ppermute(x, axis, [(i, (i + distance) % size) for i in range(size)])  16.9 us
    ppermute x6, starting transfers between devices, swap(): return lax.ppermute(x, 'c', [(0, 1), (1, 0)])  9.88 us
    unnamed x44, local copies, waits for them, and re-layouts  6.55 us
    pallas_call x1, Pallas kernels, layer(): call(agg_oth_kernel, (feat_half, jax.ShapeDtypeStruct((depth, half), BF16...  5.36 us
    pallas_call x1, Pallas kernels, layer(): call(chain_kernel, jax.ShapeDtypeStruct((CHIPS, cols, width), BF16), [ssp...  4.43 us
    ppermute x12, waiting for transfers between devices, shift(): lax.ppermute(x, axis, [(i, (i + distance) % size) for i in range(size)])  2.45 us
  transfers between devices with their start and end apart: 21, of which 7 were waited for; matrix products, arithmetic and copies ran while one was open for 3% of the time, Pallas kernels for 14%

profile of v2, /device:TPU:1, one launch (start us, length us, event | category | flops | bytes accessed | tf_op | source)
XLA Modules:
  0.0 106.4 jit_solution(9129535294630517735)
XLA Ops:
  3.6 3.3 %collective-permute-start.4 = (bf16[256,256]{1,0:T(8,128)(2,1)S(1)}, bf16[256,256]{1,0:T(8,128)(2,1)S(1)}, u32[]{:S(2)}, u32[]{:S(2)}) collective-permute-start(bf16[256,256]{1,0:T(8,128)(2,1)S(1)} %get-tuple-element.15), channel_id=1, source_target_pairs={{0,8},{8,0},{1,9},{9,1},{2,10},{10,2},{3,11},{11,3},{4,12},{12,4},... | collective-permute-start | bytes 393224 | tf_op jit(solution)/shard_map/ppermute | solution.py:197
  10.0 2.9 %collective-permute-start.10 = (bf16[2,128,256]{2,1,0:T(8,128)(2,1)S(1)}, bf16[2,128,256]{2,1,0:T(8,128)(2,1)S(1)}, u32[]{:S(2)}, u32[]{:S(2)}) collective-permute-start(bf16[2,128,256]{2,1,0:T(8,128)(2,1)S(1)} %bitcast.25), channel_id=1, source_target_pairs={{0,32},{16,48},{32,0},{48,16},{1,33},{17,49},{33,1},{49,17},{2,34}... | collective-permute-start | bytes 393224 | tf_op jit(solution)/shard_map/ppermute | solution.py:206
  14.5 1.3 %collective-permute-start.8 = (bf16[2,128,256]{2,1,0:T(8,128)(2,1)S(1)}, bf16[2,128,256]{2,1,0:T(8,128)(2,1)}, u32[]{:S(2)}, u32[]{:S(2)}) collective-permute-start(bf16[2,128,256]{2,1,0:T(8,128)(2,1)S(1)} %bitcast.27), channel_id=1, source_target_pairs={{0,16},{16,32},{32,48},{48,0},{1,17},{17,33},{33,49},{49,1},{2,18}... | collective-permute-start | bytes 393224 | tf_op jit(solution)/shard_map/ppermute | solution.py:206
  16.5 1.3 %collective-permute-start.3 = (bf16[24,128,128]{2,1,0:T(8,128)(2,1)}, bf16[24,128,128]{2,1,0:T(8,128)(2,1)S(1)}, u32[]{:S(2)}, u32[]{:S(2)}) collective-permute-start(bf16[24,128,128]{2,1,0:T(8,128)(2,1)} %bitcast.18), channel_id=1, source_target_pairs={{0,8},{8,0},{1,9},{9,1},{2,10},{10,2},{3,11},{11,3},{4,12},{12,4},... | collective-permute-start | bytes 2359304 | tf_op jit(solution)/shard_map/ppermute | solution.py:197
  17.8 1.8 %collective-permute-done.9.refs_6_ = bf16[2,128,256]{2,1,0:T(8,128)(2,1)} collective-permute-done((bf16[2,128,256]{2,1,0:T(8,128)(2,1)S(1)}, bf16[2,128,256]{2,1,0:T(8,128)(2,1)}, u32[]{:S(2)}, u32[]{:S(2)}) %collective-permute-start.9) | collective-permute-done | bytes 131104 | tf_op jit(solution)/shard_map/ppermute | solution.py:206
  19.7 2.3 %shard_map.116 = (bf16[8,128,256]{2,1,0:T(8,128)(2,1)}, bf16[8,128,256]{2,1,0:T(8,128)(2,1)}) custom-call(bf16[2,128,256]{2,1,0:T(8,128)(2,1)} %bitcast.23, bf16[2,128,256]{2,1,0:T(8,128)(2,1)} %copy-done.17, bf16[2,128,256]{2,1,0:T(8,128)(2,1)} %copy-done.16, bf16[2,128,256]{2,1,0:T(8,128)(2,1)} %copy-done.15, bf16[2,128,256]{2,1,0:T(8,128)(2,1)} %bitcast.28, ...), custom_call_target="tpu_custom_call" | custom-call | bytes 1000000 | tf_op jit(solution)/shard_map/pallas_call | solution.py:89
  22.1 2.0 %collective-permute-start.13 = (bf16[8,128,256]{2,1,0:T(8,128)(2,1)}, bf16[8,128,256]{2,1,0:T(8,128)(2,1)}, u32[]{:S(2)}, u32[]{:S(2)}) collective-permute-start(bf16[8,128,256]{2,1,0:T(8,128)(2,1)} %get-tuple-element.16.refs_0_), channel_id=1, source_target_pairs={{0,32},{16,48},{32,0},{48,16},{1,33},{17,49},{33,1},{49,17},{2,34}... | collective-permute-start | bytes 1572872 | tf_op jit(solution)/shard_map/ppermute | solution.py:206
  24.1 1.9 %collective-permute-start.12 = (bf16[8,128,256]{2,1,0:T(8,128)(2,1)}, bf16[8,128,256]{2,1,0:T(8,128)(2,1)}, u32[]{:S(2)}, u32[]{:S(2)}) collective-permute-start(bf16[8,128,256]{2,1,0:T(8,128)(2,1)} %get-tuple-element.16.refs_0_), channel_id=1, source_target_pairs={{0,48},{16,0},{32,16},{48,32},{1,49},{17,1},{33,17},{49,33},{2,50}... | collective-permute-start | bytes 1572872 | tf_op jit(solution)/shard_map/ppermute | solution.py:206
  26.0 1.7 %add_convert_fusion = bf16[256,512]{1,0:T(8,128)(2,1)} fusion(f32[256,512]{1,0:T(8,128)S(1)} %get-tuple-element.12, bf16[256,512]{1,0:T(8,128)(2,1)} %collective-permute-done), kind=kLoop, calls=%fused_computation | loop fusion | flops 393216 | bytes 1048576 | tf_op jit(solution)/shard_map/convert_element_type | solution.py:245
  27.7 4.7 %all-to-all-start = ((bf16[16,16,512]{2,1,0:T(8,128)(2,1)}), bf16[16,16,512]{2,1,0:T(8,128)(2,1)S(1)}, u32[]{:S(2)}, u32[]{:S(2)}) async-start(bf16[16,16,512]{2,1,0:T(8,128)(2,1)} %bitcast.4), calls=%async_computation | async-start | bytes 524288 | tf_op jit(solution)/shard_map/all_to_all | solution.py:201
  32.5 1.4 %collective-permute-start.11 = (bf16[8,128,256]{2,1,0:T(8,128)(2,1)S(1)}, bf16[8,128,256]{2,1,0:T(8,128)(2,1)}, u32[]{:S(2)}, u32[]{:S(2)}) collective-permute-start(bf16[8,128,256]{2,1,0:T(8,128)(2,1)S(1)} %copy-done.11), channel_id=1, source_target_pairs={{0,16},{16,32},{32,48},{48,0},{1,17},{17,33},{33,49},{49,1},{2,18}... | collective-permute-start | bytes 1572872 | tf_op jit(solution)/shard_map/ppermute | solution.py:206
  33.9 2.8 %collective-permute-start.2 = (s32[2,24]{1,0:T(2,128)S(1)}, s32[2,24]{1,0:T(2,128)S(1)}, u32[]{:S(2)}, u32[]{:S(2)}) collective-permute-start(s32[2,24]{1,0:T(2,128)S(1)} %pad_add_fusion.own_idx), channel_id=1, source_target_pairs={{0,8},{8,0},{1,9},{9,1},{2,10},{10,2},{3,11},{11,3},{4,12},{12,4},... | collective-permute-start | bytes 584 | tf_op jit(solution)/shard_map/ppermute | solution.py:197
  36.8 13.9 %all-to-all-done.parts_ref = bf16[16,16,512]{2,1,0:T(8,128)(2,1)S(1)} async-done(((bf16[16,16,512]{2,1,0:T(8,128)(2,1)}), bf16[16,16,512]{2,1,0:T(8,128)(2,1)S(1)}, u32[]{:S(2)}, u32[]{:S(2)}) %all-to-all-start) | async-done | bytes 262176 | tf_op jit(solution)/shard_map/all_to_all | solution.py:201
  51.4 1.6 %shard_map.114 = bf16[8,16,512]{2,1,0:T(8,128)(2,1)} custom-call(bf16[16,16,512]{2,1,0:T(8,128)(2,1)} %copy-done.9), custom_call_target="tpu_custom_call" | custom-call | flops 10000000 | bytes 1000000 | tf_op jit(solution)/shard_map/pallas_call | solution.py:250
  53.0 8.2 %all-to-all-start.1 = ((bf16[8,16,512]{2,1,0:T(8,128)(2,1)}), bf16[8,16,512]{2,1,0:T(8,128)(2,1)S(1)}, u32[]{:S(2)}, u32[]{:S(2)}) async-start(bf16[8,16,512]{2,1,0:T(8,128)(2,1)} %shard_map.114), calls=%async_computation.1 | async-start | bytes 262144 | tf_op jit(solution)/shard_map/all_to_all | solution.py:201
  62.3 2.7 %collective-permute-start.15 = (bf16[8,128,256]{2,1,0:T(8,128)(2,1)}, bf16[8,128,256]{2,1,0:T(8,128)(2,1)}, u32[]{:S(2)}, u32[]{:S(2)}) collective-permute-start(bf16[8,128,256]{2,1,0:T(8,128)(2,1)} %get-tuple-element.17.refs_4_), channel_id=1, source_target_pairs={{0,192},{64,0},{128,64},{192,128},{1,193},{65,1},{129,65},{193,129... | collective-permute-start | bytes 1572872 | tf_op jit(solution)/shard_map/ppermute | solution.py:206
  66.4 2.8 %all-to-all-done.1.summ_ref = bf16[8,16,512]{2,1,0:T(8,128)(2,1)S(1)} async-done(((bf16[8,16,512]{2,1,0:T(8,128)(2,1)}), bf16[8,16,512]{2,1,0:T(8,128)(2,1)S(1)}, u32[]{:S(2)}, u32[]{:S(2)}) %all-to-all-start.1) | async-done | bytes 131104 | tf_op jit(solution)/shard_map/all_to_all | solution.py:201
  69.8 4.4 %shard_map.115 = bf16[16,16,512]{2,1,0:T(8,128)(2,1)} custom-call(s32[2]{0:T(128)} %pad_add_fusion.1.meta_ref, bf16[8,16,512]{2,1,0:T(8,128)(2,1)} %copy-done.13, bf16[3,512,512]{2,1,0:T(8,128)(2,1)} %w_in_hbm.1, bf16[3,512,512]{2,1,0:T(8,128)(2,1)} %w_state_hbm.1, f32[1,512]{1,0:T(1,128)} %bitcast.29, f32[512,128]{1,0:T(8,128)} %constant_dynamic-slice_fusion.start_ref), custom_call_target="tpu_custom_call" | custom-call | flops 100000000 | bytes 1000000 | tf_op jit(solution)/shard_map/pallas_call | solution.py:291
  74.3 6.9 %all-to-all-start.2 = ((bf16[16,16,512]{2,1,0:T(8,128)(2,1)}), bf16[16,16,512]{2,1,0:T(8,128)(2,1)S(1)}, u32[]{:S(2)}, u32[]{:S(2)}) async-start(bf16[16,16,512]{2,1,0:T(8,128)(2,1)} %shard_map.115), calls=%async_computation.2 | async-start | bytes 524288 | tf_op jit(solution)/shard_map/all_to_all | solution.py:201
  81.2 11.7 %all-to-all-done.2 = bf16[16,16,512]{2,1,0:T(8,128)(2,1)S(1)} async-done(((bf16[16,16,512]{2,1,0:T(8,128)(2,1)}), bf16[16,16,512]{2,1,0:T(8,128)(2,1)S(1)}, u32[]{:S(2)}, u32[]{:S(2)}) %all-to-all-start.2) | async-done | bytes 262176 | tf_op jit(solution)/shard_map/all_to_all | solution.py:201
  92.9 1.7 %collective-permute-start.1 = (bf16[256,512]{1,0:T(8,128)(2,1)S(1)}, bf16[256,512]{1,0:T(8,128)(2,1)S(1)}, u32[]{:S(2)}, u32[]{:S(2)}) collective-permute-start(bf16[256,512]{1,0:T(8,128)(2,1)S(1)} %bitcast.16), channel_id=1, source_target_pairs={{0,8},{8,0},{1,9},{9,1},{2,10},{10,2},{3,11},{11,3},{4,12},{12,4},... | collective-permute-start | bytes 786440 | tf_op jit(solution)/shard_map/ppermute | solution.py:197
  96.9 5.4 %shard_map.117 = (bf16[256,256]{1,0:T(8,128)(2,1)}, bf16[3072,256]{1,0:T(8,128)(2,1)}) custom-call(s32[3]{0:T(128)} %pad_add_fusion.2.here, s32[2,24]{1,0:T(2,128)} %copy-done.7, s32[2,24]{1,0:T(2,128)} %copy-done.19, bf16[24,128,128]{2,1,0:T(8,128)(2,1)} %copy-done.10, bf16[256,256]{1,0:T(8,128)(2,1)} %copy-done.14, ...), custom_call_target="tpu_custom_call" | custom-call | flops 100000000 | bytes 1000000 | tf_op jit(solution)/shard_map/pallas_call | solution.py:270
  102.4 1.4 %copy-done.1 = bf16[3072,256]{1,0:T(8,128)(2,1)S(1)} copy-done((bf16[3072,256]{1,0:T(8,128)(2,1)S(1)}, bf16[3072,256]{1,0:T(8,128)(2,1)}, u32[]{:S(2)}) %copy-start.1) | copy-done | bytes 1572888
  105.0 1.4 %shard_map.119 = (bf16[256,512]{1,0:T(8,128)(2,1)}, f32[512,512]{1,0:T(8,128)}) custom-call(s32[1]{0:T(128)} %bitcast.core_ref, bf16[256,512]{1,0:T(8,128)(2,1)S(1)} %bitcast.17, bf16[256,512]{1,0:T(8,128)(2,1)S(1)} %collective-permute-done.1.wt_oth, bf16[256,256]{1,0:T(8,128)(2,1)S(1)} %shard_map.118.agg_own, ...), custom_call_target="tpu_custom_call" | custom-call | flops 100000000 | bytes 1000000 | tf_op jit(solution)/shard_map/pallas_call | solution.py:308
  (75 shorter events, 15.2 us)
Async XLA Ops:
  0.6 65.0 %copy-start = (f32[512,512]{1,0:T(8,128)S(1)}, f32[512,512]{1,0:T(8,128)}, u32[]{:S(2)}) copy-start(f32[512,512]{1,0:T(8,128)} %param.19) | copy-start | bytes 3145732
  2.7 31.2 %copy-start.21 = (s32[1,24]{1,0:T(1,128)S(1)}, s32[1,24]{1,0:T(1,128)}, u32[]{:S(2)}) copy-start(s32[1,24]{1,0:T(1,128)} %param.12) | copy-start | bytes 292
  3.6 6.5 %collective-permute-start.4 = (bf16[256,256]{1,0:T(8,128)(2,1)S(1)}, bf16[256,256]{1,0:T(8,128)(2,1)S(1)}, u32[]{:S(2)}, u32[]{:S(2)}) collective-permute-start(bf16[256,256]{1,0:T(8,128)(2,1)S(1)} %get-tuple-element.15), channel_id=1, source_target_pairs={{0,8},{8,0},{1,9},{9,1},{2,10},{10,2},{3,11},{11,3},{4,12},{12,4},... | collective-permute-start | bytes 393224 | tf_op jit(solution)/shard_map/ppermute | solution.py:197
  6.8 6.5 %collective-permute-start.7 = (bf16[2,128,256]{2,1,0:T(8,128)(2,1)S(1)}, bf16[2,128,256]{2,1,0:T(8,128)(2,1)S(1)}, u32[]{:S(2)}, u32[]{:S(2)}) collective-permute-start(bf16[2,128,256]{2,1,0:T(8,128)(2,1)S(1)} %bitcast.20), channel_id=1, source_target_pairs={{0,128},{64,192},{128,0},{192,64},{1,129},{65,193},{129,1},{193,65... | collective-permute-start | bytes 393224 | tf_op jit(solution)/shard_map/ppermute | solution.py:206
  7.9 6.6 %collective-permute-start.6 = (bf16[2,128,256]{2,1,0:T(8,128)(2,1)S(1)}, bf16[2,128,256]{2,1,0:T(8,128)(2,1)S(1)}, u32[]{:S(2)}, u32[]{:S(2)}) collective-permute-start(bf16[2,128,256]{2,1,0:T(8,128)(2,1)S(1)} %bitcast.21), channel_id=1, source_target_pairs={{0,192},{64,0},{128,64},{192,128},{1,193},{65,1},{129,65},{193,129... | collective-permute-start | bytes 393224 | tf_op jit(solution)/shard_map/ppermute | solution.py:206
  8.7 17.3 %collective-permute-start = (bf16[256,512]{1,0:T(8,128)(2,1)S(1)}, bf16[256,512]{1,0:T(8,128)(2,1)}, u32[]{:S(2)}, u32[]{:S(2)}) collective-permute-start(bf16[256,512]{1,0:T(8,128)(2,1)S(1)} %get-tuple-element.13), channel_id=1, source_target_pairs={{0,8},{8,0},{1,9},{9,1},{2,10},{10,2},{3,11},{11,3},{4,12},{12,4},... | collective-permute-start | bytes 786440 | tf_op jit(solution)/shard_map/ppermute | solution.py:197
  9.4 7.0 %collective-permute-start.5 = (bf16[2,128,256]{2,1,0:T(8,128)(2,1)S(1)}, bf16[2,128,256]{2,1,0:T(8,128)(2,1)S(1)}, u32[]{:S(2)}, u32[]{:S(2)}) collective-permute-start(bf16[2,128,256]{2,1,0:T(8,128)(2,1)S(1)} %bitcast.22), channel_id=1, source_target_pairs={{0,64},{64,128},{128,192},{192,0},{1,65},{65,129},{129,193},{193,1... | collective-permute-start | bytes 393224 | tf_op jit(solution)/shard_map/ppermute | solution.py:206
  10.0 7.8 %collective-permute-start.10 = (bf16[2,128,256]{2,1,0:T(8,128)(2,1)S(1)}, bf16[2,128,256]{2,1,0:T(8,128)(2,1)S(1)}, u32[]{:S(2)}, u32[]{:S(2)}) collective-permute-start(bf16[2,128,256]{2,1,0:T(8,128)(2,1)S(1)} %bitcast.25), channel_id=1, source_target_pairs={{0,32},{16,48},{32,0},{48,16},{1,33},{17,49},{33,1},{49,17},{2,34}... | collective-permute-start | bytes 393224 | tf_op jit(solution)/shard_map/ppermute | solution.py:206
  13.3 6.2 %collective-permute-start.9 = (bf16[2,128,256]{2,1,0:T(8,128)(2,1)S(1)}, bf16[2,128,256]{2,1,0:T(8,128)(2,1)}, u32[]{:S(2)}, u32[]{:S(2)}) collective-permute-start(bf16[2,128,256]{2,1,0:T(8,128)(2,1)S(1)} %bitcast.26), channel_id=1, source_target_pairs={{0,48},{16,0},{32,16},{48,32},{1,49},{17,1},{33,17},{49,33},{2,50}... | collective-permute-start | bytes 393224 | tf_op jit(solution)/shard_map/ppermute | solution.py:206
  14.5 5.2 %collective-permute-start.8 = (bf16[2,128,256]{2,1,0:T(8,128)(2,1)S(1)}, bf16[2,128,256]{2,1,0:T(8,128)(2,1)}, u32[]{:S(2)}, u32[]{:S(2)}) collective-permute-start(bf16[2,128,256]{2,1,0:T(8,128)(2,1)S(1)} %bitcast.27), channel_id=1, source_target_pairs={{0,16},{16,32},{32,48},{48,0},{1,17},{17,33},{33,49},{49,1},{2,18}... | collective-permute-start | bytes 393224 | tf_op jit(solution)/shard_map/ppermute | solution.py:206
  16.5 78.8 %collective-permute-start.3 = (bf16[24,128,128]{2,1,0:T(8,128)(2,1)}, bf16[24,128,128]{2,1,0:T(8,128)(2,1)S(1)}, u32[]{:S(2)}, u32[]{:S(2)}) collective-permute-start(bf16[24,128,128]{2,1,0:T(8,128)(2,1)} %bitcast.18), channel_id=1, source_target_pairs={{0,8},{8,0},{1,9},{9,1},{2,10},{10,2},{3,11},{11,3},{4,12},{12,4},... | collective-permute-start | bytes 2359304 | tf_op jit(solution)/shard_map/ppermute | solution.py:197
  22.1 40.3 %collective-permute-start.13 = (bf16[8,128,256]{2,1,0:T(8,128)(2,1)}, bf16[8,128,256]{2,1,0:T(8,128)(2,1)}, u32[]{:S(2)}, u32[]{:S(2)}) collective-permute-start(bf16[8,128,256]{2,1,0:T(8,128)(2,1)} %get-tuple-element.16.refs_0_), channel_id=1, source_target_pairs={{0,32},{16,48},{32,0},{48,16},{1,33},{17,49},{33,1},{49,17},{2,34}... | collective-permute-start | bytes 1572872 | tf_op jit(solution)/shard_map/ppermute | solution.py:206
  24.1 41.0 %collective-permute-start.12 = (bf16[8,128,256]{2,1,0:T(8,128)(2,1)}, bf16[8,128,256]{2,1,0:T(8,128)(2,1)}, u32[]{:S(2)}, u32[]{:S(2)}) collective-permute-start(bf16[8,128,256]{2,1,0:T(8,128)(2,1)} %get-tuple-element.16.refs_0_), channel_id=1, source_target_pairs={{0,48},{16,0},{32,16},{48,32},{1,49},{17,1},{33,17},{49,33},{2,50}... | collective-permute-start | bytes 1572872 | tf_op jit(solution)/shard_map/ppermute | solution.py:206
  27.7 22.9 %all-to-all-start = ((bf16[16,16,512]{2,1,0:T(8,128)(2,1)}), bf16[16,16,512]{2,1,0:T(8,128)(2,1)S(1)}, u32[]{:S(2)}, u32[]{:S(2)}) async-start(bf16[16,16,512]{2,1,0:T(8,128)(2,1)} %bitcast.4), calls=%async_computation | async-start | bytes 524288 | tf_op jit(solution)/shard_map/all_to_all | solution.py:201
  32.5 48.7 %collective-permute-start.11 = (bf16[8,128,256]{2,1,0:T(8,128)(2,1)S(1)}, bf16[8,128,256]{2,1,0:T(8,128)(2,1)}, u32[]{:S(2)}, u32[]{:S(2)}) collective-permute-start(bf16[8,128,256]{2,1,0:T(8,128)(2,1)S(1)} %copy-done.11), channel_id=1, source_target_pairs={{0,16},{16,32},{32,48},{48,0},{1,17},{17,33},{33,49},{49,1},{2,18}... | collective-permute-start | bytes 1572872 | tf_op jit(solution)/shard_map/ppermute | solution.py:206
  33.9 40.3 %copy-start.7 = (s32[2,24]{1,0:T(2,128)}, s32[2,24]{1,0:T(2,128)S(1)}, u32[]{:S(2)}) copy-start(s32[2,24]{1,0:T(2,128)S(1)} %pad_add_fusion.own_idx) | copy-start | bytes 580
  33.9 27.3 %collective-permute-start.2 = (s32[2,24]{1,0:T(2,128)S(1)}, s32[2,24]{1,0:T(2,128)S(1)}, u32[]{:S(2)}, u32[]{:S(2)}) collective-permute-start(s32[2,24]{1,0:T(2,128)S(1)} %pad_add_fusion.own_idx), channel_id=1, source_target_pairs={{0,8},{8,0},{1,9},{9,1},{2,10},{10,2},{3,11},{11,3},{4,12},{12,4},... | collective-permute-start | bytes 584 | tf_op jit(solution)/shard_map/ppermute | solution.py:197
  53.0 16.1 %all-to-all-start.1 = ((bf16[8,16,512]{2,1,0:T(8,128)(2,1)}), bf16[8,16,512]{2,1,0:T(8,128)(2,1)S(1)}, u32[]{:S(2)}, u32[]{:S(2)}) async-start(bf16[8,16,512]{2,1,0:T(8,128)(2,1)} %shard_map.114), calls=%async_computation.1 | async-start | bytes 262144 | tf_op jit(solution)/shard_map/all_to_all | solution.py:201
  61.2 34.0 %collective-permute-start.16 = (bf16[8,128,256]{2,1,0:T(8,128)(2,1)}, bf16[8,128,256]{2,1,0:T(8,128)(2,1)S(1)}, u32[]{:S(2)}, u32[]{:S(2)}) collective-permute-start(bf16[8,128,256]{2,1,0:T(8,128)(2,1)} %get-tuple-element.17.refs_4_), channel_id=1, source_target_pairs={{0,128},{64,192},{128,0},{192,64},{1,129},{65,193},{129,1},{193,65... | collective-permute-start | bytes 1572872 | tf_op jit(solution)/shard_map/ppermute | solution.py:206
  62.3 32.9 %collective-permute-start.15 = (bf16[8,128,256]{2,1,0:T(8,128)(2,1)}, bf16[8,128,256]{2,1,0:T(8,128)(2,1)}, u32[]{:S(2)}, u32[]{:S(2)}) collective-permute-start(bf16[8,128,256]{2,1,0:T(8,128)(2,1)} %get-tuple-element.17.refs_4_), channel_id=1, source_target_pairs={{0,192},{64,0},{128,64},{192,128},{1,193},{65,1},{129,65},{193,129... | collective-permute-start | bytes 1572872 | tf_op jit(solution)/shard_map/ppermute | solution.py:206
  65.0 30.2 %collective-permute-start.14 = (bf16[8,128,256]{2,1,0:T(8,128)(2,1)}, bf16[8,128,256]{2,1,0:T(8,128)(2,1)}, u32[]{:S(2)}, u32[]{:S(2)}) collective-permute-start(bf16[8,128,256]{2,1,0:T(8,128)(2,1)} %get-tuple-element.17.refs_4_), channel_id=1, source_target_pairs={{0,64},{64,128},{128,192},{192,0},{1,65},{65,129},{129,193},{193,1... | collective-permute-start | bytes 1572872 | tf_op jit(solution)/shard_map/ppermute | solution.py:206
  74.3 18.6 %all-to-all-start.2 = ((bf16[16,16,512]{2,1,0:T(8,128)(2,1)}), bf16[16,16,512]{2,1,0:T(8,128)(2,1)S(1)}, u32[]{:S(2)}, u32[]{:S(2)}) async-start(bf16[16,16,512]{2,1,0:T(8,128)(2,1)} %shard_map.115), calls=%async_computation.2 | async-start | bytes 524288 | tf_op jit(solution)/shard_map/all_to_all | solution.py:201
  92.9 12.1 %collective-permute-start.1 = (bf16[256,512]{1,0:T(8,128)(2,1)S(1)}, bf16[256,512]{1,0:T(8,128)(2,1)S(1)}, u32[]{:S(2)}, u32[]{:S(2)}) collective-permute-start(bf16[256,512]{1,0:T(8,128)(2,1)S(1)} %bitcast.16), channel_id=1, source_target_pairs={{0,8},{8,0},{1,9},{9,1},{2,10},{10,2},{3,11},{11,3},{4,12},{12,4},... | collective-permute-start | bytes 786440 | tf_op jit(solution)/shard_map/ppermute | solution.py:197
  102.3 2.7 %collective-permute-start.17 = (bf16[256,256]{1,0:T(8,128)(2,1)}, bf16[256,256]{1,0:T(8,128)(2,1)S(1)}, u32[]{:S(2)}, u32[]{:S(2)}) collective-permute-start(bf16[256,256]{1,0:T(8,128)(2,1)} %get-tuple-element.19), channel_id=1, source_target_pairs={{0,8},{8,0},{1,9},{9,1},{2,10},{10,2},{3,11},{11,3},{4,12},{12,4},... | collective-permute-start | bytes 393224 | tf_op jit(solution)/shard_map/ppermute | solution.py:197
  (19 other events, 123.9 us)

commit v3 on v2

--- a/solution.py
+++ b/solution.py
@@ -10,7 +10,6 @@
 
 BLOCK = 128
 X, Y, C = 4, 4, 2
-WHOLE = 60
 CHIPS = X * Y
 F32 = jnp.float32
 BF16 = jnp.bfloat16
@@ -51,15 +50,20 @@
     )
 
 
-def pool_kernel(core_ref, feat_hbm, pool_hbm, send_ref, keep_ref, mine_ref, give_ref, feat_ref, pool_ref, sems):
+def place():
+    return tuple(lax.axis_index(axis).astype(jnp.int32) for axis in ("x", "y", "c", "z"))
+
+
+def pool_kernel(feat_hbm, pool_hbm, send_ref, keep_ref, mine_ref, give_ref, feat_ref, pool_ref, sems):
     fetch = [pltpu.make_async_copy(feat_hbm, feat_ref, sems.at[0]), pltpu.make_async_copy(pool_hbm, pool_ref, sems.at[1])]
     for cp in fetch:
         cp.start()
     for cp in fetch:
         cp.wait()
     half = send_ref.shape[0]
-    own = pl.multiple_of(core_ref[0] * half, half)
-    other = pl.multiple_of((1 - core_ref[0]) * half, half)
+    core = place()[2]
+    own = pl.multiple_of(core * half, half)
+    other = pl.multiple_of((1 - core) * half, half)
     feat = feat_ref[...]
     gates = jax.nn.sigmoid(mm(feat, pool_ref[:, pl.ds(other, half)], NN)).astype(BF16)
     send_ref[...] = mm(gates, feat, TN).astype(BF16)
@@ -92,7 +96,6 @@
         [pl.BlockSpec(memory_space=pl.ANY)] * len(pieces),
         scratch=[pltpu.SemaphoreType.DMA((len(pieces),))],
         flops=0,
-        vmem_mib=WHOLE,
     )(*pieces)
 
 
@@ -101,26 +104,19 @@
     out_ref[...] = jnp.broadcast_to(total.astype(BF16)[None], out_ref.shape)
 
 
-def chain_kernel(
-    meta_ref, summ_ref, w_in_hbm, w_state_hbm, offset_ref, start_ref, out_hbm, side_ref, startt_ref, w_in_ref, w_ref, out_ref, sems
-):
-    fetch_in = pltpu.make_async_copy(w_in_hbm, w_in_ref, sems.at[2])
-    fetch_in.start()
-    fetch = pltpu.make_async_copy(w_state_hbm, w_ref, sems.at[0])
-    fetch.start()
+def chain_kernel(summ_ref, w_in_ref, w_ref, offset_ref, start_ref, out_ref, side_ref, startt_ref):
     n_t, cols, width = summ_ref.shape
+    x, y, core, last = place()
+    col0 = core * (width // C) + (x * Y + y) * cols
+    window = pl.multiple_of((col0 // BLOCK) * BLOCK, BLOCK)
+    startt_ref[...] = start_ref[:, pl.ds(window, BLOCK)].T
     summ = summ_ref[...].reshape(n_t * cols, width)
-    startt_ref[...] = start_ref[...].T
-    fetch_in.wait()
     for g in range(3):
         side = mm(summ, w_in_ref[g], NT)
         if g == 0:
             side = side - offset_ref[...]
         side_ref[g] = side.reshape(n_t, cols, width)
-    col0 = pl.multiple_of(meta_ref[1], cols)
-    state = startt_ref[pl.ds(col0, cols), :]
-    last = meta_ref[0]
-    fetch.wait()
+    state = startt_ref[pl.ds(pl.multiple_of(lax.rem(col0, BLOCK), cols), cols), :]
 
     def step(t, state):
         state_b = state.astype(BF16)
@@ -131,17 +127,15 @@
 
     state = lax.fori_loop(0, last + 1, step, state)
     out_ref[...] = jnp.broadcast_to(state.astype(BF16)[None], out_ref.shape)
-    store = pltpu.make_async_copy(out_ref, out_hbm, sems.at[1])
-    store.start()
-    store.wait()
-
-
-def masked(idx, tiles, lhs):
+
+
+def masked(rows, used, tiles, lhs):
     for j in range(tiles.shape[0]):
         tile = tiles[j]
+        at = jnp.where(j < used[0, 0], rows[0, j] & 1, 2)
         for r in range(2):
             lhs[r * BLOCK : (r + 1) * BLOCK, j * BLOCK : (j + 1) * BLOCK] = jnp.where(
-                idx[1, j] == r, tile, jnp.zeros_like(tile)
+                at == r, tile, jnp.zeros_like(tile)
             )
 
 
@@ -149,7 +143,7 @@
     return jnp.where(step == 0, 0, jnp.where(step == 3, 1, step + 1))
 
 
-def agg_oth_kernel(here, own_idx, oth_idx, tiles, feat, *refs):
+def agg_oth_kernel(cols_own, cols_oth, rows_oth, used_oth, tiles, feat, *refs):
     pieces, (agg, rhs_own, blocks, rhs, lhs, sems) = refs[:-6], refs[-6:]
     copies = []
     first = 0
@@ -158,31 +152,31 @@
         cp.start()
         copies.append(cp)
         first += piece.shape[0]
-    masked(oth_idx, tiles, lhs)
+    masked(rows_oth, used_oth, tiles, lhs)
     for cp in copies:
         cp.wait()
-    per_dev = first // (CHIPS * C)
-    for idx, out in ((oth_idx, rhs), (own_idx, rhs_own)):
+    x, y, core, _ = place()
+    for cols, out in ((cols_oth, rhs), (cols_own, rhs_own)):
         for j in range(tiles.shape[0]):
-            col = idx[0, j]
-            owner = lax.div(col, per_dev)
-            in_x = slot_of((lax.div(owner, Y * C) - here[0]) & 3)
-            in_y = slot_of((lax.div(owner, C) - here[1]) & 3)
-            same = (owner & 1) == here[2]
-            place = jnp.where(same, in_y * 4 + in_x, in_x * 4 + in_y + CHIPS)
-            out[j * BLOCK : (j + 1) * BLOCK, :] = blocks[place * per_dev + lax.rem(col, per_dev)]
+            col = cols[0, j]
+            owner = col >> 1
+            in_x = slot_of(((owner >> 3) - x) & 3)
+            in_y = slot_of(((owner >> 1) - y) & 3)
+            slot = jnp.where((owner & 1) == core, in_y * 4 + in_x, in_x * 4 + in_y + CHIPS)
+            out[j * BLOCK : (j + 1) * BLOCK, :] = blocks[slot * 2 + (col & 1)]
     agg[...] = (feat[...].astype(F32) + mm(lhs[...], rhs[...], NN)).astype(BF16)
 
 
-def agg_own_kernel(own_idx, tiles, feat, rhs, agg, lhs):
-    masked(own_idx, tiles, lhs)
+def agg_own_kernel(rows, used, tiles, feat, rhs, agg, lhs):
+    masked(rows, used, tiles, lhs)
     agg[...] = (feat[...].astype(F32) + mm(lhs[...], rhs[...], NN)).astype(BF16)
 
 
-def final_kernel(core_ref, wt_own, wt_oth, agg_own, agg_oth, hid_ref, w_ref, wt, agg):
+def final_kernel(wt_own, wt_oth, agg_own, agg_oth, hid_ref, w_ref, wt, agg):
     half = wt_own.shape[0]
-    own = pl.multiple_of(core_ref[0] * half, half)
-    oth = pl.multiple_of((1 - core_ref[0]) * half, half)
+    core = place()[2]
+    own = pl.multiple_of(core * half, half)
+    oth = pl.multiple_of((1 - core) * half, half)
     wt[pl.ds(own, half), :] = wt_own[...]
     wt[pl.ds(oth, half), :] = wt_oth[...]
     agg[:, pl.ds(own, half)] = agg_own[...]
@@ -226,11 +220,6 @@
     slots = tile_rows.shape[1]
     half = width // 2
     n_tm = lax.axis_size("z")
-    core = lax.axis_index("c").astype(jnp.int32)
-    chip = (lax.axis_index("x") * Y + lax.axis_index("y")).astype(jnp.int32)
-    dom = chip * C + core
-    t_index = lax.axis_index("z").astype(jnp.int32)
-    core_s = core.reshape(1)
     feat = features[0]
     blocks_dev = rows_dev // BLOCK
 
@@ -239,15 +228,15 @@
     send, keep, feat_mine, feat_give = call(
         pool_kernel,
         (bf_half, jax.ShapeDtypeStruct((half, width), F32), feat_half, feat_half),
-        [sspec(), hspec(), hspec()],
+        [hspec(), hspec()],
         scratch=[pltpu.VMEM(feat.shape, BF16), pltpu.VMEM(pool_weight.shape, BF16), pltpu.SemaphoreType.DMA((2,))],
-    )(core_s, feat, pool_weight)
+    )(feat, pool_weight)
     partial = (keep + swap(send).astype(F32)).astype(BF16)
     cols = half // CHIPS
     parts = trade(partial.reshape(CHIPS, cols, width), ("x", "y"))
     snaps = jax.ShapeDtypeStruct((n_tm, cols, width), BF16)
     scale = (rows_dev * CHIPS * C) ** (-0.5)
-    summ = call(functools.partial(sum_kernel, scale), snaps, [vspec()], flops=10**7, vmem_mib=WHOLE)(parts)
+    summ = call(functools.partial(sum_kernel, scale), snaps, [vspec()], flops=10**7)(parts)
     summ = trade(summ, "z")
 
     feat_oth = swap(feat_give)
@@ -257,60 +246,46 @@
     joined_a, joined_b = join(blocks_a, blocks_b)
     gathered = spread(joined_a, "y") + spread(joined_b, "x")
 
-    live = jnp.arange(slots, dtype=jnp.int32) < tile_used[0, 0]
-    where_to = jnp.where(live, tile_rows[0] - dom * blocks_dev, blocks_dev)
-    own_idx = jnp.stack([tile_cols[0], where_to])
-    oth_idx = swap(own_idx)
-
+    rows_oth, cols_oth, used_oth = swap(tile_rows), swap(tile_cols), swap(tile_used)
     tiles_own = tile_vals[0]
     tiles_oth = swap(tiles_own)
-    here = jnp.stack([lax.axis_index("x"), lax.axis_index("y"), core]).astype(jnp.int32)
     depth = slots * BLOCK
     lhs = pltpu.VMEM((rows_dev, depth), BF16)
     agg_give, rhs_own = call(
         agg_oth_kernel,
         (feat_half, jax.ShapeDtypeStruct((depth, half), BF16)),
-        [sspec()] * 3 + [vspec()] * 2 + [pl.BlockSpec(memory_space=pl.ANY)] * len(gathered),
+        [sspec()] * 4 + [vspec()] * 2 + [pl.BlockSpec(memory_space=pl.ANY)] * len(gathered),
         scratch=[
             pltpu.VMEM((CHIPS * C * blocks_dev, BLOCK, half), BF16),
             pltpu.VMEM((depth, half), BF16),
             lhs,
             pltpu.SemaphoreType.DMA((len(gathered),)),
         ],
-        vmem_mib=WHOLE,
-    )(here, own_idx, oth_idx, tiles_oth, feat_oth, *gathered)
+        vmem_mib=16,
+    )(tile_cols, cols_oth, rows_oth, used_oth, tiles_oth, feat_oth, *gathered)
     agg_oth = swap(agg_give)
     agg_own = call(
-        agg_own_kernel, feat_half, [sspec()] + [vspec()] * 3, scratch=[lhs], vmem_mib=8
-    )(own_idx, tiles_own, feat_mine, rhs_own)
-
-    col0 = core * half + chip * cols
-    lane0 = col0 // BLOCK
-    start_cols = lax.dynamic_slice_in_dim(start_weight, lane0 * BLOCK, BLOCK, 1)
-    meta = jnp.stack([t_index, col0 % BLOCK])
+        agg_own_kernel, feat_half, [sspec()] * 2 + [vspec()] * 3, scratch=[lhs], vmem_mib=8
+    )(tile_rows, tile_used, tiles_own, feat_mine, rhs_own)
+
     evolved = call(
         chain_kernel,
         jax.ShapeDtypeStruct((CHIPS, cols, width), BF16),
-        [sspec(), vspec(), hspec(), hspec(), vspec(), vspec()],
+        [vspec()] * 5,
         scratch=[
             pltpu.VMEM((3, n_tm, cols, width), F32),
             pltpu.VMEM((BLOCK, width), F32),
-            pltpu.VMEM(w_in.shape, BF16),
-            pltpu.VMEM(w_state.shape, BF16),
-            pltpu.VMEM((CHIPS, cols, width), BF16),
-            pltpu.SemaphoreType.DMA((3,)),
         ],
-        out=hspec(),
-        vmem_mib=WHOLE,
-    )(meta, summ, w_in, w_state, gate_offset[None, :], start_cols)
+        vmem_mib=8,
+    )(summ, w_in, w_state, gate_offset[None, :], start_weight)
     wt_own = trade(evolved, ("x", "y")).reshape(half, width)
     wt_oth = swap(wt_own)
     hidden, weights = call(
         final_kernel,
         (jax.ShapeDtypeStruct((rows_dev, width), BF16), jax.ShapeDtypeStruct((width, width), F32)),
-        [sspec(), vspec(), vspec(), vspec(), vspec()],
+        [vspec(), vspec(), vspec(), vspec()],
         scratch=[pltpu.VMEM((width, width), BF16), pltpu.VMEM((rows_dev, width), BF16)],
-    )(core_s, wt_own, wt_oth, agg_own, agg_oth)
+    )(wt_own, wt_oth, agg_own, agg_oth)
     return hidden[None], weights[None]
 
 

time: 107 us -> 108 us (level)
  waiting for transfers between devices: 30.8 us -> 40.7 us
  Pallas kernels: 17.2 us -> 13 us
  other arithmetic: 2.94 us -> 0.77 us
  local copies, waits for them, and re-layouts: 7.29 us -> 5.69 us
    all_to_all x3, waiting for transfers between devices: 28.4 us -> 33.8 us  [trade(): return lax.all_to_all(x, axes, split_axis=0, concat_axis=0, tiled=True)]
    pallas_call x3, Pallas kernels: 7.26 us -> 3.88 us  [the longest x1 1.97 us: layer(): call(chain_kernel, jax.ShapeDtypeStruct((CHIPS, cols, width), BF16), [vsp...]
    ppermute x6 -> x8, waiting for transfers between devices: 0.02 us -> 2.74 us  [swap(): return lax.ppermute(x, 'c', [(0, 1), (1, 0)])]
    ppermute x12, waiting for transfers between devices: 2.45 us -> 4.21 us  [shift(): lax.ppermute(x, axis, [(i, (i + distance) % size) for i in range(size)])]
    another operation x3 -> x0, other arithmetic: 1.21 us -> none  [the longest x1 0.61 us: layer(): meta = jnp.stack([t_index, col0 % BLOCK])]
    unnamed x44 -> x30, local copies, waits for them, and re-layouts: 6.55 us -> 5.69 us
    ppermute x6 -> x8, starting transfers between devices: 9.88 us -> 9.97 us  [swap(): return lax.ppermute(x, 'c', [(0, 1), (1, 0)])]
  transfers between devices with their start and end apart: 21 -> 23, of which waited for: 7 -> 9; matrix products, arithmetic and copies ran while one was open for 3% -> 1% of each run, Pallas kernels for 14% -> 10%
where the time goes in v3:
time: 108 us
  starting transfers between devices  46 us (43%)
  waiting for transfers between devices  40.7 us (38%)
  Pallas kernels  13 us (12%)
  local copies, waits for them, and re-layouts  5.69 us (5%)
  between operations  1.51 us (1%)
    all_to_all x3, waiting for transfers between devices, trade(): return lax.all_to_all(x, axes, split_axis=0, concat_axis=0, tiled=True)  33.8 us
    all_to_all x3, starting transfers between devices, trade(): return lax.all_to_all(x, axes, split_axis=0, concat_axis=0, tiled=True)  19.1 us
    ppermute x12, starting transfers between devices, shift(): lax.ppermute(x, axis, [(i, (i + distance) % size) for i in range(size)])  16.9 us
    ppermute x8, starting transfers between devices, swap(): return lax.ppermute(x, 'c', [(0, 1), (1, 0)])  9.97 us
    unnamed x30, local copies, waits for them, and re-layouts  5.69 us
    pallas_call x1, Pallas kernels, layer(): call(agg_oth_kernel, (feat_half, jax.ShapeDtypeStruct((depth, half), BF16...  4.61 us
    ppermute x12, waiting for transfers between devices, shift(): lax.ppermute(x, axis, [(i, (i + distance) % size) for i in range(size)])  4.21 us
    ppermute x8, waiting for transfers between devices, swap(): return lax.ppermute(x, 'c', [(0, 1), (1, 0)])  2.74 us
  transfers between devices with their start and end apart: 23, of which 9 were waited for; matrix products, arithmetic and copies ran while one was open for 1% of the time, Pallas kernels for 10%

profile of v3, /device:TPU:1, one launch (start us, length us, event | category | flops | bytes accessed | tf_op | source)
XLA Modules:
  0.0 107.6 jit_solution(5326224653564729753)
XLA Ops:
  3.4 3.3 %collective-permute-start.6 = (bf16[256,256]{1,0:T(8,128)(2,1)S(1)}, bf16[256,256]{1,0:T(8,128)(2,1)S(1)}, u32[]{:S(2)}, u32[]{:S(2)}) collective-permute-start(bf16[256,256]{1,0:T(8,128)(2,1)S(1)} %get-tuple-element.15), channel_id=1, source_target_pairs={{0,8},{8,0},{1,9},{9,1},{2,10},{10,2},{3,11},{11,3},{4,12},{12,4},... | collective-permute-start | bytes 393224 | tf_op jit(solution)/shard_map/ppermute | solution.py:191
  6.7 1.0 collective-permute-start.9
  9.9 3.0 %collective-permute-start.12 = (bf16[2,128,256]{2,1,0:T(8,128)(2,1)S(1)}, bf16[2,128,256]{2,1,0:T(8,128)(2,1)S(1)}, u32[]{:S(2)}, u32[]{:S(2)}) collective-permute-start(bf16[2,128,256]{2,1,0:T(8,128)(2,1)S(1)} %bitcast.17), channel_id=1, source_target_pairs={{0,32},{16,48},{32,0},{48,16},{1,33},{17,49},{33,1},{49,17},{2,34}... | collective-permute-start | bytes 393224 | tf_op jit(solution)/shard_map/ppermute | solution.py:200
  14.4 1.3 %collective-permute-start.10 = (bf16[2,128,256]{2,1,0:T(8,128)(2,1)S(1)}, bf16[2,128,256]{2,1,0:T(8,128)(2,1)S(1)}, u32[]{:S(2)}, u32[]{:S(2)}) collective-permute-start(bf16[2,128,256]{2,1,0:T(8,128)(2,1)S(1)} %bitcast.19), channel_id=1, source_target_pairs={{0,16},{16,32},{32,48},{48,0},{1,17},{17,33},{33,49},{49,1},{2,18}... | collective-permute-start | bytes 393224 | tf_op jit(solution)/shard_map/ppermute | solution.py:200
  16.3 3.1 %collective-permute-done.11.refs_6_ = bf16[2,128,256]{2,1,0:T(8,128)(2,1)S(1)} collective-permute-done((bf16[2,128,256]{2,1,0:T(8,128)(2,1)S(1)}, bf16[2,128,256]{2,1,0:T(8,128)(2,1)S(1)}, u32[]{:S(2)}, u32[]{:S(2)}) %collective-permute-start.11) | collective-permute-done | bytes 131104 | tf_op jit(solution)/shard_map/ppermute | solution.py:200
  19.5 2.2 %shard_map.116 = (bf16[8,128,256]{2,1,0:T(8,128)(2,1)}, bf16[8,128,256]{2,1,0:T(8,128)(2,1)S(1)}) custom-call(bf16[2,128,256]{2,1,0:T(8,128)(2,1)S(1)} %bitcast.16, bf16[2,128,256]{2,1,0:T(8,128)(2,1)S(1)} %collective-permute-done.7.refs_1_, bf16[2,128,256]{2,1,0:T(8,128)(2,1)S(1)} %collective-permute-done.8.refs_2_, ...), custom_call_target="tpu_custom_call" | custom-call | bytes 1000000 | tf_op jit(solution)/shard_map/pallas_call | solution.py:93
  22.5 2.0 %collective-permute-start.15 = (bf16[8,128,256]{2,1,0:T(8,128)(2,1)}, bf16[8,128,256]{2,1,0:T(8,128)(2,1)}, u32[]{:S(2)}, u32[]{:S(2)}) collective-permute-start(bf16[8,128,256]{2,1,0:T(8,128)(2,1)} %get-tuple-element.16.refs_0_), channel_id=1, source_target_pairs={{0,32},{16,48},{32,0},{48,16},{1,33},{17,49},{33,1},{49,17},{2,34}... | collective-permute-start | bytes 1572872 | tf_op jit(solution)/shard_map/ppermute | solution.py:200
  24.5 2.0 %collective-permute-start.14 = (bf16[8,128,256]{2,1,0:T(8,128)(2,1)}, bf16[8,128,256]{2,1,0:T(8,128)(2,1)}, u32[]{:S(2)}, u32[]{:S(2)}) collective-permute-start(bf16[8,128,256]{2,1,0:T(8,128)(2,1)} %get-tuple-element.16.refs_0_), channel_id=1, source_target_pairs={{0,48},{16,0},{32,16},{48,32},{1,49},{17,1},{33,17},{49,33},{2,50}... | collective-permute-start | bytes 1572872 | tf_op jit(solution)/shard_map/ppermute | solution.py:200
  27.3 4.6 %all-to-all-start = ((bf16[16,16,512]{2,1,0:T(8,128)(2,1)}), bf16[16,16,512]{2,1,0:T(8,128)(2,1)S(1)}, u32[]{:S(2)}, u32[]{:S(2)}) async-start(bf16[16,16,512]{2,1,0:T(8,128)(2,1)} %bitcast.23), calls=%async_computation | async-start | bytes 524288 | tf_op jit(solution)/shard_map/all_to_all | solution.py:195
  31.8 2.3 %collective-permute-start.5 = (bf16[24,128,128]{2,1,0:T(8,128)(2,1)}, bf16[24,128,128]{2,1,0:T(8,128)(2,1)}, u32[]{:S(2)}, u32[]{:S(2)}) collective-permute-start(bf16[24,128,128]{2,1,0:T(8,128)(2,1)} %bitcast.11), channel_id=1, source_target_pairs={{0,8},{8,0},{1,9},{9,1},{2,10},{10,2},{3,11},{11,3},{4,12},{12,4},... | collective-permute-start | bytes 2359304 | tf_op jit(solution)/shard_map/ppermute | solution.py:191
  34.1 1.6 %collective-permute-start.13 = (bf16[8,128,256]{2,1,0:T(8,128)(2,1)}, bf16[8,128,256]{2,1,0:T(8,128)(2,1)}, u32[]{:S(2)}, u32[]{:S(2)}) collective-permute-start(bf16[8,128,256]{2,1,0:T(8,128)(2,1)} %get-tuple-element.16.refs_0_), channel_id=1, source_target_pairs={{0,16},{16,32},{32,48},{48,0},{1,17},{17,33},{33,49},{49,1},{2,18}... | collective-permute-start | bytes 1572872 | tf_op jit(solution)/shard_map/ppermute | solution.py:200
  35.7 15.6 %all-to-all-done.parts_ref = bf16[16,16,512]{2,1,0:T(8,128)(2,1)S(1)} async-done(((bf16[16,16,512]{2,1,0:T(8,128)(2,1)}), bf16[16,16,512]{2,1,0:T(8,128)(2,1)S(1)}, u32[]{:S(2)}, u32[]{:S(2)}) %all-to-all-start) | async-done | bytes 262176 | tf_op jit(solution)/shard_map/all_to_all | solution.py:195
  51.9 8.2 %all-to-all-start.1 = ((bf16[8,16,512]{2,1,0:T(8,128)(2,1)}), bf16[8,16,512]{2,1,0:T(8,128)(2,1)S(1)}, u32[]{:S(2)}, u32[]{:S(2)}) async-start(bf16[8,16,512]{2,1,0:T(8,128)(2,1)} %shard_map.114), calls=%async_computation.1 | async-start | bytes 262144 | tf_op jit(solution)/shard_map/all_to_all | solution.py:195
  60.1 1.9 %collective-permute-start.4 = (s32[1,1]{1,0:T(1,128)}, s32[1,1]{1,0:T(1,128)}, u32[]{:S(2)}, u32[]{:S(2)}) collective-permute-start(s32[1,1]{1,0:T(1,128)} %param.14), channel_id=1, source_target_pairs={{0,8},{8,0},{1,9},{9,1},{2,10},{10,2},{3,11},{11,3},{4,12},{12,4},... | collective-permute-start | bytes 20 | tf_op jit(solution)/shard_map/ppermute | solution.py:191
  62.0 1.1 %collective-permute-done.4.used_oth = s32[1,1]{1,0:T(1,128)} collective-permute-done((s32[1,1]{1,0:T(1,128)}, s32[1,1]{1,0:T(1,128)}, u32[]{:S(2)}, u32[]{:S(2)}) %collective-permute-start.4) | collective-permute-done | bytes 36 | tf_op jit(solution)/shard_map/ppermute | solution.py:191
  66.2 2.8 %collective-permute-start.17 = (bf16[8,128,256]{2,1,0:T(8,128)(2,1)}, bf16[8,128,256]{2,1,0:T(8,128)(2,1)}, u32[]{:S(2)}, u32[]{:S(2)}) collective-permute-start(bf16[8,128,256]{2,1,0:T(8,128)(2,1)} %copy-done.4), channel_id=1, source_target_pairs={{0,192},{64,0},{128,64},{192,128},{1,193},{65,1},{129,65},{193,129... | collective-permute-start | bytes 1572872 | tf_op jit(solution)/shard_map/ppermute | solution.py:200
  69.0 1.2 %copy-done.2 = f32[512,512]{1,0:T(8,128)S(1)} copy-done((f32[512,512]{1,0:T(8,128)S(1)}, f32[512,512]{1,0:T(8,128)}, u32[]{:S(2)}) %copy-start.2) | copy-done | bytes 1048600
  70.2 2.0 %shard_map.115 = bf16[16,16,512]{2,1,0:T(8,128)(2,1)} custom-call(bf16[8,16,512]{2,1,0:T(8,128)(2,1)S(1)} %all-to-all-done.1.summ_ref, bf16[3,512,512]{2,1,0:T(8,128)(2,1)S(1)} %copy-done, bf16[3,512,512]{2,1,0:T(8,128)(2,1)S(1)} %copy-done.1, f32[1,512]{1,0:T(1,128)S(1)} %bitcast.22, f32[512,512]{1,0:T(8,128)S(1)} %copy-done.2), custom_call_target="tpu_custom_call" | custom-call | flops 100000000 | bytes 1000000 | tf_op jit(solution)/shard_map/pallas_call | solution.py:271
  72.2 6.3 %all-to-all-start.2 = ((bf16[16,16,512]{2,1,0:T(8,128)(2,1)}), bf16[16,16,512]{2,1,0:T(8,128)(2,1)S(1)}, u32[]{:S(2)}, u32[]{:S(2)}) async-start(bf16[16,16,512]{2,1,0:T(8,128)(2,1)} %shard_map.115), calls=%async_computation.2 | async-start | bytes 524288 | tf_op jit(solution)/shard_map/all_to_all | solution.py:195
  78.5 18.2 %all-to-all-done.2 = bf16[16,16,512]{2,1,0:T(8,128)(2,1)S(1)} async-done(((bf16[16,16,512]{2,1,0:T(8,128)(2,1)}), bf16[16,16,512]{2,1,0:T(8,128)(2,1)S(1)}, u32[]{:S(2)}, u32[]{:S(2)}) %all-to-all-start.2) | async-done | bytes 262176 | tf_op jit(solution)/shard_map/all_to_all | solution.py:195
  96.8 1.0 collective-permute-start.1
  99.5 4.6 %shard_map.117 = (bf16[256,256]{1,0:T(8,128)(2,1)S(1)}, bf16[3072,256]{1,0:T(8,128)(2,1)S(1)}) custom-call(s32[1,24]{1,0:T(1,128)S(1)} %copy-done.11, s32[1,24]{1,0:T(1,128)S(1)} %copy-done.14, s32[1,24]{1,0:T(1,128)S(1)} %collective-permute-done.3.rows_oth, s32[1,1]{1,0:T(1,128)} %collective-permute-done.4.used_oth, ...), custom_call_target="tpu_custom_call" | custom-call | flops 100000000 | bytes 1000000 | tf_op jit(solution)/shard_map/pallas_call | solution.py:254
  104.9 1.2 %shard_map.118.agg_own = bf16[256,256]{1,0:T(8,128)(2,1)S(1)} custom-call(s32[1,24]{1,0:T(1,128)S(1)} %copy-done.12, s32[1,1]{1,0:T(1,128)S(6)} %copy.12.used, bf16[24,128,128]{2,1,0:T(8,128)(2,1)S(1)} %bitcast.12, bf16[256,256]{1,0:T(8,128)(2,1)S(1)} %get-tuple-element.14.feat, bf16[3072,256]{1,0:T(8,128)(2,1)S(1)} %get-tuple-element.18.rhs), custom_call_target="tpu_custom_call" | custom-call | flops 100000000 | bytes 1000000 | tf_op jit(solution)/shard_map/pallas_call | solution.py:267
  106.2 1.4 %shard_map.119 = (bf16[256,512]{1,0:T(8,128)(2,1)}, f32[512,512]{1,0:T(8,128)}) custom-call(bf16[256,512]{1,0:T(8,128)(2,1)S(1)} %bitcast.10, bf16[256,512]{1,0:T(8,128)(2,1)S(1)} %collective-permute-done.1.wt_oth, bf16[256,256]{1,0:T(8,128)(2,1)S(1)} %shard_map.118.agg_own, bf16[256,256]{1,0:T(8,128)(2,1)S(1)} %collective-permute-done.19.agg_oth), custom_call_target="tpu_custom_call" | custom-call | flops 100000000 | bytes 1000000 | tf_op jit(solution)/shard_map/pallas_call | solution.py:283
  (60 shorter events, 14.3 us)
Async XLA Ops:
  3.4 6.4 %collective-permute-start.6 = (bf16[256,256]{1,0:T(8,128)(2,1)S(1)}, bf16[256,256]{1,0:T(8,128)(2,1)S(1)}, u32[]{:S(2)}, u32[]{:S(2)}) collective-permute-start(bf16[256,256]{1,0:T(8,128)(2,1)S(1)} %get-tuple-element.15), channel_id=1, source_target_pairs={{0,8},{8,0},{1,9},{9,1},{2,10},{10,2},{3,11},{11,3},{4,12},{12,4},... | collective-permute-start | bytes 393224 | tf_op jit(solution)/shard_map/ppermute | solution.py:191
  6.7 6.5 %collective-permute-start.9 = (bf16[2,128,256]{2,1,0:T(8,128)(2,1)S(1)}, bf16[2,128,256]{2,1,0:T(8,128)(2,1)S(1)}, u32[]{:S(2)}, u32[]{:S(2)}) collective-permute-start(bf16[2,128,256]{2,1,0:T(8,128)(2,1)S(1)} %bitcast.13), channel_id=1, source_target_pairs={{0,128},{64,192},{128,0},{192,64},{1,129},{65,193},{129,1},{193,65... | collective-permute-start | bytes 393224 | tf_op jit(solution)/shard_map/ppermute | solution.py:200
  7.8 6.6 %collective-permute-start.8 = (bf16[2,128,256]{2,1,0:T(8,128)(2,1)S(1)}, bf16[2,128,256]{2,1,0:T(8,128)(2,1)S(1)}, u32[]{:S(2)}, u32[]{:S(2)}) collective-permute-start(bf16[2,128,256]{2,1,0:T(8,128)(2,1)S(1)} %bitcast.14), channel_id=1, source_target_pairs={{0,192},{64,0},{128,64},{192,128},{1,193},{65,1},{129,65},{193,129... | collective-permute-start | bytes 393224 | tf_op jit(solution)/shard_map/ppermute | solution.py:200
  8.6 17.9 %collective-permute-start = (bf16[256,512]{1,0:T(8,128)(2,1)S(1)}, bf16[256,512]{1,0:T(8,128)(2,1)S(1)}, u32[]{:S(2)}, u32[]{:S(2)}) collective-permute-start(bf16[256,512]{1,0:T(8,128)(2,1)S(1)} %get-tuple-element.13), channel_id=1, source_target_pairs={{0,8},{8,0},{1,9},{9,1},{2,10},{10,2},{3,11},{11,3},{4,12},{12,4},... | collective-permute-start | bytes 786440 | tf_op jit(solution)/shard_map/ppermute | solution.py:191
  9.3 7.0 %collective-permute-start.7 = (bf16[2,128,256]{2,1,0:T(8,128)(2,1)S(1)}, bf16[2,128,256]{2,1,0:T(8,128)(2,1)S(1)}, u32[]{:S(2)}, u32[]{:S(2)}) collective-permute-start(bf16[2,128,256]{2,1,0:T(8,128)(2,1)S(1)} %bitcast.15), channel_id=1, source_target_pairs={{0,64},{64,128},{128,192},{192,0},{1,65},{65,129},{129,193},{193,1... | collective-permute-start | bytes 393224 | tf_op jit(solution)/shard_map/ppermute | solution.py:200
  9.9 59.1 %copy-start = (bf16[3,512,512]{2,1,0:T(8,128)(2,1)S(1)}, bf16[3,512,512]{2,1,0:T(8,128)(2,1)}, u32[]{:S(2)}) copy-start(bf16[3,512,512]{2,1,0:T(8,128)(2,1)} %w_in_ref.1) | copy-start | bytes 4718596
  9.9 6.4 %collective-permute-start.12 = (bf16[2,128,256]{2,1,0:T(8,128)(2,1)S(1)}, bf16[2,128,256]{2,1,0:T(8,128)(2,1)S(1)}, u32[]{:S(2)}, u32[]{:S(2)}) collective-permute-start(bf16[2,128,256]{2,1,0:T(8,128)(2,1)S(1)} %bitcast.17), channel_id=1, source_target_pairs={{0,32},{16,48},{32,0},{48,16},{1,33},{17,49},{33,1},{49,17},{2,34}... | collective-permute-start | bytes 393224 | tf_op jit(solution)/shard_map/ppermute | solution.py:200
  13.2 6.3 %collective-permute-start.11 = (bf16[2,128,256]{2,1,0:T(8,128)(2,1)S(1)}, bf16[2,128,256]{2,1,0:T(8,128)(2,1)S(1)}, u32[]{:S(2)}, u32[]{:S(2)}) collective-permute-start(bf16[2,128,256]{2,1,0:T(8,128)(2,1)S(1)} %bitcast.18), channel_id=1, source_target_pairs={{0,48},{16,0},{32,16},{48,32},{1,49},{17,1},{33,17},{49,33},{2,50}... | collective-permute-start | bytes 393224 | tf_op jit(solution)/shard_map/ppermute | solution.py:200
  14.4 5.1 %collective-permute-start.10 = (bf16[2,128,256]{2,1,0:T(8,128)(2,1)S(1)}, bf16[2,128,256]{2,1,0:T(8,128)(2,1)S(1)}, u32[]{:S(2)}, u32[]{:S(2)}) collective-permute-start(bf16[2,128,256]{2,1,0:T(8,128)(2,1)S(1)} %bitcast.19), channel_id=1, source_target_pairs={{0,16},{16,32},{32,48},{48,0},{1,17},{17,33},{33,49},{49,1},{2,18}... | collective-permute-start | bytes 393224 | tf_op jit(solution)/shard_map/ppermute | solution.py:200
  22.5 43.7 %collective-permute-start.15 = (bf16[8,128,256]{2,1,0:T(8,128)(2,1)}, bf16[8,128,256]{2,1,0:T(8,128)(2,1)}, u32[]{:S(2)}, u32[]{:S(2)}) collective-permute-start(bf16[8,128,256]{2,1,0:T(8,128)(2,1)} %get-tuple-element.16.refs_0_), channel_id=1, source_target_pairs={{0,32},{16,48},{32,0},{48,16},{1,33},{17,49},{33,1},{49,17},{2,34}... | collective-permute-start | bytes 1572872 | tf_op jit(solution)/shard_map/ppermute | solution.py:200
  24.5 44.5 %collective-permute-start.14 = (bf16[8,128,256]{2,1,0:T(8,128)(2,1)}, bf16[8,128,256]{2,1,0:T(8,128)(2,1)}, u32[]{:S(2)}, u32[]{:S(2)}) collective-permute-start(bf16[8,128,256]{2,1,0:T(8,128)(2,1)} %get-tuple-element.16.refs_0_), channel_id=1, source_target_pairs={{0,48},{16,0},{32,16},{48,32},{1,49},{17,1},{33,17},{49,33},{2,50}... | collective-permute-start | bytes 1572872 | tf_op jit(solution)/shard_map/ppermute | solution.py:200
  27.3 24.0 %all-to-all-start = ((bf16[16,16,512]{2,1,0:T(8,128)(2,1)}), bf16[16,16,512]{2,1,0:T(8,128)(2,1)S(1)}, u32[]{:S(2)}, u32[]{:S(2)}) async-start(bf16[16,16,512]{2,1,0:T(8,128)(2,1)} %bitcast.23), calls=%async_computation | async-start | bytes 524288 | tf_op jit(solution)/shard_map/all_to_all | solution.py:195
  31.8 66.0 %collective-permute-start.5 = (bf16[24,128,128]{2,1,0:T(8,128)(2,1)}, bf16[24,128,128]{2,1,0:T(8,128)(2,1)}, u32[]{:S(2)}, u32[]{:S(2)}) collective-permute-start(bf16[24,128,128]{2,1,0:T(8,128)(2,1)} %bitcast.11), channel_id=1, source_target_pairs={{0,8},{8,0},{1,9},{9,1},{2,10},{10,2},{3,11},{11,3},{4,12},{12,4},... | collective-permute-start | bytes 2359304 | tf_op jit(solution)/shard_map/ppermute | solution.py:191
  34.1 44.4 %collective-permute-start.13 = (bf16[8,128,256]{2,1,0:T(8,128)(2,1)}, bf16[8,128,256]{2,1,0:T(8,128)(2,1)}, u32[]{:S(2)}, u32[]{:S(2)}) collective-permute-start(bf16[8,128,256]{2,1,0:T(8,128)(2,1)} %get-tuple-element.16.refs_0_), channel_id=1, source_target_pairs={{0,16},{16,32},{32,48},{48,0},{1,17},{17,33},{33,49},{49,1},{2,18}... | collective-permute-start | bytes 1572872 | tf_op jit(solution)/shard_map/ppermute | solution.py:200
  51.9 17.0 %all-to-all-start.1 = ((bf16[8,16,512]{2,1,0:T(8,128)(2,1)}), bf16[8,16,512]{2,1,0:T(8,128)(2,1)S(1)}, u32[]{:S(2)}, u32[]{:S(2)}) async-start(bf16[8,16,512]{2,1,0:T(8,128)(2,1)} %shard_map.114), calls=%async_computation.1 | async-start | bytes 262144 | tf_op jit(solution)/shard_map/all_to_all | solution.py:195
  60.1 3.0 %collective-permute-start.4 = (s32[1,1]{1,0:T(1,128)}, s32[1,1]{1,0:T(1,128)}, u32[]{:S(2)}, u32[]{:S(2)}) collective-permute-start(s32[1,1]{1,0:T(1,128)} %param.14), channel_id=1, source_target_pairs={{0,8},{8,0},{1,9},{9,1},{2,10},{10,2},{3,11},{11,3},{4,12},{12,4},... | collective-permute-start | bytes 20 | tf_op jit(solution)/shard_map/ppermute | solution.py:191
  63.1 1.2 %collective-permute-start.3 = (s32[1,24]{1,0:T(1,128)S(1)}, s32[1,24]{1,0:T(1,128)S(1)}, u32[]{:S(2)}, u32[]{:S(2)}) collective-permute-start(s32[1,24]{1,0:T(1,128)S(1)} %copy-done.12), channel_id=1, source_target_pairs={{0,8},{8,0},{1,9},{9,1},{2,10},{10,2},{3,11},{11,3},{4,12},{12,4},... | collective-permute-start | bytes 296 | tf_op jit(solution)/shard_map/ppermute | solution.py:191
  64.2 1.2 %collective-permute-start.2 = (s32[1,24]{1,0:T(1,128)S(1)}, s32[1,24]{1,0:T(1,128)S(1)}, u32[]{:S(2)}, u32[]{:S(2)}) collective-permute-start(s32[1,24]{1,0:T(1,128)S(1)} %copy-done.11), channel_id=1, source_target_pairs={{0,8},{8,0},{1,9},{9,1},{2,10},{10,2},{3,11},{11,3},{4,12},{12,4},... | collective-permute-start | bytes 296 | tf_op jit(solution)/shard_map/ppermute | solution.py:191
  65.4 32.4 %collective-permute-start.18 = (bf16[8,128,256]{2,1,0:T(8,128)(2,1)}, bf16[8,128,256]{2,1,0:T(8,128)(2,1)}, u32[]{:S(2)}, u32[]{:S(2)}) collective-permute-start(bf16[8,128,256]{2,1,0:T(8,128)(2,1)} %copy-done.4), channel_id=1, source_target_pairs={{0,128},{64,192},{128,0},{192,64},{1,129},{65,193},{129,1},{193,65... | collective-permute-start | bytes 1572872 | tf_op jit(solution)/shard_map/ppermute | solution.py:200
  66.2 31.6 %collective-permute-start.17 = (bf16[8,128,256]{2,1,0:T(8,128)(2,1)}, bf16[8,128,256]{2,1,0:T(8,128)(2,1)}, u32[]{:S(2)}, u32[]{:S(2)}) collective-permute-start(bf16[8,128,256]{2,1,0:T(8,128)(2,1)} %copy-done.4), channel_id=1, source_target_pairs={{0,192},{64,0},{128,64},{192,128},{1,193},{65,1},{129,65},{193,129... | collective-permute-start | bytes 1572872 | tf_op jit(solution)/shard_map/ppermute | solution.py:200
  68.9 28.9 %collective-permute-start.16 = (bf16[8,128,256]{2,1,0:T(8,128)(2,1)}, bf16[8,128,256]{2,1,0:T(8,128)(2,1)}, u32[]{:S(2)}, u32[]{:S(2)}) collective-permute-start(bf16[8,128,256]{2,1,0:T(8,128)(2,1)} %copy-done.4), channel_id=1, source_target_pairs={{0,64},{64,128},{128,192},{192,0},{1,65},{65,129},{129,193},{193,1... | collective-permute-start | bytes 1572872 | tf_op jit(solution)/shard_map/ppermute | solution.py:200
  72.2 24.6 %all-to-all-start.2 = ((bf16[16,16,512]{2,1,0:T(8,128)(2,1)}), bf16[16,16,512]{2,1,0:T(8,128)(2,1)S(1)}, u32[]{:S(2)}, u32[]{:S(2)}) async-start(bf16[16,16,512]{2,1,0:T(8,128)(2,1)} %shard_map.115), calls=%async_computation.2 | async-start | bytes 524288 | tf_op jit(solution)/shard_map/all_to_all | solution.py:195
  96.8 9.4 %collective-permute-start.1 = (bf16[256,512]{1,0:T(8,128)(2,1)S(1)}, bf16[256,512]{1,0:T(8,128)(2,1)S(1)}, u32[]{:S(2)}, u32[]{:S(2)}) collective-permute-start(bf16[256,512]{1,0:T(8,128)(2,1)S(1)} %bitcast.9), channel_id=1, source_target_pairs={{0,8},{8,0},{1,9},{9,1},{2,10},{10,2},{3,11},{11,3},{4,12},{12,4},... | collective-permute-start | bytes 786440 | tf_op jit(solution)/shard_map/ppermute | solution.py:191
  104.1 2.1 %collective-permute-start.19 = (bf16[256,256]{1,0:T(8,128)(2,1)S(1)}, bf16[256,256]{1,0:T(8,128)(2,1)S(1)}, u32[]{:S(2)}, u32[]{:S(2)}) collective-permute-start(bf16[256,256]{1,0:T(8,128)(2,1)S(1)} %get-tuple-element.19), channel_id=1, source_target_pairs={{0,8},{8,0},{1,9},{9,1},{2,10},{10,2},{3,11},{11,3},{4,12},{12,4},... | collective-permute-start | bytes 393224 | tf_op jit(solution)/shard_map/ppermute | solution.py:191
  (14 other events, 282.4 us)

commit v4 on v3

v4 whole, which is shorter than its diff:
```python
import functools

import jax
import jax.numpy as jnp
from jax import lax
from jax.experimental import pallas as pl
from jax.experimental.pallas import tpu as pltpu
from jax.sharding import Mesh, PartitionSpec as P


BLOCK = 128
X, Y, C = 4, 4, 2
PAIR = 2
CHIPS = X * Y
F32 = jnp.float32
BF16 = jnp.bfloat16
VM = pltpu.MemorySpace.VMEM
SM = pltpu.MemorySpace.SMEM
HB = pltpu.MemorySpace.HBM
NN = (((1,), (0,)), ((), ()))
NT = (((1,), (1,)), ((), ()))
TN = (((0,), (0,)), ((), ()))


def mm(a, b, dims):
    return lax.dot_general(a, b, dims, preferred_element_type=F32)


def vspec():
    return pl.BlockSpec(memory_space=VM)


def hspec():
    return pl.BlockSpec(memory_space=HB)


def sspec():
    return pl.BlockSpec(memory_space=SM)


def call(kernel, out_shape, in_specs, scratch=(), flops=10**8, bytes_accessed=10**6, vmem_mib=8, out=None):
    many = isinstance(out_shape, (tuple, list))
    return pl.pallas_call(
        kernel,
        out_shape=out_shape,
        in_specs=in_specs,
        out_specs=out or (tuple(vspec() for _ in out_shape) if many else vspec()),
        scratch_shapes=list(scratch),
        cost_estimate=pl.CostEstimate(flops=flops, bytes_accessed=bytes_accessed, transcendentals=0),
        compiler_params=pltpu.CompilerParams(vmem_limit_bytes=vmem_mib * 2**20),
    )


def place():
    return tuple(lax.axis_index(axis).astype(jnp.int32) for axis in ("x", "y", "c", "z"))


def pool_kernel(
    feat_hbm, pool_hbm, send_ref, keep_ref, mine_hbm, give_ref, feat_ref, pool_ref, mine_ref, sems
):
    fetch = [pltpu.make_async_copy(feat_hbm, feat_ref, sems.at[0]), pltpu.make_async_copy(pool_hbm, pool_ref, sems.at[1])]
    for cp in fetch:
        cp.start()
    for cp in fetch:
        cp.wait()
    half = send_ref.shape[0]
    core = place()[2]
    own = pl.multiple_of(core * half, half)
    other = pl.multiple_of((1 - core) * half, half)
    feat = feat_ref[...]
    gates = jax.nn.sigmoid(mm(feat, pool_ref[:, pl.ds(other, half)], NN)).astype(BF16)
    send_ref[...] = mm(gates, feat, TN).astype(BF16)
    gates = jax.nn.sigmoid(mm(feat, pool_ref[:, pl.ds(own, half)], NN)).astype(BF16)
    mine_ref[...] = feat_ref[:, pl.ds(own, half)]
    give_ref[...] = feat_ref[:, pl.ds(other, half)]
    store = pltpu.make_async_copy(mine_ref, mine_hbm, sems.at[2])
    store.start()
    keep_ref[...] = mm(gates, feat, TN)
    store.wait()


def column0(width):
    x, y, core, z = place()
    return core * (width // C) + ((x * Y + y) * lax.axis_size("z") + z) * PAIR


def pack_kernel(keep_ref, recv_ref, out_hbm, out_ref, sem, rows_ref, tiles_ref):
    n = rows_ref.shape[1] // PAIR
    for b in range(rows_ref.shape[0]):
        at = slice(b * BLOCK, (b + 1) * BLOCK)
        rows_ref[b] = keep_ref[:, at] + recv_ref[:, at].astype(F32)
        for i in range(PAIR):
            tiles_ref[pl.ds(PAIR * b + i, n, stride=8), :] = rows_ref[b, pl.ds(i, n, stride=PAIR), :]
    out_ref[...] = tiles_ref[...].astype(BF16)
    store = pltpu.make_async_copy(out_ref, out_hbm, sem)
    store.start()
    store.wait()


def unpack(packed_ref, tiles_ref, rows_ref):
    tiles_ref[...] = packed_ref[...].astype(F32)
    n = rows_ref.shape[1] // PAIR
    for b in range(rows_ref.shape[0]):
        for i in range(PAIR):
            rows_ref[b, pl.ds(i, n, stride=PAIR), :] = tiles_ref[pl.ds(PAIR * b + i, n, stride=8), :]


def join_kernel(*refs):
    pieces, (start_hbm, low, high, startt_hbm, start_ref, turned_ref, startt, sems) = refs[:-8], refs[-8:]
    half = len(pieces) // 2
    copies = []
    for n, piece in enumerate(pieces):
        out = low if n < half else high
        size = piece.shape[0]
        cp = pltpu.make_async_copy(piece, out.at[pl.ds((n % half) * size, size)], sems.at[n])
        cp.start()
        copies.append(cp)
    col0 = column0(start_hbm.shape[1])
    window = pl.multiple_of((col0 // BLOCK) * BLOCK, BLOCK)
    cp = pltpu.make_async_copy(start_hbm.at[:, pl.ds(window, BLOCK)], start_ref, sems.at[len(pieces)])
    cp.start()
    cp.wait()
    turned_ref[...] = start_ref[...].T
    row0 = lax.rem(col0, BLOCK)
    skip = lax.rem(row0, 8)
    rows = turned_ref[pl.ds(pl.multiple_of(row0 - skip, 8), 8), :]
    startt[...] = pltpu.roll(rows, lax.rem(8 - skip, 8), 0)
    store = pltpu.make_async_copy(startt, startt_hbm, sems.at[len(pieces) + 1])
    store.start()
    store.wait()
    for cp in copies:
        cp.wait()


def in_hbm(x):
    return pltpu.with_memory_space_constraint(x, HB)


def join(a, b, start_weight):
    shape = jax.ShapeDtypeStruct((len(a) * a[0].shape[0],) + a[0].shape[1:], a[0].dtype)
    pieces = a + b
    rows = start_weight.shape[0]
    return call(
        join_kernel,
        (shape, shape, pltpu.HBM((8, rows), F32)),
        [pl.BlockSpec(memory_space=pl.ANY)] * len(pieces) + [hspec()],
        out=(vspec(), vspec(), hspec()),
        scratch=[
            pltpu.VMEM((rows, BLOCK), F32),
            pltpu.VMEM((BLOCK, rows), F32),
            pltpu.VMEM((8, rows), F32),
            pltpu.SemaphoreType.DMA((len(pieces) + 2,)),
        ],
        flops=0,
    )(*pieces, in_hbm(start_weight))


def chain_kernel(
    scale, parts_ref, w_in_ref, w_ref, offset_ref, start_hbm, out_hbm, side_ref, hist_ref, start_ref, out_ref, sems
):
    fetch = pltpu.make_async_copy(start_hbm, start_ref, sems.at[0])
    fetch.start()
    _, n_t, sub, lanes = parts_ref.shape
    width = w_ref.shape[2]
    lane_blocks = width // lanes
    total = (jnp.sum(parts_ref[...].astype(F32), axis=0) * scale).reshape(n_t * sub, lanes)
    pieces = [total] + [pltpu.roll(total, n_t * sub - PAIR * b, 0) for b in range(1, lane_blocks)]
    summ = jnp.concatenate(pieces, axis=1).astype(BF16)
    for g in range(3):
        side = mm(summ, w_in_ref[g], NT)
        if g == 0:
            side = side - offset_ref[...]
        side_ref[g] = side.reshape(n_t, sub, width)
    fetch.wait()
    state = start_ref[...]
    row_pair = lax.broadcasted_iota(jnp.int32, (sub, lanes), 0) // PAIR

    def step(t, state):
        state_b = state.astype(BF16)
        update = jax.nn.sigmoid(side_ref[0, t] + mm(state_b, w_ref[0], NT))
        reset = jax.nn.sigmoid(side_ref[1, t] + mm(state_b, w_ref[1], NT))
        cand = jnp.tanh(side_ref[2, t] + mm((reset * state).astype(BF16), w_ref[2], NT))
        state = (1.0 - update) * state + update * cand
        tile = state[:, :lanes]
        for b in range(1, lane_blocks):
            tile = jnp.where(row_pair == b, pltpu.roll(state[:, b * lanes : (b + 1) * lanes], PAIR * b, 0), tile)
        hist_ref[t] = tile
        return state

    lax.fori_loop(0, n_t, step, state)
    out_ref[...] = jnp.broadcast_to(hist_ref[...].astype(BF16)[None], out_ref.shape)
    store = pltpu.make_async_copy(out_ref, out_hbm, sems.at[1])
    store.start()
    store.wait()


def masked(rows, used, tiles, lhs):
    for j in range(tiles.shape[0]):
        tile = tiles[j]
        at = jnp.where(j < used[0, 0], rows[0, j] & 1, 2)
        for r in range(2):
            lhs[r * BLOCK : (r + 1) * BLOCK, j * BLOCK : (j + 1) * BLOCK] = jnp.where(
                at == r, tile, jnp.zeros_like(tile)
            )


def slot_of(step):
    return jnp.where(step == 0, 0, jnp.where(step == 3, 1, step + 1))


def mask_kernel(rows_oth, used_oth, tiles_oth, rows_own, used_own, tiles_hbm, lhs_oth, lhs_own, tiles_own, sem):
    fetch = pltpu.make_async_copy(tiles_hbm, tiles_own, sem)
    fetch.start()
    masked(rows_oth, used_oth, tiles_oth, lhs_oth)
    fetch.wait()
    masked(rows_own, used_own, tiles_own, lhs_own)


def agg_oth_kernel(cols_own, cols_oth, lhs, feat, *refs):
    pieces, (agg, rhs_own, blocks, rhs, sems) = refs[:-5], refs[-5:]
    copies = []
    first = 0
    for n, piece in enumerate(pieces):
        cp = pltpu.make_async_copy(piece, blocks.at[pl.ds(first, piece.shape[0])], sems.at[n])
        cp.start()
        copies.append(cp)
        first += piece.shape[0]
    for cp in copies:
        cp.wait()
    x, y, core, _ = place()
    for cols, out in ((cols_oth, rhs), (cols_own, rhs_own)):
        for j in range(cols.shape[1]):
            col = cols[0, j]
            owner = col >> 1
            in_x = slot_of(((owner >> 3) - x) & 3)
            in_y = slot_of(((owner >> 1) - y) & 3)
            slot = jnp.where((owner & 1) == core, in_y * 4 + in_x, in_x * 4 + in_y + CHIPS)
            out[j * BLOCK : (j + 1) * BLOCK, :] = blocks[slot * 2 + (col & 1)]
    agg[...] = (feat[...].astype(F32) + mm(lhs[...], rhs[...], NN)).astype(BF16)


def agg_own_kernel(lhs, feat, rhs, agg):
    agg[...] = (feat[...].astype(F32) + mm(lhs[...], rhs[...], NN)).astype(BF16)


def final_kernel(wt_own, wt_oth, agg_own, agg_oth, hid_ref, w_ref, tiles, wt_f32, wt, agg):
    half = wt_f32.shape[1]
    core = place()[2]
    own = pl.multiple_of(core * half, half)
    oth = pl.multiple_of((1 - core) * half, half)
    for packed, at in ((wt_own, own), (wt_oth, oth)):
        unpack(packed, tiles, wt_f32)
        for b in range(wt_f32.shape[0]):
            lanes = slice(b * BLOCK, (b + 1) * BLOCK)
            wt[pl.ds(at, half), lanes] = wt_f32[b].astype(BF16)
            w_ref[lanes, pl.ds(at, half)] = wt_f32[b].T
    agg[:, pl.ds(own, half)] = agg_own[...]
    agg[:, pl.ds(oth, half)] = agg_oth[...]
    width = wt.shape[0]
    mixed = mm(agg[...], wt[...], NT)
    hid_ref[...] = jnp.maximum(mixed * width ** (-0.5), 0.0).astype(BF16)


def swap(x):
    return lax.ppermute(x, "c", [(0, 1), (1, 0)])


def trade(x, axes):
    return lax.all_to_all(x, axes, split_axis=0, concat_axis=0, tiled=True)


def shift(x, axis, distance):
    size = lax.axis_size(axis)
    return lax.ppermute(x, axis, [(i, (i + distance) % size) for i in range(size)])


def spread(x, axis):
    return [x] + [shift(x, axis, step) for step in (1, -1, 2)]


def layer(
    features,
    tile_rows,
    tile_cols,
    tile_vals,
    tile_used,
    pool_weight,
    w_in,
    w_state,
    gate_offset,
    start_weight,
):
    rows_dev, width = features.shape[1:]
    slots = tile_rows.shape[1]
    half = width // 2
    n_tm = lax.axis_size("z")
    feat = features[0]
    blocks_dev = rows_dev // BLOCK

    bf_half = jax.ShapeDtypeStruct((half, width), BF16)
    feat_half = jax.ShapeDtypeStruct((rows_dev, half), BF16)
    send, keep, feat_mine, feat_give = call(
        pool_kernel,
        (bf_half, jax.ShapeDtypeStruct((half, width), F32), pltpu.HBM(feat_half.shape, BF16), feat_half),
        [hspec(), hspec()],
        out=(vspec(), vspec(), hspec(), vspec()),
        scratch=[
            pltpu.VMEM(feat.shape, BF16),
            pltpu.VMEM(pool_weight.shape, BF16),
            pltpu.VMEM(feat_half.shape, BF16),
            pltpu.SemaphoreType.DMA((3,)),
        ],
    )(in_hbm(feat), in_hbm(pool_weight))
    packed = jax.ShapeDtypeStruct((half // PAIR * 8, BLOCK), BF16)
    partial = call(
        pack_kernel,
        pltpu.HBM(packed.shape, BF16),
        [vspec(), vspec()],
        out=hspec(),
        scratch=[pltpu.VMEM(packed.shape, BF16), pltpu.SemaphoreType.DMA(()), pltpu.VMEM((width // BLOCK, half, BLOCK), F32), pltpu.VMEM(packed.shape, F32)],
    )(keep, swap(send))
    everyone = ("x", "y", "z")
    parts = trade(partial.reshape(CHIPS * n_tm, 8, BLOCK), everyone)

    feat_oth = swap(feat_give)
    four = (blocks_dev, BLOCK, half)
    blocks_a = spread(feat_mine.reshape(four), "x")
    blocks_b = spread(feat_oth.reshape(four), "y")
    joined_a, joined_b, startt = join(blocks_a, blocks_b, start_weight)
    gathered = spread(joined_a, "y") + spread(joined_b, "x")

    rows_oth, cols_oth, used_oth = swap(tile_rows), swap(tile_cols), swap(tile_used)
    tiles_own = tile_vals[0]
    tiles_oth = swap(tiles_own)
    depth = slots * BLOCK
    lhs = jax.ShapeDtypeStruct((rows_dev, depth), BF16)
    lhs_oth, lhs_own = call(
        mask_kernel,
        (lhs, lhs),
        [sspec(), sspec(), vspec(), sspec(), sspec(), hspec()],
        scratch=[pltpu.VMEM(tiles_own.shape, BF16), pltpu.SemaphoreType.DMA(())],
    )(rows_oth, used_oth, tiles_oth, tile_rows, tile_used, in_hbm(tiles_own))
    agg_give, rhs_own = call(
        agg_oth_kernel,
        (feat_half, jax.ShapeDtypeStruct((depth, half), BF16)),
        [sspec()] * 2 + [vspec()] * 2 + [pl.BlockSpec(memory_space=pl.ANY)] * len(gathered),
        scratch=[
            pltpu.VMEM((CHIPS * C * blocks_dev, BLOCK, half), BF16),
            pltpu.VMEM((depth, half), BF16),
            pltpu.SemaphoreType.DMA((len(gathered),)),
        ],
        vmem_mib=16,
    )(tile_cols, cols_oth, lhs_oth, feat_oth, *gathered)
    agg_oth = swap(agg_give)
    agg_own = call(agg_own_kernel, feat_half, [vspec()] * 3)(lhs_own, feat_mine, rhs_own)

    scale = (rows_dev * CHIPS * C) ** (-0.5)
    evolved = call(
        functools.partial(chain_kernel, scale),
        pltpu.HBM((CHIPS, n_tm, 8, BLOCK), BF16),
        [vspec()] * 4 + [hspec()],
        out=hspec(),
        scratch=[
            pltpu.VMEM((3, n_tm, 8, width), F32),
            pltpu.VMEM((n_tm, 8, BLOCK), F32),
            pltpu.VMEM((8, width), F32),
            pltpu.VMEM((CHIPS, n_tm, 8, BLOCK), BF16),
            pltpu.SemaphoreType.DMA((2,)),
        ],
    )(parts.reshape(CHIPS, n_tm, 8, BLOCK), w_in, w_state, gate_offset[None, :], startt)
    wt_own = trade(evolved.reshape(CHIPS * n_tm, 8, BLOCK), everyone).reshape(packed.shape)
    wt_oth = swap(wt_own)
    hidden, weights = call(
        final_kernel,
        (jax.ShapeDtypeStruct((rows_dev, width), BF16), jax.ShapeDtypeStruct((width, width), F32)),
        [vspec()] * 4,
        scratch=[
            pltpu.VMEM(packed.shape, F32),
            pltpu.VMEM((width // BLOCK, half, BLOCK), F32),
            pltpu.VMEM((width, width), BF16),
            pltpu.VMEM((rows_dev, width), BF16),
        ],
    )(wt_own, wt_oth, agg_own, agg_oth)
    return hidden[None], weights[None]


def solution(mesh):
    n_tm = mesh.shape["tm"]
    fine = Mesh(mesh.devices.reshape(X, Y, C, n_tm), ("x", "y", "c", "z"))
    dom = ("x", "y", "c")
    in_specs = (
        P("z", dom, None),
        P("z", dom),
        P("z", dom),
        P("z", dom, None, None),
        P("z", dom),
        P(),
        P(),
        P(),
        P(),
        P(),
    )
    out_specs = (P("z", dom, None), P("z", None, None))
    return jax.shard_map(layer, mesh=fine, in_specs=in_specs, out_specs=out_specs, check_vma=False)
```

time: 108 us -> 100 us (0.926)
  waiting for transfers between devices: 40.7 us -> 22.2 us
  Pallas kernels: 13 us -> 21.2 us
  starting transfers between devices: 46 us -> 50.9 us
  local copies, waits for them, and re-layouts: 5.69 us -> 3.99 us
    all_to_all x3 -> x2, waiting for transfers between devices: 33.8 us -> 6.4 us  [trade(): return lax.all_to_all(x, axes, split_axis=0, concat_axis=0, tiled=True)]
    ppermute x12, waiting for transfers between devices: 4.21 us -> 14.1 us  [shift(): lax.ppermute(x, axis, [(i, (i + distance) % size) for i in range(size)])]
    pallas_call x5 -> x6, Pallas kernels: 6.9 us -> 16.6 us  [the longest x1 6.08 us: layer(): call(functools.partial(chain_kernel, scale), pltpu.HBM((CHIPS, n_tm, 8, B...]
    all_to_all x3 -> x2, starting transfers between devices: 19.1 us -> 25.7 us  [trade(): return lax.all_to_all(x, axes, split_axis=0, concat_axis=0, tiled=True)]
    ppermute x12, starting transfers between devices: 16.9 us -> 14.7 us  [shift(): lax.ppermute(x, axis, [(i, (i + distance) % size) for i in range(size)])]
    pallas_call x1, Pallas kernels: 4.61 us -> 2.74 us  [layer(): call(agg_oth_kernel, (feat_half, jax.ShapeDtypeStruct((depth, half), BF16...]
    unnamed x30 -> x24, local copies, waits for them, and re-layouts: 5.69 us -> 3.99 us
    ppermute x8, waiting for transfers between devices: 2.74 us -> 1.63 us  [swap(): return lax.ppermute(x, 'c', [(0, 1), (1, 0)])]
  transfers between devices with their start and end apart: 23 -> 22, of which waited for: 9 -> 7; matrix products, arithmetic and copies ran while one was open for 1% -> 0% of each run, Pallas kernels for 10% -> 17%
where the time goes in v4:
time: 100 us; the launch traced here: 99.7 us
  starting transfers between devices  50.9 us (51%)
  waiting for transfers between devices  22.2 us (22%)
  Pallas kernels  21.2 us (21%)
  local copies, waits for them, and re-layouts  3.99 us (4%)
  between operations  1.48 us (1%)
    all_to_all x2, starting transfers between devices, trade(): return lax.all_to_all(x, axes, split_axis=0, concat_axis=0, tiled=True)  25.7 us
    ppermute x12, starting transfers between devices, shift(): lax.ppermute(x, axis, [(i, (i + distance) % size) for i in range(size)])  14.7 us
    ppermute x12, waiting for transfers between devices, shift(): lax.ppermute(x, axis, [(i, (i + distance) % size) for i in range(size)])  14.1 us
    ppermute x8, starting transfers between devices, swap(): return lax.ppermute(x, 'c', [(0, 1), (1, 0)])  10.4 us
    all_to_all x2, waiting for transfers between devices, trade(): return lax.all_to_all(x, axes, split_axis=0, concat_axis=0, tiled=True)  6.4 us
    pallas_call x1, Pallas kernels, layer(): call(functools.partial(chain_kernel, scale), pltpu.HBM((CHIPS, n_tm, 8, B...  6.08 us
    unnamed x24, local copies, waits for them, and re-layouts  3.99 us
    pallas_call x1, Pallas kernels, layer(): call(mask_kernel, (lhs, lhs), [sspec(), sspec(), vspec(), sspec(), sspec(...  3.35 us
  transfers between devices with their start and end apart: 22, of which 7 were waited for; matrix products, arithmetic and copies ran while one was open for 0% of the time, Pallas kernels for 17%

profile of v4, /device:TPU:1, one launch (start us, length us, event | category | flops | bytes accessed | tf_op | source)
XLA Modules:
  0.0 99.7 jit_solution(15489542499698684149)
XLA Ops:
  0.6 2.5 %shard_map.113 = (bf16[256,512]{1,0:T(8,128)(2,1)S(1)}, f32[256,512]{1,0:T(8,128)S(1)}, bf16[256,256]{1,0:T(8,128)(2,1)}, bf16[256,256]{1,0:T(8,128)(2,1)S(1)}) custom-call(bf16[256,512]{1,0:T(8,128)(2,1)} %bitcast.27, bf16[512,512]{1,0:T(8,128)(2,1)} %pool_hbm.1), custom_call_target="tpu_custom_call" | custom-call | flops 100000000 | bytes 1000000 | tf_op jit(solution)/shard_map/pallas_call | solution.py:302
  3.1 3.3 %collective-permute-start = (bf16[256,512]{1,0:T(8,128)(2,1)S(1)}, bf16[256,512]{1,0:T(8,128)(2,1)S(1)}, u32[]{:S(2)}, u32[]{:S(2)}) collective-permute-start(bf16[256,512]{1,0:T(8,128)(2,1)S(1)} %get-tuple-element.16), channel_id=1, source_target_pairs={{0,8},{8,0},{1,9},{9,1},{2,10},{10,2},{3,11},{11,3},{4,12},{12,4},... | collective-permute-start | bytes 786440 | tf_op jit(solution)/shard_map/ppermute | solution.py:265
  6.5 2.7 %collective-permute-start.2 = (bf16[2,128,256]{2,1,0:T(8,128)(2,1)}, bf16[2,128,256]{2,1,0:T(8,128)(2,1)}, u32[]{:S(2)}, u32[]{:S(2)}) collective-permute-start(bf16[2,128,256]{2,1,0:T(8,128)(2,1)} %bitcast.19), channel_id=1, source_target_pairs={{0,192},{64,0},{128,64},{192,128},{1,193},{65,1},{129,65},{193,129... | collective-permute-start | bytes 393224 | tf_op jit(solution)/shard_map/ppermute | solution.py:274
  9.2 1.1 %collective-permute-start.5 = (bf16[2,128,256]{2,1,0:T(8,128)(2,1)S(1)}, bf16[2,128,256]{2,1,0:T(8,128)(2,1)}, u32[]{:S(2)}, u32[]{:S(2)}) collective-permute-start(bf16[2,128,256]{2,1,0:T(8,128)(2,1)S(1)} %bitcast.14), channel_id=1, source_target_pairs={{0,16},{16,32},{32,48},{48,0},{1,17},{17,33},{33,49},{49,1},{2,18}... | collective-permute-start | bytes 393224 | tf_op jit(solution)/shard_map/ppermute | solution.py:274
  10.3 2.3 %collective-permute-done.1.refs_1_ = bf16[2,128,256]{2,1,0:T(8,128)(2,1)S(1)} collective-permute-done((bf16[2,128,256]{2,1,0:T(8,128)(2,1)}, bf16[2,128,256]{2,1,0:T(8,128)(2,1)S(1)}, u32[]{:S(2)}, u32[]{:S(2)}) %collective-permute-start.1) | collective-permute-done | bytes 131104 | tf_op jit(solution)/shard_map/ppermute | solution.py:274
  13.2 1.0 %collective-permute-start.6 = (bf16[2,128,256]{2,1,0:T(8,128)(2,1)S(1)}, bf16[2,128,256]{2,1,0:T(8,128)(2,1)}, u32[]{:S(2)}, u32[]{:S(2)}) collective-permute-start(bf16[2,128,256]{2,1,0:T(8,128)(2,1)S(1)} %bitcast.15), channel_id=1, source_target_pairs={{0,48},{16,0},{32,16},{48,32},{1,49},{17,1},{33,17},{49,33},{2,50}... | collective-permute-start | bytes 393224 | tf_op jit(solution)/shard_map/ppermute | solution.py:274
  15.5 14.1 %all-to-all-start = ((bf16[128,8,128]{2,1,0:T(8,128)(2,1)}), bf16[128,8,128]{2,1,0:T(8,128)(2,1)S(1)}, u32[]{:S(2)}, u32[]{:S(2)}) async-start(bf16[128,8,128]{2,1,0:T(8,128)(2,1)} %bitcast.24), calls=%async_computation | async-start | bytes 524288 | tf_op jit(solution)/shard_map/all_to_all | solution.py:269
  31.5 3.3 %shard_map.115 = (bf16[8,128,256]{2,1,0:T(8,128)(2,1)}, bf16[8,128,256]{2,1,0:T(8,128)(2,1)S(1)}, f32[8,512]{1,0:T(8,128)}) custom-call(bf16[2,128,256]{2,1,0:T(8,128)(2,1)S(1)} %bitcast.21, bf16[2,128,256]{2,1,0:T(8,128)(2,1)S(1)} %copy-done.7, bf16[2,128,256]{2,1,0:T(8,128)(2,1)} %collective-permute-done.2.refs_2_, ...), custom_call_target="tpu_custom_call" | custom-call | bytes 1000000 | tf_op jit(solution)/shard_map/pallas_call | solution.py:143
  36.2 2.1 %collective-permute-start.14 = (bf16[8,128,256]{2,1,0:T(8,128)(2,1)}, bf16[8,128,256]{2,1,0:T(8,128)(2,1)}, u32[]{:S(2)}, u32[]{:S(2)}) collective-permute-start(bf16[8,128,256]{2,1,0:T(8,128)(2,1)} %get-tuple-element.22.refs_0_), channel_id=1, source_target_pairs={{0,48},{16,0},{32,16},{48,32},{1,49},{17,1},{33,17},{49,33},{2,50}... | collective-permute-start | bytes 1572872 | tf_op jit(solution)/shard_map/ppermute | solution.py:274
  38.3 3.2 %collective-permute-start.11 = (bf16[24,128,128]{2,1,0:T(8,128)(2,1)}, bf16[24,128,128]{2,1,0:T(8,128)(2,1)}, u32[]{:S(2)}, u32[]{:S(2)}) collective-permute-start(bf16[24,128,128]{2,1,0:T(8,128)(2,1)} %bitcast.25), channel_id=1, source_target_pairs={{0,8},{8,0},{1,9},{9,1},{2,10},{10,2},{3,11},{11,3},{4,12},{12,4},... | collective-permute-start | bytes 2359304 | tf_op jit(solution)/shard_map/ppermute | solution.py:265
  43.2 6.1 %shard_map.116 = bf16[16,8,8,128]{3,2,1,0:T(8,128)(2,1)} custom-call(bf16[16,8,8,128]{3,2,1,0:T(8,128)(2,1)S(1)} %bitcast.13, bf16[3,512,512]{2,1,0:T(8,128)(2,1)S(1)} %copy-done, bf16[3,512,512]{2,1,0:T(8,128)(2,1)S(1)} %copy-done.1, f32[1,512]{1,0:T(1,128)S(1)} %bitcast.22, f32[8,512]{1,0:T(8,128)S(1)} %copy-done.8), custom_call_target="tpu_custom_call" | custom-call | flops 100000000 | bytes 1000000 | tf_op jit(solution)/shard_map/pallas_call | solution.py:358
  49.2 11.6 %all-to-all-start.1 = ((bf16[128,8,128]{2,1,0:T(8,128)(2,1)}), bf16[128,8,128]{2,1,0:T(8,128)(2,1)S(1)}, u32[]{:S(2)}, u32[]{:S(2)}) async-start(bf16[128,8,128]{2,1,0:T(8,128)(2,1)} %bitcast.23), calls=%async_computation.1 | async-start | bytes 524288 | tf_op jit(solution)/shard_map/all_to_all | solution.py:269
  61.4 1.2 %collective-permute-done.10.used_oth = s32[1,1]{1,0:T(1,128)} collective-permute-done((s32[1,1]{1,0:T(1,128)}, s32[1,1]{1,0:T(1,128)}, u32[]{:S(2)}, u32[]{:S(2)}) %collective-permute-start.10) | collective-permute-done | bytes 36 | tf_op jit(solution)/shard_map/ppermute | solution.py:265
  62.9 2.3 %collective-permute-start.15 = (bf16[8,128,256]{2,1,0:T(8,128)(2,1)}, bf16[8,128,256]{2,1,0:T(8,128)(2,1)S(1)}, u32[]{:S(2)}, u32[]{:S(2)}) collective-permute-start(bf16[8,128,256]{2,1,0:T(8,128)(2,1)} %get-tuple-element.22.refs_0_), channel_id=1, source_target_pairs={{0,32},{16,48},{32,0},{48,16},{1,33},{17,49},{33,1},{49,17},{2,34}... | collective-permute-start | bytes 1572872 | tf_op jit(solution)/shard_map/ppermute | solution.py:274
  65.2 1.4 %collective-permute-start.16 = (bf16[8,128,256]{2,1,0:T(8,128)(2,1)}, bf16[8,128,256]{2,1,0:T(8,128)(2,1)S(1)}, u32[]{:S(2)}, u32[]{:S(2)}) collective-permute-start(bf16[8,128,256]{2,1,0:T(8,128)(2,1)} %copy-done.2), channel_id=1, source_target_pairs={{0,64},{64,128},{128,192},{192,0},{1,65},{65,129},{129,193},{193,1... | collective-permute-start | bytes 1572872 | tf_op jit(solution)/shard_map/ppermute | solution.py:274
  66.6 1.7 %collective-permute-start.17 = (bf16[8,128,256]{2,1,0:T(8,128)(2,1)}, bf16[8,128,256]{2,1,0:T(8,128)(2,1)S(1)}, u32[]{:S(2)}, u32[]{:S(2)}) collective-permute-start(bf16[8,128,256]{2,1,0:T(8,128)(2,1)} %copy-done.2), channel_id=1, source_target_pairs={{0,192},{64,0},{128,64},{192,128},{1,193},{65,1},{129,65},{193,129... | collective-permute-start | bytes 1572872 | tf_op jit(solution)/shard_map/ppermute | solution.py:274
  68.3 1.5 %collective-permute-start.18 = (bf16[8,128,256]{2,1,0:T(8,128)(2,1)}, bf16[8,128,256]{2,1,0:T(8,128)(2,1)S(1)}, u32[]{:S(2)}, u32[]{:S(2)}) collective-permute-start(bf16[8,128,256]{2,1,0:T(8,128)(2,1)} %copy-done.2), channel_id=1, source_target_pairs={{0,128},{64,192},{128,0},{192,64},{1,129},{65,193},{129,1},{193,65... | collective-permute-start | bytes 1572872 | tf_op jit(solution)/shard_map/ppermute | solution.py:274
  69.8 5.5 %all-to-all-done.1 = bf16[128,8,128]{2,1,0:T(8,128)(2,1)S(1)} async-done(((bf16[128,8,128]{2,1,0:T(8,128)(2,1)}), bf16[128,8,128]{2,1,0:T(8,128)(2,1)S(1)}, u32[]{:S(2)}, u32[]{:S(2)}) %all-to-all-start.1) | async-done | bytes 262176 | tf_op jit(solution)/shard_map/all_to_all | solution.py:269
  75.2 1.6 %collective-permute-start.8 = (bf16[1024,128]{1,0:T(8,128)(2,1)S(1)}, bf16[1024,128]{1,0:T(8,128)(2,1)S(1)}, u32[]{:S(2)}, u32[]{:S(2)}) collective-permute-start(bf16[1024,128]{1,0:T(8,128)(2,1)S(1)} %bitcast.11), channel_id=1, source_target_pairs={{0,8},{8,0},{1,9},{9,1},{2,10},{10,2},{3,11},{11,3},{4,12},{12,4},... | collective-permute-start | bytes 786440 | tf_op jit(solution)/shard_map/ppermute | solution.py:265
  77.5 3.4 %shard_map.117 = (bf16[256,3072]{1,0:T(8,128)(2,1)S(1)}, bf16[256,3072]{1,0:T(8,128)(2,1)S(1)}) custom-call(s32[1,24]{1,0:T(1,128)S(1)} %collective-permute-done.9.rows_oth, s32[1,1]{1,0:T(1,128)} %collective-permute-done.10.used_oth, bf16[24,128,128]{2,1,0:T(8,128)(2,1)} %collective-permute-done.11.tiles_oth, s32[1,24]{1,0:T(1,128)S(1)} %copy-done.10, ...), custom_call_target="tpu_custom_call" | custom-call | flops 100000000 | bytes 1000000 | tf_op jit(solution)/shard_map/pallas_call | solution.py:337
  81.1 11.7 %collective-permute-done.18.refs_7_ = bf16[8,128,256]{2,1,0:T(8,128)(2,1)S(1)} collective-permute-done((bf16[8,128,256]{2,1,0:T(8,128)(2,1)}, bf16[8,128,256]{2,1,0:T(8,128)(2,1)S(1)}, u32[]{:S(2)}, u32[]{:S(2)}) %collective-permute-start.18) | collective-permute-done | bytes 524320 | tf_op jit(solution)/shard_map/ppermute | solution.py:274
  92.8 2.7 %shard_map.118 = (bf16[256,256]{1,0:T(8,128)(2,1)S(1)}, bf16[3072,256]{1,0:T(8,128)(2,1)S(1)}) custom-call(s32[1,24]{1,0:T(1,128)S(1)} %copy-done.11, s32[1,24]{1,0:T(1,128)S(1)} %collective-permute-done.12.cols_oth, bf16[256,3072]{1,0:T(8,128)(2,1)S(1)} %get-tuple-element.21.lhs, bf16[256,256]{1,0:T(8,128)(2,1)S(1)} %collective-permute-done.4.feat, ...), custom_call_target="tpu_custom_call" | custom-call | flops 100000000 | bytes 1000000 | tf_op jit(solution)/shard_map/pallas_call | solution.py:343
  95.5 1.4 %collective-permute-start.19 = (bf16[256,256]{1,0:T(8,128)(2,1)S(1)}, bf16[256,256]{1,0:T(8,128)(2,1)S(1)}, u32[]{:S(2)}, u32[]{:S(2)}) collective-permute-start(bf16[256,256]{1,0:T(8,128)(2,1)S(1)} %get-tuple-element.25), channel_id=1, source_target_pairs={{0,8},{8,0},{1,9},{9,1},{2,10},{10,2},{3,11},{11,3},{4,12},{12,4},... | collective-permute-start | bytes 393224 | tf_op jit(solution)/shard_map/ppermute | solution.py:265
  97.9 1.8 %shard_map.120 = (bf16[256,512]{1,0:T(8,128)(2,1)}, f32[512,512]{1,0:T(8,128)}) custom-call(bf16[1024,128]{1,0:T(8,128)(2,1)S(1)} %bitcast.12, bf16[1024,128]{1,0:T(8,128)(2,1)S(1)} %collective-permute-done.8.wt_oth, bf16[256,256]{1,0:T(8,128)(2,1)S(1)} %shard_map.119.agg_own, bf16[256,256]{1,0:T(8,128)(2,1)S(1)} %collective-permute-done.19.agg_oth), custom_call_target="tpu_custom_call" | custom-call | flops 100000000 | bytes 1000000 | tf_op jit(solution)/shard_map/pallas_call | solution.py:373
  (52 shorter events, 8.8 us)
Async XLA Ops:
  3.1 11.1 %collective-permute-start = (bf16[256,512]{1,0:T(8,128)(2,1)S(1)}, bf16[256,512]{1,0:T(8,128)(2,1)S(1)}, u32[]{:S(2)}, u32[]{:S(2)}) collective-permute-start(bf16[256,512]{1,0:T(8,128)(2,1)S(1)} %get-tuple-element.16), channel_id=1, source_target_pairs={{0,8},{8,0},{1,9},{9,1},{2,10},{10,2},{3,11},{11,3},{4,12},{12,4},... | collective-permute-start | bytes 786440 | tf_op jit(solution)/shard_map/ppermute | solution.py:265
  6.4 2.8 %collective-permute-start.4 = (bf16[256,256]{1,0:T(8,128)(2,1)S(1)}, bf16[256,256]{1,0:T(8,128)(2,1)S(1)}, u32[]{:S(2)}, u32[]{:S(2)}) collective-permute-start(bf16[256,256]{1,0:T(8,128)(2,1)S(1)} %get-tuple-element.18), channel_id=1, source_target_pairs={{0,8},{8,0},{1,9},{9,1},{2,10},{10,2},{3,11},{11,3},{4,12},{12,4},... | collective-permute-start | bytes 393224 | tf_op jit(solution)/shard_map/ppermute | solution.py:265
  6.5 6.1 %collective-permute-start.1 = (bf16[2,128,256]{2,1,0:T(8,128)(2,1)}, bf16[2,128,256]{2,1,0:T(8,128)(2,1)S(1)}, u32[]{:S(2)}, u32[]{:S(2)}) collective-permute-start(bf16[2,128,256]{2,1,0:T(8,128)(2,1)} %bitcast.18), channel_id=1, source_target_pairs={{0,64},{64,128},{128,192},{192,0},{1,65},{65,129},{129,193},{193,1... | collective-permute-start | bytes 393224 | tf_op jit(solution)/shard_map/ppermute | solution.py:274
  6.5 23.2 %collective-permute-start.2 = (bf16[2,128,256]{2,1,0:T(8,128)(2,1)}, bf16[2,128,256]{2,1,0:T(8,128)(2,1)}, u32[]{:S(2)}, u32[]{:S(2)}) collective-permute-start(bf16[2,128,256]{2,1,0:T(8,128)(2,1)} %bitcast.19), channel_id=1, source_target_pairs={{0,192},{64,0},{128,64},{192,128},{1,193},{65,1},{129,65},{193,129... | collective-permute-start | bytes 393224 | tf_op jit(solution)/shard_map/ppermute | solution.py:274
  9.2 20.5 %collective-permute-start.3 = (bf16[2,128,256]{2,1,0:T(8,128)(2,1)}, bf16[2,128,256]{2,1,0:T(8,128)(2,1)}, u32[]{:S(2)}, u32[]{:S(2)}) collective-permute-start(bf16[2,128,256]{2,1,0:T(8,128)(2,1)} %bitcast.20), channel_id=1, source_target_pairs={{0,128},{64,192},{128,0},{192,64},{1,129},{65,193},{129,1},{193,65... | collective-permute-start | bytes 393224 | tf_op jit(solution)/shard_map/ppermute | solution.py:274
  9.2 20.5 %collective-permute-start.5 = (bf16[2,128,256]{2,1,0:T(8,128)(2,1)S(1)}, bf16[2,128,256]{2,1,0:T(8,128)(2,1)}, u32[]{:S(2)}, u32[]{:S(2)}) collective-permute-start(bf16[2,128,256]{2,1,0:T(8,128)(2,1)S(1)} %bitcast.14), channel_id=1, source_target_pairs={{0,16},{16,32},{32,48},{48,0},{1,17},{17,33},{33,49},{49,1},{2,18}... | collective-permute-start | bytes 393224 | tf_op jit(solution)/shard_map/ppermute | solution.py:274
  13.2 16.5 %collective-permute-start.6 = (bf16[2,128,256]{2,1,0:T(8,128)(2,1)S(1)}, bf16[2,128,256]{2,1,0:T(8,128)(2,1)}, u32[]{:S(2)}, u32[]{:S(2)}) collective-permute-start(bf16[2,128,256]{2,1,0:T(8,128)(2,1)S(1)} %bitcast.15), channel_id=1, source_target_pairs={{0,48},{16,0},{32,16},{48,32},{1,49},{17,1},{33,17},{49,33},{2,50}... | collective-permute-start | bytes 393224 | tf_op jit(solution)/shard_map/ppermute | solution.py:274
  14.2 15.5 %collective-permute-start.7 = (bf16[2,128,256]{2,1,0:T(8,128)(2,1)S(1)}, bf16[2,128,256]{2,1,0:T(8,128)(2,1)}, u32[]{:S(2)}, u32[]{:S(2)}) collective-permute-start(bf16[2,128,256]{2,1,0:T(8,128)(2,1)S(1)} %bitcast.16), channel_id=1, source_target_pairs={{0,32},{16,48},{32,0},{48,16},{1,33},{17,49},{33,1},{49,17},{2,34}... | collective-permute-start | bytes 393224 | tf_op jit(solution)/shard_map/ppermute | solution.py:274
  14.6 27.8 %copy-start.1 = (bf16[3,512,512]{2,1,0:T(8,128)(2,1)S(1)}, bf16[3,512,512]{2,1,0:T(8,128)(2,1)}, u32[]{:S(2)}) copy-start(bf16[3,512,512]{2,1,0:T(8,128)(2,1)} %w_ref.1) | copy-start | bytes 4718596
  15.5 26.9 %all-to-all-start = ((bf16[128,8,128]{2,1,0:T(8,128)(2,1)}), bf16[128,8,128]{2,1,0:T(8,128)(2,1)S(1)}, u32[]{:S(2)}, u32[]{:S(2)}) async-start(bf16[128,8,128]{2,1,0:T(8,128)(2,1)} %bitcast.24), calls=%async_computation | async-start | bytes 524288 | tf_op jit(solution)/shard_map/all_to_all | solution.py:269
  35.6 31.0 %collective-permute-start.13 = (bf16[8,128,256]{2,1,0:T(8,128)(2,1)}, bf16[8,128,256]{2,1,0:T(8,128)(2,1)}, u32[]{:S(2)}, u32[]{:S(2)}) collective-permute-start(bf16[8,128,256]{2,1,0:T(8,128)(2,1)} %get-tuple-element.22.refs_0_), channel_id=1, source_target_pairs={{0,16},{16,32},{32,48},{48,0},{1,17},{17,33},{33,49},{49,1},{2,18}... | collective-permute-start | bytes 1572872 | tf_op jit(solution)/shard_map/ppermute | solution.py:274
  36.2 32.1 %collective-permute-start.14 = (bf16[8,128,256]{2,1,0:T(8,128)(2,1)}, bf16[8,128,256]{2,1,0:T(8,128)(2,1)}, u32[]{:S(2)}, u32[]{:S(2)}) collective-permute-start(bf16[8,128,256]{2,1,0:T(8,128)(2,1)} %get-tuple-element.22.refs_0_), channel_id=1, source_target_pairs={{0,48},{16,0},{32,16},{48,32},{1,49},{17,1},{33,17},{49,33},{2,50}... | collective-permute-start | bytes 1572872 | tf_op jit(solution)/shard_map/ppermute | solution.py:274
  38.3 31.5 %collective-permute-start.11 = (bf16[24,128,128]{2,1,0:T(8,128)(2,1)}, bf16[24,128,128]{2,1,0:T(8,128)(2,1)}, u32[]{:S(2)}, u32[]{:S(2)}) collective-permute-start(bf16[24,128,128]{2,1,0:T(8,128)(2,1)} %bitcast.25), channel_id=1, source_target_pairs={{0,8},{8,0},{1,9},{9,1},{2,10},{10,2},{3,11},{11,3},{4,12},{12,4},... | collective-permute-start | bytes 2359304 | tf_op jit(solution)/shard_map/ppermute | solution.py:265
  49.2 43.5 %copy-start.3 = (bf16[8,128,256]{2,1,0:T(8,128)(2,1)S(1)}, bf16[8,128,256]{2,1,0:T(8,128)(2,1)}, u32[]{:S(2)}) copy-start(bf16[8,128,256]{2,1,0:T(8,128)(2,1)} %copy-done.2) | copy-start | bytes 1572868
  49.2 26.0 %all-to-all-start.1 = ((bf16[128,8,128]{2,1,0:T(8,128)(2,1)}), bf16[128,8,128]{2,1,0:T(8,128)(2,1)S(1)}, u32[]{:S(2)}, u32[]{:S(2)}) async-start(bf16[128,8,128]{2,1,0:T(8,128)(2,1)} %bitcast.23), calls=%async_computation.1 | async-start | bytes 524288 | tf_op jit(solution)/shard_map/all_to_all | solution.py:269
  60.8 2.0 %collective-permute-start.9 = (s32[1,24]{1,0:T(1,128)S(1)}, s32[1,24]{1,0:T(1,128)S(1)}, u32[]{:S(2)}, u32[]{:S(2)}) collective-permute-start(s32[1,24]{1,0:T(1,128)S(1)} %copy-done.10), channel_id=1, source_target_pairs={{0,8},{8,0},{1,9},{9,1},{2,10},{10,2},{3,11},{11,3},{4,12},{12,4},... | collective-permute-start | bytes 296 | tf_op jit(solution)/shard_map/ppermute | solution.py:265
  61.2 1.4 %collective-permute-start.10 = (s32[1,1]{1,0:T(1,128)}, s32[1,1]{1,0:T(1,128)}, u32[]{:S(2)}, u32[]{:S(2)}) collective-permute-start(s32[1,1]{1,0:T(1,128)} %param.14), channel_id=1, source_target_pairs={{0,8},{8,0},{1,9},{9,1},{2,10},{10,2},{3,11},{11,3},{4,12},{12,4},... | collective-permute-start | bytes 20 | tf_op jit(solution)/shard_map/ppermute | solution.py:265
  62.6 2.5 %collective-permute-start.12 = (s32[1,24]{1,0:T(1,128)S(1)}, s32[1,24]{1,0:T(1,128)S(1)}, u32[]{:S(2)}, u32[]{:S(2)}) collective-permute-start(s32[1,24]{1,0:T(1,128)S(1)} %copy-done.11), channel_id=1, source_target_pairs={{0,8},{8,0},{1,9},{9,1},{2,10},{10,2},{3,11},{11,3},{4,12},{12,4},... | collective-permute-start | bytes 296 | tf_op jit(solution)/shard_map/ppermute | solution.py:265
  62.9 18.0 %collective-permute-start.15 = (bf16[8,128,256]{2,1,0:T(8,128)(2,1)}, bf16[8,128,256]{2,1,0:T(8,128)(2,1)S(1)}, u32[]{:S(2)}, u32[]{:S(2)}) collective-permute-start(bf16[8,128,256]{2,1,0:T(8,128)(2,1)} %get-tuple-element.22.refs_0_), channel_id=1, source_target_pairs={{0,32},{16,48},{32,0},{48,16},{1,33},{17,49},{33,1},{49,17},{2,34}... | collective-permute-start | bytes 1572872 | tf_op jit(solution)/shard_map/ppermute | solution.py:274
  65.2 15.9 %collective-permute-start.16 = (bf16[8,128,256]{2,1,0:T(8,128)(2,1)}, bf16[8,128,256]{2,1,0:T(8,128)(2,1)S(1)}, u32[]{:S(2)}, u32[]{:S(2)}) collective-permute-start(bf16[8,128,256]{2,1,0:T(8,128)(2,1)} %copy-done.2), channel_id=1, source_target_pairs={{0,64},{64,128},{128,192},{192,0},{1,65},{65,129},{129,193},{193,1... | collective-permute-start | bytes 1572872 | tf_op jit(solution)/shard_map/ppermute | solution.py:274
  66.6 14.5 %collective-permute-start.17 = (bf16[8,128,256]{2,1,0:T(8,128)(2,1)}, bf16[8,128,256]{2,1,0:T(8,128)(2,1)S(1)}, u32[]{:S(2)}, u32[]{:S(2)}) collective-permute-start(bf16[8,128,256]{2,1,0:T(8,128)(2,1)} %copy-done.2), channel_id=1, source_target_pairs={{0,192},{64,0},{128,64},{192,128},{1,193},{65,1},{129,65},{193,129... | collective-permute-start | bytes 1572872 | tf_op jit(solution)/shard_map/ppermute | solution.py:274
  68.3 24.5 %collective-permute-start.18 = (bf16[8,128,256]{2,1,0:T(8,128)(2,1)}, bf16[8,128,256]{2,1,0:T(8,128)(2,1)S(1)}, u32[]{:S(2)}, u32[]{:S(2)}) collective-permute-start(bf16[8,128,256]{2,1,0:T(8,128)(2,1)} %copy-done.2), channel_id=1, source_target_pairs={{0,128},{64,192},{128,0},{192,64},{1,129},{65,193},{129,1},{193,65... | collective-permute-start | bytes 1572872 | tf_op jit(solution)/shard_map/ppermute | solution.py:274
  75.2 22.6 %collective-permute-start.8 = (bf16[1024,128]{1,0:T(8,128)(2,1)S(1)}, bf16[1024,128]{1,0:T(8,128)(2,1)S(1)}, u32[]{:S(2)}, u32[]{:S(2)}) collective-permute-start(bf16[1024,128]{1,0:T(8,128)(2,1)S(1)} %bitcast.11), channel_id=1, source_target_pairs={{0,8},{8,0},{1,9},{9,1},{2,10},{10,2},{3,11},{11,3},{4,12},{12,4},... | collective-permute-start | bytes 786440 | tf_op jit(solution)/shard_map/ppermute | solution.py:265
  95.5 2.3 %collective-permute-start.19 = (bf16[256,256]{1,0:T(8,128)(2,1)S(1)}, bf16[256,256]{1,0:T(8,128)(2,1)S(1)}, u32[]{:S(2)}, u32[]{:S(2)}) collective-permute-start(bf16[256,256]{1,0:T(8,128)(2,1)S(1)} %get-tuple-element.25), channel_id=1, source_target_pairs={{0,8},{8,0},{1,9},{9,1},{2,10},{10,2},{3,11},{11,3},{4,12},{12,4},... | collective-permute-start | bytes 393224 | tf_op jit(solution)/shard_map/ppermute | solution.py:265
  (10 other events, 83.1 us)

commit v5 on v3

--- a/solution.py
+++ b/solution.py
@@ -54,7 +54,9 @@
     return tuple(lax.axis_index(axis).astype(jnp.int32) for axis in ("x", "y", "c", "z"))
 
 
-def pool_kernel(feat_hbm, pool_hbm, send_ref, keep_ref, mine_ref, give_ref, feat_ref, pool_ref, sems):
+def pool_kernel(
+    feat_hbm, pool_hbm, send_ref, keep_ref, mine_hbm, give_ref, feat_ref, pool_ref, mine_ref, sems
+):
     fetch = [pltpu.make_async_copy(feat_hbm, feat_ref, sems.at[0]), pltpu.make_async_copy(pool_hbm, pool_ref, sems.at[1])]
     for cp in fetch:
         cp.start()
@@ -68,9 +70,16 @@
     gates = jax.nn.sigmoid(mm(feat, pool_ref[:, pl.ds(other, half)], NN)).astype(BF16)
     send_ref[...] = mm(gates, feat, TN).astype(BF16)
     gates = jax.nn.sigmoid(mm(feat, pool_ref[:, pl.ds(own, half)], NN)).astype(BF16)
-    keep_ref[...] = mm(gates, feat, TN)
     mine_ref[...] = feat_ref[:, pl.ds(own, half)]
     give_ref[...] = feat_ref[:, pl.ds(other, half)]
+    store = pltpu.make_async_copy(mine_ref, mine_hbm, sems.at[2])
+    store.start()
+    keep_ref[...] = mm(gates, feat, TN)
+    store.wait()
+
+
+def in_hbm(x):
+    return pltpu.with_memory_space_constraint(x, HB)
 
 
 def join_kernel(*refs):
@@ -104,18 +113,21 @@
     out_ref[...] = jnp.broadcast_to(total.astype(BF16)[None], out_ref.shape)
 
 
-def chain_kernel(summ_ref, w_in_ref, w_ref, offset_ref, start_ref, out_ref, side_ref, startt_ref):
+def chain_kernel(summ_ref, w_in_ref, w_ref, offset_ref, start_hbm, out_ref, side_ref, startt_ref, start_ref, sem):
     n_t, cols, width = summ_ref.shape
     x, y, core, last = place()
     col0 = core * (width // C) + (x * Y + y) * cols
     window = pl.multiple_of((col0 // BLOCK) * BLOCK, BLOCK)
-    startt_ref[...] = start_ref[:, pl.ds(window, BLOCK)].T
+    fetch = pltpu.make_async_copy(start_hbm.at[:, pl.ds(window, BLOCK)], start_ref, sem)
+    fetch.start()
     summ = summ_ref[...].reshape(n_t * cols, width)
     for g in range(3):
         side = mm(summ, w_in_ref[g], NT)
         if g == 0:
             side = side - offset_ref[...]
         side_ref[g] = side.reshape(n_t, cols, width)
+    fetch.wait()
+    startt_ref[...] = start_ref[...].T
     state = startt_ref[pl.ds(pl.multiple_of(lax.rem(col0, BLOCK), cols), cols), :]
 
     def step(t, state):
@@ -227,10 +239,16 @@
     feat_half = jax.ShapeDtypeStruct((rows_dev, half), BF16)
     send, keep, feat_mine, feat_give = call(
         pool_kernel,
-        (bf_half, jax.ShapeDtypeStruct((half, width), F32), feat_half, feat_half),
+        (bf_half, jax.ShapeDtypeStruct((half, width), F32), pltpu.HBM(feat_half.shape, BF16), feat_half),
         [hspec(), hspec()],
-        scratch=[pltpu.VMEM(feat.shape, BF16), pltpu.VMEM(pool_weight.shape, BF16), pltpu.SemaphoreType.DMA((2,))],
-    )(feat, pool_weight)
+        out=(vspec(), vspec(), hspec(), vspec()),
+        scratch=[
+            pltpu.VMEM(feat.shape, BF16),
+            pltpu.VMEM(pool_weight.shape, BF16),
+            pltpu.VMEM(feat_half.shape, BF16),
+            pltpu.SemaphoreType.DMA((3,)),
+        ],
+    )(in_hbm(feat), in_hbm(pool_weight))
     partial = (keep + swap(send).astype(F32)).astype(BF16)
     cols = half // CHIPS
     parts = trade(partial.reshape(CHIPS, cols, width), ("x", "y"))
@@ -271,13 +289,15 @@
     evolved = call(
         chain_kernel,
         jax.ShapeDtypeStruct((CHIPS, cols, width), BF16),
-        [vspec()] * 5,
+        [vspec()] * 4 + [hspec()],
         scratch=[
             pltpu.VMEM((3, n_tm, cols, width), F32),
             pltpu.VMEM((BLOCK, width), F32),
+            pltpu.VMEM((width, BLOCK), F32),
+            pltpu.SemaphoreType.DMA(()),
         ],
         vmem_mib=8,
-    )(summ, w_in, w_state, gate_offset[None, :], start_weight)
+    )(summ, w_in, w_state, gate_offset[None, :], in_hbm(start_weight))
     wt_own = trade(evolved, ("x", "y")).reshape(half, width)
     wt_oth = swap(wt_own)
     hidden, weights = call(

time: 108 us -> 108 us (level)
  local copies, waits for them, and re-layouts: 5.69 us -> 2.75 us
  Pallas kernels: 13 us -> 15.5 us
    unnamed x30 -> x20, local copies, waits for them, and re-layouts: 5.69 us -> 2.75 us
    pallas_call x1, Pallas kernels: 0.82 us -> 2.45 us  [layer(): call(pool_kernel, (bf_half, jax.ShapeDtypeStruct((half, width), F32), plt...]
  transfers between devices with their start and end apart: 23 -> 23, of which waited for: 9 -> 10; matrix products, arithmetic and copies ran while one was open for 1% -> 1% of each run, Pallas kernels for 10% -> 11%
where the time goes in v5:
time: 108 us
  starting transfers between devices  46.7 us (43%)
  waiting for transfers between devices  40.5 us (38%)
  Pallas kernels  15.5 us (14%)
  local copies, waits for them, and re-layouts  2.75 us (3%)
  between operations  1.48 us (1%)
    all_to_all x3, waiting for transfers between devices, trade(): return lax.all_to_all(x, axes, split_axis=0, concat_axis=0, tiled=True)  33.4 us
    all_to_all x3, starting transfers between devices, trade(): return lax.all_to_all(x, axes, split_axis=0, concat_axis=0, tiled=True)  19.5 us
    ppermute x12, starting transfers between devices, shift(): lax.ppermute(x, axis, [(i, (i + distance) % size) for i in range(size)])  17 us
    ppermute x8, starting transfers between devices, swap(): return lax.ppermute(x, 'c', [(0, 1), (1, 0)])  10.2 us
    pallas_call x1, Pallas kernels, layer(): call(agg_oth_kernel, (feat_half, jax.ShapeDtypeStruct((depth, half), BF16...  4.62 us
    ppermute x12, waiting for transfers between devices, shift(): lax.ppermute(x, axis, [(i, (i + distance) % size) for i in range(size)])  4.44 us
    pallas_call x1, Pallas kernels, layer(): call(chain_kernel, jax.ShapeDtypeStruct((CHIPS, cols, width), BF16), [vsp...  2.91 us
    unnamed x20, local copies, waits for them, and re-layouts  2.75 us
  transfers between devices with their start and end apart: 23, of which 10 were waited for; matrix products, arithmetic and copies ran while one was open for 1% of the time, Pallas kernels for 11%

profile of v5, /device:TPU:1, one launch (start us, length us, event | category | flops | bytes accessed | tf_op | source)
XLA Modules:
  0.0 107.7 jit_solution(3995551455798535610)
XLA Ops:
  0.6 2.4 %shard_map.113 = (bf16[256,512]{1,0:T(8,128)(2,1)S(1)}, f32[256,512]{1,0:T(8,128)S(1)}, bf16[256,256]{1,0:T(8,128)(2,1)}, bf16[256,256]{1,0:T(8,128)(2,1)S(1)}) custom-call(bf16[256,512]{1,0:T(8,128)(2,1)} %bitcast.23, bf16[512,512]{1,0:T(8,128)(2,1)} %pool_hbm.1), custom_call_target="tpu_custom_call" | custom-call | flops 100000000 | bytes 1000000 | tf_op jit(solution)/shard_map/pallas_call | solution.py:240
  3.1 3.3 %collective-permute-start.6 = (bf16[256,256]{1,0:T(8,128)(2,1)S(1)}, bf16[256,256]{1,0:T(8,128)(2,1)S(1)}, u32[]{:S(2)}, u32[]{:S(2)}) collective-permute-start(bf16[256,256]{1,0:T(8,128)(2,1)S(1)} %get-tuple-element.15), channel_id=1, source_target_pairs={{0,8},{8,0},{1,9},{9,1},{2,10},{10,2},{3,11},{11,3},{4,12},{12,4},... | collective-permute-start | bytes 393224 | tf_op jit(solution)/shard_map/ppermute | solution.py:203
  9.6 3.0 %collective-permute-start.12 = (bf16[2,128,256]{2,1,0:T(8,128)(2,1)S(1)}, bf16[2,128,256]{2,1,0:T(8,128)(2,1)S(1)}, u32[]{:S(2)}, u32[]{:S(2)}) collective-permute-start(bf16[2,128,256]{2,1,0:T(8,128)(2,1)S(1)} %bitcast.17), channel_id=1, source_target_pairs={{0,32},{16,48},{32,0},{48,16},{1,33},{17,49},{33,1},{49,17},{2,34}... | collective-permute-start | bytes 393224 | tf_op jit(solution)/shard_map/ppermute | solution.py:212
  14.2 1.3 %collective-permute-start.10 = (bf16[2,128,256]{2,1,0:T(8,128)(2,1)S(1)}, bf16[2,128,256]{2,1,0:T(8,128)(2,1)S(1)}, u32[]{:S(2)}, u32[]{:S(2)}) collective-permute-start(bf16[2,128,256]{2,1,0:T(8,128)(2,1)S(1)} %bitcast.19), channel_id=1, source_target_pairs={{0,16},{16,32},{32,48},{48,0},{1,17},{17,33},{33,49},{49,1},{2,18}... | collective-permute-start | bytes 393224 | tf_op jit(solution)/shard_map/ppermute | solution.py:212
  16.2 2.9 %collective-permute-done.11.refs_6_ = bf16[2,128,256]{2,1,0:T(8,128)(2,1)S(1)} collective-permute-done((bf16[2,128,256]{2,1,0:T(8,128)(2,1)S(1)}, bf16[2,128,256]{2,1,0:T(8,128)(2,1)S(1)}, u32[]{:S(2)}, u32[]{:S(2)}) %collective-permute-start.11) | collective-permute-done | bytes 131104 | tf_op jit(solution)/shard_map/ppermute | solution.py:212
  20.2 2.2 %shard_map.116 = (bf16[8,128,256]{2,1,0:T(8,128)(2,1)}, bf16[8,128,256]{2,1,0:T(8,128)(2,1)S(1)}) custom-call(bf16[2,128,256]{2,1,0:T(8,128)(2,1)S(1)} %bitcast.16, bf16[2,128,256]{2,1,0:T(8,128)(2,1)S(1)} %collective-permute-done.7.refs_1_, bf16[2,128,256]{2,1,0:T(8,128)(2,1)S(1)} %collective-permute-done.8.refs_2_, ...), custom_call_target="tpu_custom_call" | custom-call | bytes 1000000 | tf_op jit(solution)/shard_map/pallas_call | solution.py:102
  23.2 1.9 %collective-permute-start.15 = (bf16[8,128,256]{2,1,0:T(8,128)(2,1)}, bf16[8,128,256]{2,1,0:T(8,128)(2,1)}, u32[]{:S(2)}, u32[]{:S(2)}) collective-permute-start(bf16[8,128,256]{2,1,0:T(8,128)(2,1)} %get-tuple-element.16.refs_0_), channel_id=1, source_target_pairs={{0,32},{16,48},{32,0},{48,16},{1,33},{17,49},{33,1},{49,17},{2,34}... | collective-permute-start | bytes 1572872 | tf_op jit(solution)/shard_map/ppermute | solution.py:212
  25.1 1.8 %collective-permute-start.14 = (bf16[8,128,256]{2,1,0:T(8,128)(2,1)}, bf16[8,128,256]{2,1,0:T(8,128)(2,1)}, u32[]{:S(2)}, u32[]{:S(2)}) collective-permute-start(bf16[8,128,256]{2,1,0:T(8,128)(2,1)} %get-tuple-element.16.refs_0_), channel_id=1, source_target_pairs={{0,48},{16,0},{32,16},{48,32},{1,49},{17,1},{33,17},{49,33},{2,50}... | collective-permute-start | bytes 1572872 | tf_op jit(solution)/shard_map/ppermute | solution.py:212
  27.7 4.8 %all-to-all-start = ((bf16[16,16,512]{2,1,0:T(8,128)(2,1)}), bf16[16,16,512]{2,1,0:T(8,128)(2,1)S(1)}, u32[]{:S(2)}, u32[]{:S(2)}) async-start(bf16[16,16,512]{2,1,0:T(8,128)(2,1)} %bitcast.22), calls=%async_computation | async-start | bytes 524288 | tf_op jit(solution)/shard_map/all_to_all | solution.py:207
  32.6 2.3 %collective-permute-start.5 = (bf16[24,128,128]{2,1,0:T(8,128)(2,1)}, bf16[24,128,128]{2,1,0:T(8,128)(2,1)}, u32[]{:S(2)}, u32[]{:S(2)}) collective-permute-start(bf16[24,128,128]{2,1,0:T(8,128)(2,1)} %bitcast.11), channel_id=1, source_target_pairs={{0,8},{8,0},{1,9},{9,1},{2,10},{10,2},{3,11},{11,3},{4,12},{12,4},... | collective-permute-start | bytes 2359304 | tf_op jit(solution)/shard_map/ppermute | solution.py:203
  34.8 1.6 %collective-permute-start.13 = (bf16[8,128,256]{2,1,0:T(8,128)(2,1)}, bf16[8,128,256]{2,1,0:T(8,128)(2,1)}, u32[]{:S(2)}, u32[]{:S(2)}) collective-permute-start(bf16[8,128,256]{2,1,0:T(8,128)(2,1)} %get-tuple-element.16.refs_0_), channel_id=1, source_target_pairs={{0,16},{16,32},{32,48},{48,0},{1,17},{17,33},{33,49},{49,1},{2,18}... | collective-permute-start | bytes 1572872 | tf_op jit(solution)/shard_map/ppermute | solution.py:212
  36.4 15.3 %all-to-all-done.parts_ref = bf16[16,16,512]{2,1,0:T(8,128)(2,1)S(1)} async-done(((bf16[16,16,512]{2,1,0:T(8,128)(2,1)}), bf16[16,16,512]{2,1,0:T(8,128)(2,1)S(1)}, u32[]{:S(2)}, u32[]{:S(2)}) %all-to-all-start) | async-done | bytes 262176 | tf_op jit(solution)/shard_map/all_to_all | solution.py:207
  52.3 8.2 %all-to-all-start.1 = ((bf16[8,16,512]{2,1,0:T(8,128)(2,1)}), bf16[8,16,512]{2,1,0:T(8,128)(2,1)S(1)}, u32[]{:S(2)}, u32[]{:S(2)}) async-start(bf16[8,16,512]{2,1,0:T(8,128)(2,1)} %shard_map.114), calls=%async_computation.1 | async-start | bytes 262144 | tf_op jit(solution)/shard_map/all_to_all | solution.py:207
  60.5 1.8 %collective-permute-start.4 = (s32[1,1]{1,0:T(1,128)}, s32[1,1]{1,0:T(1,128)}, u32[]{:S(2)}, u32[]{:S(2)}) collective-permute-start(s32[1,1]{1,0:T(1,128)} %param.14), channel_id=1, source_target_pairs={{0,8},{8,0},{1,9},{9,1},{2,10},{10,2},{3,11},{11,3},{4,12},{12,4},... | collective-permute-start | bytes 20 | tf_op jit(solution)/shard_map/ppermute | solution.py:203
  62.3 1.1 %collective-permute-done.4.used_oth = s32[1,1]{1,0:T(1,128)} collective-permute-done((s32[1,1]{1,0:T(1,128)}, s32[1,1]{1,0:T(1,128)}, u32[]{:S(2)}, u32[]{:S(2)}) %collective-permute-start.4) | collective-permute-done | bytes 36 | tf_op jit(solution)/shard_map/ppermute | solution.py:203
  65.8 1.1 %collective-permute-start.18 = (bf16[8,128,256]{2,1,0:T(8,128)(2,1)}, bf16[8,128,256]{2,1,0:T(8,128)(2,1)}, u32[]{:S(2)}, u32[]{:S(2)}) collective-permute-start(bf16[8,128,256]{2,1,0:T(8,128)(2,1)} %copy-done.3), channel_id=1, source_target_pairs={{0,128},{64,192},{128,0},{192,64},{1,129},{65,193},{129,1},{193,65... | collective-permute-start | bytes 1572872 | tf_op jit(solution)/shard_map/ppermute | solution.py:212
  66.9 2.8 %collective-permute-start.17 = (bf16[8,128,256]{2,1,0:T(8,128)(2,1)}, bf16[8,128,256]{2,1,0:T(8,128)(2,1)}, u32[]{:S(2)}, u32[]{:S(2)}) collective-permute-start(bf16[8,128,256]{2,1,0:T(8,128)(2,1)} %copy-done.3), channel_id=1, source_target_pairs={{0,192},{64,0},{128,64},{192,128},{1,193},{65,1},{129,65},{193,129... | collective-permute-start | bytes 1572872 | tf_op jit(solution)/shard_map/ppermute | solution.py:212
  69.7 2.9 %shard_map.115 = bf16[16,16,512]{2,1,0:T(8,128)(2,1)} custom-call(bf16[8,16,512]{2,1,0:T(8,128)(2,1)S(1)} %all-to-all-done.1.summ_ref, bf16[3,512,512]{2,1,0:T(8,128)(2,1)S(1)} %copy-done, bf16[3,512,512]{2,1,0:T(8,128)(2,1)S(1)} %copy-done.1, f32[1,512]{1,0:T(1,128)S(1)} %bitcast.21, f32[512,512]{1,0:T(8,128)} %start_hbm.1), custom_call_target="tpu_custom_call" | custom-call | flops 100000000 | bytes 1000000 | tf_op jit(solution)/shard_map/pallas_call | solution.py:289
  72.6 6.5 %all-to-all-start.2 = ((bf16[16,16,512]{2,1,0:T(8,128)(2,1)}), bf16[16,16,512]{2,1,0:T(8,128)(2,1)S(1)}, u32[]{:S(2)}, u32[]{:S(2)}) async-start(bf16[16,16,512]{2,1,0:T(8,128)(2,1)} %shard_map.115), calls=%async_computation.2 | async-start | bytes 524288 | tf_op jit(solution)/shard_map/all_to_all | solution.py:207
  79.1 18.1 %all-to-all-done.2 = bf16[16,16,512]{2,1,0:T(8,128)(2,1)S(1)} async-done(((bf16[16,16,512]{2,1,0:T(8,128)(2,1)}), bf16[16,16,512]{2,1,0:T(8,128)(2,1)S(1)}, u32[]{:S(2)}, u32[]{:S(2)}) %all-to-all-start.2) | async-done | bytes 262176 | tf_op jit(solution)/shard_map/all_to_all | solution.py:207
  97.2 1.3 %collective-permute-start.1 = (bf16[256,512]{1,0:T(8,128)(2,1)S(1)}, bf16[256,512]{1,0:T(8,128)(2,1)S(1)}, u32[]{:S(2)}, u32[]{:S(2)}) collective-permute-start(bf16[256,512]{1,0:T(8,128)(2,1)S(1)} %bitcast.9), channel_id=1, source_target_pairs={{0,8},{8,0},{1,9},{9,1},{2,10},{10,2},{3,11},{11,3},{4,12},{12,4},... | collective-permute-start | bytes 786440 | tf_op jit(solution)/shard_map/ppermute | solution.py:203
  99.6 4.6 %shard_map.117 = (bf16[256,256]{1,0:T(8,128)(2,1)S(1)}, bf16[3072,256]{1,0:T(8,128)(2,1)S(1)}) custom-call(s32[1,24]{1,0:T(1,128)S(1)} %copy-done.8, s32[1,24]{1,0:T(1,128)S(1)} %collective-permute-done.2.cols_oth, s32[1,24]{1,0:T(1,128)S(1)} %collective-permute-done.3.rows_oth, s32[1,1]{1,0:T(1,128)} %collective-permute-done.4.used_oth, ...), custom_call_target="tpu_custom_call" | custom-call | flops 100000000 | bytes 1000000 | tf_op jit(solution)/shard_map/pallas_call | solution.py:272
  105.0 1.2 %shard_map.118.agg_own = bf16[256,256]{1,0:T(8,128)(2,1)S(1)} custom-call(s32[1,24]{1,0:T(1,128)S(1)} %copy-done.9, s32[1,1]{1,0:T(1,128)S(6)} %copy.12.used, bf16[24,128,128]{2,1,0:T(8,128)(2,1)S(1)} %bitcast.12, bf16[256,256]{1,0:T(8,128)(2,1)S(1)} %copy-done.6, bf16[3072,256]{1,0:T(8,128)(2,1)S(1)} %get-tuple-element.18.rhs), custom_call_target="tpu_custom_call" | custom-call | flops 100000000 | bytes 1000000 | tf_op jit(solution)/shard_map/pallas_call | solution.py:285
  106.3 1.5 %shard_map.119 = (bf16[256,512]{1,0:T(8,128)(2,1)}, f32[512,512]{1,0:T(8,128)}) custom-call(bf16[256,512]{1,0:T(8,128)(2,1)S(1)} %bitcast.10, bf16[256,512]{1,0:T(8,128)(2,1)S(1)} %collective-permute-done.1.wt_oth, bf16[256,256]{1,0:T(8,128)(2,1)S(1)} %shard_map.118.agg_own, bf16[256,256]{1,0:T(8,128)(2,1)S(1)} %collective-permute-done.19.agg_oth), custom_call_target="tpu_custom_call" | custom-call | flops 100000000 | bytes 1000000 | tf_op jit(solution)/shard_map/pallas_call | solution.py:303
  (50 shorter events, 12.5 us)
Async XLA Ops:
  3.1 6.4 %collective-permute-start.6 = (bf16[256,256]{1,0:T(8,128)(2,1)S(1)}, bf16[256,256]{1,0:T(8,128)(2,1)S(1)}, u32[]{:S(2)}, u32[]{:S(2)}) collective-permute-start(bf16[256,256]{1,0:T(8,128)(2,1)S(1)} %get-tuple-element.15), channel_id=1, source_target_pairs={{0,8},{8,0},{1,9},{9,1},{2,10},{10,2},{3,11},{11,3},{4,12},{12,4},... | collective-permute-start | bytes 393224 | tf_op jit(solution)/shard_map/ppermute | solution.py:203
  6.4 6.7 %collective-permute-start.9 = (bf16[2,128,256]{2,1,0:T(8,128)(2,1)}, bf16[2,128,256]{2,1,0:T(8,128)(2,1)S(1)}, u32[]{:S(2)}, u32[]{:S(2)}) collective-permute-start(bf16[2,128,256]{2,1,0:T(8,128)(2,1)} %bitcast.13), channel_id=1, source_target_pairs={{0,128},{64,192},{128,0},{192,64},{1,129},{65,193},{129,1},{193,65... | collective-permute-start | bytes 393224 | tf_op jit(solution)/shard_map/ppermute | solution.py:212
  7.4 6.8 %collective-permute-start.8 = (bf16[2,128,256]{2,1,0:T(8,128)(2,1)}, bf16[2,128,256]{2,1,0:T(8,128)(2,1)S(1)}, u32[]{:S(2)}, u32[]{:S(2)}) collective-permute-start(bf16[2,128,256]{2,1,0:T(8,128)(2,1)} %bitcast.14), channel_id=1, source_target_pairs={{0,192},{64,0},{128,64},{192,128},{1,193},{65,1},{129,65},{193,129... | collective-permute-start | bytes 393224 | tf_op jit(solution)/shard_map/ppermute | solution.py:212
  8.3 61.4 %copy-start.7 = (f32[512]{0:T(512)S(1)}, f32[512]{0:T(512)}, u32[]{:S(2)}) copy-start(f32[512]{0:T(512)} %param.18) | copy-start | bytes 6148
  8.3 18.7 %collective-permute-start = (bf16[256,512]{1,0:T(8,128)(2,1)S(1)}, bf16[256,512]{1,0:T(8,128)(2,1)S(1)}, u32[]{:S(2)}, u32[]{:S(2)}) collective-permute-start(bf16[256,512]{1,0:T(8,128)(2,1)S(1)} %get-tuple-element.13), channel_id=1, source_target_pairs={{0,8},{8,0},{1,9},{9,1},{2,10},{10,2},{3,11},{11,3},{4,12},{12,4},... | collective-permute-start | bytes 786440 | tf_op jit(solution)/shard_map/ppermute | solution.py:203
  8.9 7.3 %collective-permute-start.7 = (bf16[2,128,256]{2,1,0:T(8,128)(2,1)}, bf16[2,128,256]{2,1,0:T(8,128)(2,1)S(1)}, u32[]{:S(2)}, u32[]{:S(2)}) collective-permute-start(bf16[2,128,256]{2,1,0:T(8,128)(2,1)} %bitcast.15), channel_id=1, source_target_pairs={{0,64},{64,128},{128,192},{192,0},{1,65},{65,129},{129,193},{193,1... | collective-permute-start | bytes 393224 | tf_op jit(solution)/shard_map/ppermute | solution.py:212
  9.6 6.6 %collective-permute-start.12 = (bf16[2,128,256]{2,1,0:T(8,128)(2,1)S(1)}, bf16[2,128,256]{2,1,0:T(8,128)(2,1)S(1)}, u32[]{:S(2)}, u32[]{:S(2)}) collective-permute-start(bf16[2,128,256]{2,1,0:T(8,128)(2,1)S(1)} %bitcast.17), channel_id=1, source_target_pairs={{0,32},{16,48},{32,0},{48,16},{1,33},{17,49},{33,1},{49,17},{2,34}... | collective-permute-start | bytes 393224 | tf_op jit(solution)/shard_map/ppermute | solution.py:212
  13.0 6.0 %collective-permute-start.11 = (bf16[2,128,256]{2,1,0:T(8,128)(2,1)S(1)}, bf16[2,128,256]{2,1,0:T(8,128)(2,1)S(1)}, u32[]{:S(2)}, u32[]{:S(2)}) collective-permute-start(bf16[2,128,256]{2,1,0:T(8,128)(2,1)S(1)} %bitcast.18), channel_id=1, source_target_pairs={{0,48},{16,0},{32,16},{48,32},{1,49},{17,1},{33,17},{49,33},{2,50}... | collective-permute-start | bytes 393224 | tf_op jit(solution)/shard_map/ppermute | solution.py:212
  14.2 5.1 %collective-permute-start.10 = (bf16[2,128,256]{2,1,0:T(8,128)(2,1)S(1)}, bf16[2,128,256]{2,1,0:T(8,128)(2,1)S(1)}, u32[]{:S(2)}, u32[]{:S(2)}) collective-permute-start(bf16[2,128,256]{2,1,0:T(8,128)(2,1)S(1)} %bitcast.19), channel_id=1, source_target_pairs={{0,16},{16,32},{32,48},{48,0},{1,17},{17,33},{33,49},{49,1},{2,18}... | collective-permute-start | bytes 393224 | tf_op jit(solution)/shard_map/ppermute | solution.py:212
  23.2 43.7 %collective-permute-start.15 = (bf16[8,128,256]{2,1,0:T(8,128)(2,1)}, bf16[8,128,256]{2,1,0:T(8,128)(2,1)}, u32[]{:S(2)}, u32[]{:S(2)}) collective-permute-start(bf16[8,128,256]{2,1,0:T(8,128)(2,1)} %get-tuple-element.16.refs_0_), channel_id=1, source_target_pairs={{0,32},{16,48},{32,0},{48,16},{1,33},{17,49},{33,1},{49,17},{2,34}... | collective-permute-start | bytes 1572872 | tf_op jit(solution)/shard_map/ppermute | solution.py:212
  25.1 44.5 %collective-permute-start.14 = (bf16[8,128,256]{2,1,0:T(8,128)(2,1)}, bf16[8,128,256]{2,1,0:T(8,128)(2,1)}, u32[]{:S(2)}, u32[]{:S(2)}) collective-permute-start(bf16[8,128,256]{2,1,0:T(8,128)(2,1)} %get-tuple-element.16.refs_0_), channel_id=1, source_target_pairs={{0,48},{16,0},{32,16},{48,32},{1,49},{17,1},{33,17},{49,33},{2,50}... | collective-permute-start | bytes 1572872 | tf_op jit(solution)/shard_map/ppermute | solution.py:212
  27.7 23.9 %all-to-all-start = ((bf16[16,16,512]{2,1,0:T(8,128)(2,1)}), bf16[16,16,512]{2,1,0:T(8,128)(2,1)S(1)}, u32[]{:S(2)}, u32[]{:S(2)}) async-start(bf16[16,16,512]{2,1,0:T(8,128)(2,1)} %bitcast.22), calls=%async_computation | async-start | bytes 524288 | tf_op jit(solution)/shard_map/all_to_all | solution.py:207
  32.6 66.0 %collective-permute-start.5 = (bf16[24,128,128]{2,1,0:T(8,128)(2,1)}, bf16[24,128,128]{2,1,0:T(8,128)(2,1)}, u32[]{:S(2)}, u32[]{:S(2)}) collective-permute-start(bf16[24,128,128]{2,1,0:T(8,128)(2,1)} %bitcast.11), channel_id=1, source_target_pairs={{0,8},{8,0},{1,9},{9,1},{2,10},{10,2},{3,11},{11,3},{4,12},{12,4},... | collective-permute-start | bytes 2359304 | tf_op jit(solution)/shard_map/ppermute | solution.py:203
  34.8 44.3 %collective-permute-start.13 = (bf16[8,128,256]{2,1,0:T(8,128)(2,1)}, bf16[8,128,256]{2,1,0:T(8,128)(2,1)}, u32[]{:S(2)}, u32[]{:S(2)}) collective-permute-start(bf16[8,128,256]{2,1,0:T(8,128)(2,1)} %get-tuple-element.16.refs_0_), channel_id=1, source_target_pairs={{0,16},{16,32},{32,48},{48,0},{1,17},{17,33},{33,49},{49,1},{2,18}... | collective-permute-start | bytes 1572872 | tf_op jit(solution)/shard_map/ppermute | solution.py:212
  52.3 17.4 %all-to-all-start.1 = ((bf16[8,16,512]{2,1,0:T(8,128)(2,1)}), bf16[8,16,512]{2,1,0:T(8,128)(2,1)S(1)}, u32[]{:S(2)}, u32[]{:S(2)}) async-start(bf16[8,16,512]{2,1,0:T(8,128)(2,1)} %shard_map.114), calls=%async_computation.1 | async-start | bytes 262144 | tf_op jit(solution)/shard_map/all_to_all | solution.py:207
  60.5 2.9 %collective-permute-start.4 = (s32[1,1]{1,0:T(1,128)}, s32[1,1]{1,0:T(1,128)}, u32[]{:S(2)}, u32[]{:S(2)}) collective-permute-start(s32[1,1]{1,0:T(1,128)} %param.14), channel_id=1, source_target_pairs={{0,8},{8,0},{1,9},{9,1},{2,10},{10,2},{3,11},{11,3},{4,12},{12,4},... | collective-permute-start | bytes 20 | tf_op jit(solution)/shard_map/ppermute | solution.py:203
  63.4 1.2 %collective-permute-start.3 = (s32[1,24]{1,0:T(1,128)S(1)}, s32[1,24]{1,0:T(1,128)S(1)}, u32[]{:S(2)}, u32[]{:S(2)}) collective-permute-start(s32[1,24]{1,0:T(1,128)S(1)} %copy-done.9), channel_id=1, source_target_pairs={{0,8},{8,0},{1,9},{9,1},{2,10},{10,2},{3,11},{11,3},{4,12},{12,4},... | collective-permute-start | bytes 296 | tf_op jit(solution)/shard_map/ppermute | solution.py:203
  64.6 1.2 %collective-permute-start.2 = (s32[1,24]{1,0:T(1,128)S(1)}, s32[1,24]{1,0:T(1,128)S(1)}, u32[]{:S(2)}, u32[]{:S(2)}) collective-permute-start(s32[1,24]{1,0:T(1,128)S(1)} %copy-done.8), channel_id=1, source_target_pairs={{0,8},{8,0},{1,9},{9,1},{2,10},{10,2},{3,11},{11,3},{4,12},{12,4},... | collective-permute-start | bytes 296 | tf_op jit(solution)/shard_map/ppermute | solution.py:203
  65.8 32.7 %collective-permute-start.18 = (bf16[8,128,256]{2,1,0:T(8,128)(2,1)}, bf16[8,128,256]{2,1,0:T(8,128)(2,1)}, u32[]{:S(2)}, u32[]{:S(2)}) collective-permute-start(bf16[8,128,256]{2,1,0:T(8,128)(2,1)} %copy-done.3), channel_id=1, source_target_pairs={{0,128},{64,192},{128,0},{192,64},{1,129},{65,193},{129,1},{193,65... | collective-permute-start | bytes 1572872 | tf_op jit(solution)/shard_map/ppermute | solution.py:212
  66.9 31.6 %collective-permute-start.17 = (bf16[8,128,256]{2,1,0:T(8,128)(2,1)}, bf16[8,128,256]{2,1,0:T(8,128)(2,1)}, u32[]{:S(2)}, u32[]{:S(2)}) collective-permute-start(bf16[8,128,256]{2,1,0:T(8,128)(2,1)} %copy-done.3), channel_id=1, source_target_pairs={{0,192},{64,0},{128,64},{192,128},{1,193},{65,1},{129,65},{193,129... | collective-permute-start | bytes 1572872 | tf_op jit(solution)/shard_map/ppermute | solution.py:212
  69.7 28.8 %collective-permute-start.16 = (bf16[8,128,256]{2,1,0:T(8,128)(2,1)}, bf16[8,128,256]{2,1,0:T(8,128)(2,1)}, u32[]{:S(2)}, u32[]{:S(2)}) collective-permute-start(bf16[8,128,256]{2,1,0:T(8,128)(2,1)} %copy-done.3), channel_id=1, source_target_pairs={{0,64},{64,128},{128,192},{192,0},{1,65},{65,129},{129,193},{193,1... | collective-permute-start | bytes 1572872 | tf_op jit(solution)/shard_map/ppermute | solution.py:212
  72.6 24.6 %all-to-all-start.2 = ((bf16[16,16,512]{2,1,0:T(8,128)(2,1)}), bf16[16,16,512]{2,1,0:T(8,128)(2,1)S(1)}, u32[]{:S(2)}, u32[]{:S(2)}) async-start(bf16[16,16,512]{2,1,0:T(8,128)(2,1)} %shard_map.115), calls=%async_computation.2 | async-start | bytes 524288 | tf_op jit(solution)/shard_map/all_to_all | solution.py:207
  97.2 9.1 %collective-permute-start.1 = (bf16[256,512]{1,0:T(8,128)(2,1)S(1)}, bf16[256,512]{1,0:T(8,128)(2,1)S(1)}, u32[]{:S(2)}, u32[]{:S(2)}) collective-permute-start(bf16[256,512]{1,0:T(8,128)(2,1)S(1)} %bitcast.9), channel_id=1, source_target_pairs={{0,8},{8,0},{1,9},{9,1},{2,10},{10,2},{3,11},{11,3},{4,12},{12,4},... | collective-permute-start | bytes 786440 | tf_op jit(solution)/shard_map/ppermute | solution.py:203
  104.2 2.1 %collective-permute-start.19 = (bf16[256,256]{1,0:T(8,128)(2,1)S(1)}, bf16[256,256]{1,0:T(8,128)(2,1)S(1)}, u32[]{:S(2)}, u32[]{:S(2)}) collective-permute-start(bf16[256,256]{1,0:T(8,128)(2,1)S(1)} %get-tuple-element.19), channel_id=1, source_target_pairs={{0,8},{8,0},{1,9},{9,1},{2,10},{10,2},{3,11},{11,3},{4,12},{12,4},... | collective-permute-start | bytes 393224 | tf_op jit(solution)/shard_map/ppermute | solution.py:203
  (9 other events, 272.2 us)

commit v6 on v5

--- a/solution.py
+++ b/solution.py
@@ -113,41 +113,67 @@
     out_ref[...] = jnp.broadcast_to(total.astype(BF16)[None], out_ref.shape)
 
 
-def chain_kernel(summ_ref, w_in_ref, w_ref, offset_ref, start_hbm, out_ref, side_ref, startt_ref, start_ref, sem):
-    n_t, cols, width = summ_ref.shape
-    x, y, core, last = place()
+def prepare_kernel(
+    tile_rows, tile_cols, used, w_in_hbm, w_state_hbm, start_hbm, w_in_t, w_state_t, start_t_hbm, slots, w_in, w_state, start_ref, turned_ref, start_t, sems
+):
+    cols, width = start_t.shape
+    x, y, core, _ = place()
     col0 = core * (width // C) + (x * Y + y) * cols
     window = pl.multiple_of((col0 // BLOCK) * BLOCK, BLOCK)
-    fetch = pltpu.make_async_copy(start_hbm.at[:, pl.ds(window, BLOCK)], start_ref, sem)
+    fetch = pltpu.make_async_copy(start_hbm.at[:, pl.ds(window, BLOCK)], start_ref, sems.at[0])
+    fetch.start()
+    copies = []
+    for n, (src, dst) in enumerate(((w_in_hbm, w_in), (w_state_hbm, w_state))):
+        for g in range(3):
+            cp = pltpu.make_async_copy(src.at[g], dst.at[g], sems.at[2 + 3 * n + g])
+            cp.start()
+            copies.append(cp)
+    for j in range(slots.shape[1]):
+        slots[0, j] = tile_cols[0, j]
+        slots[1, j] = jnp.where(j < used[0, 0], tile_rows[0, j] & 1, 2)
+    fetch.wait()
+    turned_ref[...] = start_ref[...].T
+    start_t[...] = turned_ref[pl.ds(pl.multiple_of(lax.rem(col0, BLOCK), cols), cols), :]
+    store = pltpu.make_async_copy(start_t, start_t_hbm, sems.at[1])
+    store.start()
+    for g in range(3):
+        copies[g].wait()
+        w_in_t[g] = w_in[g].T
+    for g in range(3):
+        copies[3 + g].wait()
+        w_state_t[g] = w_state[g].T
+    store.wait()
+
+
+def chain_kernel(summ_ref, w_in_ref, w_ref, offset_ref, start_hbm, out_ref, side_ref, start_ref, sem):
+    n_t, cols, width = summ_ref.shape
+    fetch = pltpu.make_async_copy(start_hbm, start_ref, sem)
     fetch.start()
     summ = summ_ref[...].reshape(n_t * cols, width)
     for g in range(3):
-        side = mm(summ, w_in_ref[g], NT)
+        side = mm(summ, w_in_ref[g], NN)
         if g == 0:
             side = side - offset_ref[...]
         side_ref[g] = side.reshape(n_t, cols, width)
-    fetch.wait()
-    startt_ref[...] = start_ref[...].T
-    state = startt_ref[pl.ds(pl.multiple_of(lax.rem(col0, BLOCK), cols), cols), :]
 
     def step(t, state):
         state_b = state.astype(BF16)
-        update = jax.nn.sigmoid(side_ref[0, t] + mm(state_b, w_ref[0], NT))
-        reset = jax.nn.sigmoid(side_ref[1, t] + mm(state_b, w_ref[1], NT))
-        cand = jnp.tanh(side_ref[2, t] + mm((reset * state).astype(BF16), w_ref[2], NT))
+        reset = jax.nn.sigmoid(side_ref[1, t] + mm(state_b, w_ref[1], NN))
+        update = jax.nn.sigmoid(side_ref[0, t] + mm(state_b, w_ref[0], NN))
+        cand = jnp.tanh(side_ref[2, t] + mm((reset * state).astype(BF16), w_ref[2], NN))
         return (1.0 - update) * state + update * cand
 
-    state = lax.fori_loop(0, last + 1, step, state)
+    fetch.wait()
+    state = lax.fori_loop(0, place()[3] + 1, step, start_ref[...])
     out_ref[...] = jnp.broadcast_to(state.astype(BF16)[None], out_ref.shape)
 
 
-def masked(rows, used, tiles, lhs):
+def masked(idx, tiles, lhs):
     for j in range(tiles.shape[0]):
         tile = tiles[j]
-        at = jnp.where(j < used[0, 0], rows[0, j] & 1, 2)
         for r in range(2):
             lhs[r * BLOCK : (r + 1) * BLOCK, j * BLOCK : (j + 1) * BLOCK] = jnp.where(
-                at == r, tile, jnp.zeros_like(tile)
+                idx[1, j] == r, tile, jnp.zeros_like(tile)
             )
 
 
@@ -155,7 +181,7 @@
     return jnp.where(step == 0, 0, jnp.where(step == 3, 1, step + 1))
 
 
-def agg_oth_kernel(cols_own, cols_oth, rows_oth, used_oth, tiles, feat, *refs):
+def agg_oth_kernel(idx_own, idx_oth, tiles, feat, *refs):
     pieces, (agg, rhs_own, blocks, rhs, lhs, sems) = refs[:-6], refs[-6:]
     copies = []
     first = 0
@@ -164,13 +190,13 @@
         cp.start()
         copies.append(cp)
         first += piece.shape[0]
-    masked(rows_oth, used_oth, tiles, lhs)
+    masked(idx_oth, tiles, lhs)
     for cp in copies:
         cp.wait()
     x, y, core, _ = place()
-    for cols, out in ((cols_oth, rhs), (cols_own, rhs_own)):
+    for idx, out in ((idx_oth, rhs), (idx_own, rhs_own)):
         for j in range(tiles.shape[0]):
-            col = cols[0, j]
+            col = idx[0, j]
             owner = col >> 1
             in_x = slot_of(((owner >> 3) - x) & 3)
             in_y = slot_of(((owner >> 1) - y) & 3)
@@ -179,8 +205,8 @@
     agg[...] = (feat[...].astype(F32) + mm(lhs[...], rhs[...], NN)).astype(BF16)
 
 
-def agg_own_kernel(rows, used, tiles, feat, rhs, agg, lhs):
-    masked(rows, used, tiles, lhs)
+def agg_own_kernel(idx, tiles, feat, rhs, agg, lhs):
+    masked(idx, tiles, lhs)
     agg[...] = (feat[...].astype(F32) + mm(lhs[...], rhs[...], NN)).astype(BF16)
 
 
@@ -264,7 +290,23 @@
     joined_a, joined_b = join(blocks_a, blocks_b)
     gathered = spread(joined_a, "y") + spread(joined_b, "x")
 
-    rows_oth, cols_oth, used_oth = swap(tile_rows), swap(tile_cols), swap(tile_used)
+    w_in_t, w_state_t, start_t, idx_own = call(
+        prepare_kernel,
+        (pltpu.VMEM(w_in.shape, BF16), pltpu.VMEM(w_state.shape, BF16), pltpu.HBM((cols, width), F32))
+        + (jax.ShapeDtypeStruct((2, slots), jnp.int32),),
+        [sspec()] * 3 + [hspec()] * 3,
+        out=(vspec(), vspec(), hspec(), sspec()),
+        scratch=[
+            pltpu.VMEM(w_in.shape, BF16),
+            pltpu.VMEM(w_state.shape, BF16),
+            pltpu.VMEM((width, BLOCK), F32),
+            pltpu.VMEM((BLOCK, width), F32),
+            pltpu.VMEM((cols, width), F32),
+            pltpu.SemaphoreType.DMA((8,)),
+        ],
+        vmem_mib=12,
+    )(tile_rows, tile_cols, tile_used, in_hbm(w_in), in_hbm(w_state), in_hbm(start_weight))
+    idx_oth = swap(idx_own)
     tiles_own = tile_vals[0]
     tiles_oth = swap(tiles_own)
     depth = slots * BLOCK
@@ -272,7 +314,7 @@
     agg_give, rhs_own = call(
         agg_oth_kernel,
         (feat_half, jax.ShapeDtypeStruct((depth, half), BF16)),
-        [sspec()] * 4 + [vspec()] * 2 + [pl.BlockSpec(memory_space=pl.ANY)] * len(gathered),
+        [sspec()] * 2 + [vspec()] * 2 + [pl.BlockSpec(memory_space=pl.ANY)] * len(gathered),
         scratch=[
             pltpu.VMEM((CHIPS * C * blocks_dev, BLOCK, half), BF16),
             pltpu.VMEM((depth, half), BF16),
@@ -280,11 +322,11 @@
             pltpu.SemaphoreType.DMA((len(gathered),)),
         ],
         vmem_mib=16,
-    )(tile_cols, cols_oth, rows_oth, used_oth, tiles_oth, feat_oth, *gathered)
+    )(idx_own, idx_oth, tiles_oth, feat_oth, *gathered)
     agg_oth = swap(agg_give)
     agg_own = call(
-        agg_own_kernel, feat_half, [sspec()] * 2 + [vspec()] * 3, scratch=[lhs], vmem_mib=8
-    )(tile_rows, tile_used, tiles_own, feat_mine, rhs_own)
+        agg_own_kernel, feat_half, [sspec()] + [vspec()] * 3, scratch=[lhs], vmem_mib=8
+    )(idx_own, tiles_own, feat_mine, rhs_own)
 
     evolved = call(
         chain_kernel,
@@ -292,12 +334,10 @@
         [vspec()] * 4 + [hspec()],
         scratch=[
             pltpu.VMEM((3, n_tm, cols, width), F32),
-            pltpu.VMEM((BLOCK, width), F32),
-            pltpu.VMEM((width, BLOCK), F32),
+            pltpu.VMEM((cols, width), F32),
             pltpu.SemaphoreType.DMA(()),
         ],
-        vmem_mib=8,
-    )(summ, w_in, w_state, gate_offset[None, :], in_hbm(start_weight))
+    )(summ, w_in_t, w_state_t, gate_offset[None, :], start_t)
     wt_own = trade(evolved, ("x", "y")).reshape(half, width)
     wt_oth = swap(wt_own)
     hidden, weights = call(

time: 108 us -> 107 us (level)
  waiting for transfers between devices: 40.5 us -> 28 us
  starting transfers between devices: 46.7 us -> 56.2 us
  Pallas kernels: 15.5 us -> 17.9 us
    all_to_all x3, waiting for transfers between devices: 33.4 us -> 19.1 us  [trade(): return lax.all_to_all(x, axes, split_axis=0, concat_axis=0, tiled=True)]
    ppermute x8 -> x6, starting transfers between devices: 10.2 us -> 23.7 us  [swap(): return lax.ppermute(x, 'c', [(0, 1), (1, 0)])]
    pallas_call x1 -> x2, Pallas kernels: 1.21 us -> 5.32 us  [the longest x1 3.51 us: layer(): call(prepare_kernel, (pltpu.VMEM(w_in.shape, BF16), pltpu.VMEM(w_state.sh...]
    ppermute x12, waiting for transfers between devices: 4.44 us -> 8.07 us  [shift(): lax.ppermute(x, axis, [(i, (i + distance) % size) for i in range(size)])]
    ppermute x12, starting transfers between devices: 17 us -> 13.6 us  [shift(): lax.ppermute(x, axis, [(i, (i + distance) % size) for i in range(size)])]
    ppermute x8 -> x6, waiting for transfers between devices: 2.74 us -> 0.83 us  [swap(): return lax.ppermute(x, 'c', [(0, 1), (1, 0)])]
    pallas_call x1, Pallas kernels: 2.91 us -> 1.48 us  [layer(): call(chain_kernel, jax.ShapeDtypeStruct((CHIPS, cols, width), BF16), [vsp...]
    unnamed x20 -> x12, local copies, waits for them, and re-layouts: 2.75 us -> 1.68 us
  transfers between devices with their start and end apart: 23 -> 21, of which waited for: 10 -> 8; matrix products, arithmetic and copies ran while one was open for 1% -> 1% of each run, Pallas kernels for 11% -> 13%
where the time goes in v6:
time: 107 us; the launch traced here: 106 us
  starting transfers between devices  56.2 us (53%)
  waiting for transfers between devices  28 us (26%)
  Pallas kernels  17.9 us (17%)
  local copies, waits for them, and re-layouts  1.68 us (2%)
  between operations  1.44 us (1%)
    ppermute x6, starting transfers between devices, swap(): return lax.ppermute(x, 'c', [(0, 1), (1, 0)])  23.7 us
    all_to_all x3, waiting for transfers between devices, trade(): return lax.all_to_all(x, axes, split_axis=0, concat_axis=0, tiled=True)  19.1 us
    all_to_all x3, starting transfers between devices, trade(): return lax.all_to_all(x, axes, split_axis=0, concat_axis=0, tiled=True)  18.8 us
    ppermute x12, starting transfers between devices, shift(): lax.ppermute(x, axis, [(i, (i + distance) % size) for i in range(size)])  13.6 us
    ppermute x12, waiting for transfers between devices, shift(): lax.ppermute(x, axis, [(i, (i + distance) % size) for i in range(size)])  8.07 us
    pallas_call x1, Pallas kernels, layer(): call(agg_oth_kernel, (feat_half, jax.ShapeDtypeStruct((depth, half), BF16...  4.13 us
    pallas_call x1, Pallas kernels, layer(): call(prepare_kernel, (pltpu.VMEM(w_in.shape, BF16), pltpu.VMEM(w_state.sh...  3.51 us
    pallas_call x1, Pallas kernels, layer(): call(pool_kernel, (bf_half, jax.ShapeDtypeStruct((half, width), F32), plt...  2.44 us
  transfers between devices with their start and end apart: 21, of which 8 were waited for; matrix products, arithmetic and copies ran while one was open for 1% of the time, Pallas kernels for 13%

profile of v6, /device:TPU:1, one launch (start us, length us, event | category | flops | bytes accessed | tf_op | source)
XLA Modules:
  0.0 106.0 jit_solution(3568934582908898737)
XLA Ops:
  0.6 2.4 %shard_map.113 = (bf16[256,512]{1,0:T(8,128)(2,1)S(1)}, f32[256,512]{1,0:T(8,128)S(1)}, bf16[256,256]{1,0:T(8,128)(2,1)}, bf16[256,256]{1,0:T(8,128)(2,1)S(1)}) custom-call(bf16[256,512]{1,0:T(8,128)(2,1)} %bitcast.20, bf16[512,512]{1,0:T(8,128)(2,1)} %pool_hbm.1), custom_call_target="tpu_custom_call" | custom-call | flops 100000000 | bytes 1000000 | tf_op jit(solution)/shard_map/pallas_call | solution.py:266
  3.1 3.3 %collective-permute-start.4 = (bf16[256,256]{1,0:T(8,128)(2,1)S(1)}, bf16[256,256]{1,0:T(8,128)(2,1)S(1)}, u32[]{:S(2)}, u32[]{:S(2)}) collective-permute-start(bf16[256,256]{1,0:T(8,128)(2,1)S(1)} %get-tuple-element.23), channel_id=1, source_target_pairs={{0,8},{8,0},{1,9},{9,1},{2,10},{10,2},{3,11},{11,3},{4,12},{12,4},... | collective-permute-start | bytes 393224 | tf_op jit(solution)/shard_map/ppermute | solution.py:229
  6.4 2.7 %collective-permute-start.6 = (bf16[2,128,256]{2,1,0:T(8,128)(2,1)}, bf16[2,128,256]{2,1,0:T(8,128)(2,1)S(1)}, u32[]{:S(2)}, u32[]{:S(2)}) collective-permute-start(bf16[2,128,256]{2,1,0:T(8,128)(2,1)} %bitcast.12), channel_id=1, source_target_pairs={{0,192},{64,0},{128,64},{192,128},{1,193},{65,1},{129,65},{193,129... | collective-permute-start | bytes 393224 | tf_op jit(solution)/shard_map/ppermute | solution.py:238
  9.7 1.1 %collective-permute-start.8 = (bf16[2,128,256]{2,1,0:T(8,128)(2,1)S(1)}, bf16[2,128,256]{2,1,0:T(8,128)(2,1)S(1)}, u32[]{:S(2)}, u32[]{:S(2)}) collective-permute-start(bf16[2,128,256]{2,1,0:T(8,128)(2,1)S(1)} %bitcast.15), channel_id=1, source_target_pairs={{0,16},{16,32},{32,48},{48,0},{1,17},{17,33},{33,49},{49,1},{2,18}... | collective-permute-start | bytes 393224 | tf_op jit(solution)/shard_map/ppermute | solution.py:238
  10.8 1.9 %collective-permute-done.5.refs_1_ = bf16[2,128,256]{2,1,0:T(8,128)(2,1)S(1)} collective-permute-done((bf16[2,128,256]{2,1,0:T(8,128)(2,1)}, bf16[2,128,256]{2,1,0:T(8,128)(2,1)S(1)}, u32[]{:S(2)}, u32[]{:S(2)}) %collective-permute-start.5) | collective-permute-done | bytes 131104 | tf_op jit(solution)/shard_map/ppermute | solution.py:238
  14.6 1.9 %collective-permute-done.7.refs_3_ = bf16[2,128,256]{2,1,0:T(8,128)(2,1)S(1)} collective-permute-done((bf16[2,128,256]{2,1,0:T(8,128)(2,1)}, bf16[2,128,256]{2,1,0:T(8,128)(2,1)S(1)}, u32[]{:S(2)}, u32[]{:S(2)}) %collective-permute-start.7) | collective-permute-done | bytes 131104 | tf_op jit(solution)/shard_map/ppermute | solution.py:238
  16.9 3.0 %collective-permute-done.10.refs_7_ = bf16[2,128,256]{2,1,0:T(8,128)(2,1)S(1)} collective-permute-done((bf16[2,128,256]{2,1,0:T(8,128)(2,1)S(1)}, bf16[2,128,256]{2,1,0:T(8,128)(2,1)S(1)}, u32[]{:S(2)}, u32[]{:S(2)}) %collective-permute-start.10) | collective-permute-done | bytes 131104 | tf_op jit(solution)/shard_map/ppermute | solution.py:238
  20.8 2.4 %shard_map.117 = (bf16[8,128,256]{2,1,0:T(8,128)(2,1)}, bf16[8,128,256]{2,1,0:T(8,128)(2,1)}) custom-call(bf16[2,128,256]{2,1,0:T(8,128)(2,1)S(1)} %bitcast.14, bf16[2,128,256]{2,1,0:T(8,128)(2,1)S(1)} %collective-permute-done.5.refs_1_, bf16[2,128,256]{2,1,0:T(8,128)(2,1)S(1)} %collective-permute-done.6.refs_2_, ...), custom_call_target="tpu_custom_call" | custom-call | bytes 1000000 | tf_op jit(solution)/shard_map/pallas_call | solution.py:102
  23.8 2.2 %collective-permute-start.12 = (bf16[8,128,256]{2,1,0:T(8,128)(2,1)}, bf16[8,128,256]{2,1,0:T(8,128)(2,1)}, u32[]{:S(2)}, u32[]{:S(2)}) collective-permute-start(bf16[8,128,256]{2,1,0:T(8,128)(2,1)} %get-tuple-element.24.refs_0_), channel_id=1, source_target_pairs={{0,48},{16,0},{32,16},{48,32},{1,49},{17,1},{33,17},{49,33},{2,50}... | collective-permute-start | bytes 1572872 | tf_op jit(solution)/shard_map/ppermute | solution.py:238
  26.8 4.8 %all-to-all-start = ((bf16[16,16,512]{2,1,0:T(8,128)(2,1)}), bf16[16,16,512]{2,1,0:T(8,128)(2,1)S(1)}, u32[]{:S(2)}, u32[]{:S(2)}) async-start(bf16[16,16,512]{2,1,0:T(8,128)(2,1)} %bitcast.1), calls=%async_computation | async-start | bytes 524288 | tf_op jit(solution)/shard_map/all_to_all | solution.py:233
  31.6 3.2 %collective-permute-start.3 = (bf16[24,128,128]{2,1,0:T(8,128)(2,1)}, bf16[24,128,128]{2,1,0:T(8,128)(2,1)}, u32[]{:S(2)}, u32[]{:S(2)}) collective-permute-start(bf16[24,128,128]{2,1,0:T(8,128)(2,1)} %bitcast.4.tiles), channel_id=1, source_target_pairs={{0,8},{8,0},{1,9},{9,1},{2,10},{10,2},{3,11},{11,3},{4,12},{12,4},... | collective-permute-start | bytes 2359304 | tf_op jit(solution)/shard_map/ppermute | solution.py:229
  34.8 3.1 %collective-permute-start.13 = (bf16[8,128,256]{2,1,0:T(8,128)(2,1)}, bf16[8,128,256]{2,1,0:T(8,128)(2,1)}, u32[]{:S(2)}, u32[]{:S(2)}) collective-permute-start(bf16[8,128,256]{2,1,0:T(8,128)(2,1)} %get-tuple-element.24.refs_0_), channel_id=1, source_target_pairs={{0,32},{16,48},{32,0},{48,16},{1,33},{17,49},{33,1},{49,17},{2,34}... | collective-permute-start | bytes 1572872 | tf_op jit(solution)/shard_map/ppermute | solution.py:238
  37.9 1.0 all-to-all-done.parts_ref
  39.6 6.9 %all-to-all-start.1 = ((bf16[8,16,512]{2,1,0:T(8,128)(2,1)}), bf16[8,16,512]{2,1,0:T(8,128)(2,1)S(1)}, u32[]{:S(2)}, u32[]{:S(2)}) async-start(bf16[8,16,512]{2,1,0:T(8,128)(2,1)} %shard_map.114), calls=%async_computation.1 | async-start | bytes 262144 | tf_op jit(solution)/shard_map/all_to_all | solution.py:233
  47.2 3.5 %shard_map.115 = (bf16[3,512,512]{2,1,0:T(8,128)(2,1)S(1)}, bf16[3,512,512]{2,1,0:T(8,128)(2,1)S(1)}, f32[16,512]{1,0:T(8,128)}, s32[2,24]{1,0:T(2,128)S(1)}) custom-call(s32[1,24]{1,0:T(1,128)S(1)} %copy-done.4, s32[1,24]{1,0:T(1,128)S(1)} %copy-done.5, s32[1,1]{1,0:T(1,128)S(6)} %copy.12.used, bf16[3,512,512]{2,1,0:T(8,128)(2,1)} %w_in_hbm.1, ...), custom_call_target="tpu_custom_call" | custom-call | flops 100000000 | bytes 1000000 | tf_op jit(solution)/shard_map/pallas_call | solution.py:293
  50.7 14.4 %collective-permute-start.2 = (s32[2,24]{1,0:T(2,128)S(1)}, s32[2,24]{1,0:T(2,128)S(1)}, u32[]{:S(2)}, u32[]{:S(2)}) collective-permute-start(s32[2,24]{1,0:T(2,128)S(1)} %get-tuple-element.21.idx_own.idx), channel_id=1, source_target_pairs={{0,8},{8,0},{1,9},{9,1},{2,10},{10,2},{3,11},{11,3},{4,12},{12,4},... | collective-permute-start | bytes 584 | tf_op jit(solution)/shard_map/ppermute | solution.py:229
  65.9 2.7 %collective-permute-start.15 = (bf16[8,128,256]{2,1,0:T(8,128)(2,1)}, bf16[8,128,256]{2,1,0:T(8,128)(2,1)}, u32[]{:S(2)}, u32[]{:S(2)}) collective-permute-start(bf16[8,128,256]{2,1,0:T(8,128)(2,1)} %get-tuple-element.25.refs_4_), channel_id=1, source_target_pairs={{0,192},{64,0},{128,64},{192,128},{1,193},{65,1},{129,65},{193,129... | collective-permute-start | bytes 1572872 | tf_op jit(solution)/shard_map/ppermute | solution.py:238
  69.6 1.5 %shard_map.116 = bf16[16,16,512]{2,1,0:T(8,128)(2,1)} custom-call(bf16[8,16,512]{2,1,0:T(8,128)(2,1)S(1)} %all-to-all-done.1.summ_ref, bf16[3,512,512]{2,1,0:T(8,128)(2,1)S(1)} %get-tuple-element.18.w_in_ref, bf16[3,512,512]{2,1,0:T(8,128)(2,1)S(1)} %get-tuple-element.19.w_ref, f32[1,512]{1,0:T(1,128)S(1)} %bitcast.19, f32[16,512]{1,0:T(8,128)S(1)} %copy-done.2), custom_call_target="tpu_custom_call" | custom-call | flops 100000000 | bytes 1000000 | tf_op jit(solution)/shard_map/pallas_call | solution.py:331
  71.1 7.1 %all-to-all-start.2 = ((bf16[16,16,512]{2,1,0:T(8,128)(2,1)}), bf16[16,16,512]{2,1,0:T(8,128)(2,1)S(1)}, u32[]{:S(2)}, u32[]{:S(2)}) async-start(bf16[16,16,512]{2,1,0:T(8,128)(2,1)} %shard_map.116), calls=%async_computation.2 | async-start | bytes 524288 | tf_op jit(solution)/shard_map/all_to_all | solution.py:233
  78.3 18.1 %all-to-all-done.2 = bf16[16,16,512]{2,1,0:T(8,128)(2,1)S(1)} async-done(((bf16[16,16,512]{2,1,0:T(8,128)(2,1)}), bf16[16,16,512]{2,1,0:T(8,128)(2,1)S(1)}, u32[]{:S(2)}, u32[]{:S(2)}) %all-to-all-start.2) | async-done | bytes 262176 | tf_op jit(solution)/shard_map/all_to_all | solution.py:233
  96.4 2.0 %collective-permute-start.1 = (bf16[256,512]{1,0:T(8,128)(2,1)S(1)}, bf16[256,512]{1,0:T(8,128)(2,1)S(1)}, u32[]{:S(2)}, u32[]{:S(2)}) collective-permute-start(bf16[256,512]{1,0:T(8,128)(2,1)S(1)} %bitcast.9), channel_id=1, source_target_pairs={{0,8},{8,0},{1,9},{9,1},{2,10},{10,2},{3,11},{11,3},{4,12},{12,4},... | collective-permute-start | bytes 786440 | tf_op jit(solution)/shard_map/ppermute | solution.py:229
  98.4 4.1 %shard_map.118 = (bf16[256,256]{1,0:T(8,128)(2,1)S(1)}, bf16[3072,256]{1,0:T(8,128)(2,1)S(1)}) custom-call(s32[2,24]{1,0:T(2,128)S(1)} %get-tuple-element.21.idx_own.idx, s32[2,24]{1,0:T(2,128)S(1)} %collective-permute-done.2.idx_oth, bf16[24,128,128]{2,1,0:T(8,128)(2,1)} %collective-permute-done.3.tiles, bf16[256,256]{1,0:T(8,128)(2,1)S(1)} %collective-permute-done.4.feat, ...), custom_call_target="tpu_custom_call" | custom-call | flops 100000000 | bytes 1000000 | tf_op jit(solution)/shard_map/pallas_call | solution.py:314
  102.7 1.8 %shard_map.119.agg_own = bf16[256,256]{1,0:T(8,128)(2,1)S(1)} custom-call(s32[2,24]{1,0:T(2,128)S(1)} %get-tuple-element.21.idx_own.idx, bf16[24,128,128]{2,1,0:T(8,128)(2,1)} %bitcast.4.tiles, bf16[256,256]{1,0:T(8,128)(2,1)S(1)} %copy-done.1, bf16[3072,256]{1,0:T(8,128)(2,1)S(1)} %get-tuple-element.26.rhs), custom_call_target="tpu_custom_call" | custom-call | flops 100000000 | bytes 1000000 | tf_op jit(solution)/shard_map/pallas_call | solution.py:327
  104.6 1.5 %shard_map.120 = (bf16[256,512]{1,0:T(8,128)(2,1)}, f32[512,512]{1,0:T(8,128)}) custom-call(bf16[256,512]{1,0:T(8,128)(2,1)S(1)} %bitcast.10, bf16[256,512]{1,0:T(8,128)(2,1)S(1)} %collective-permute-done.1.wt_oth, bf16[256,256]{1,0:T(8,128)(2,1)S(1)} %shard_map.119.agg_own, bf16[256,256]{1,0:T(8,128)(2,1)S(1)} %collective-permute-done.17.agg_oth), custom_call_target="tpu_custom_call" | custom-call | flops 100000000 | bytes 1000000 | tf_op jit(solution)/shard_map/pallas_call | solution.py:343
  (39 shorter events, 7.9 us)
Async XLA Ops:
  3.1 6.6 %collective-permute-start.4 = (bf16[256,256]{1,0:T(8,128)(2,1)S(1)}, bf16[256,256]{1,0:T(8,128)(2,1)S(1)}, u32[]{:S(2)}, u32[]{:S(2)}) collective-permute-start(bf16[256,256]{1,0:T(8,128)(2,1)S(1)} %get-tuple-element.23), channel_id=1, source_target_pairs={{0,8},{8,0},{1,9},{9,1},{2,10},{10,2},{3,11},{11,3},{4,12},{12,4},... | collective-permute-start | bytes 393224 | tf_op jit(solution)/shard_map/ppermute | solution.py:229
  6.4 6.4 %collective-permute-start.5 = (bf16[2,128,256]{2,1,0:T(8,128)(2,1)}, bf16[2,128,256]{2,1,0:T(8,128)(2,1)S(1)}, u32[]{:S(2)}, u32[]{:S(2)}) collective-permute-start(bf16[2,128,256]{2,1,0:T(8,128)(2,1)} %bitcast.11), channel_id=1, source_target_pairs={{0,64},{64,128},{128,192},{192,0},{1,65},{65,129},{129,193},{193,1... | collective-permute-start | bytes 393224 | tf_op jit(solution)/shard_map/ppermute | solution.py:238
  6.4 8.2 %collective-permute-start.6 = (bf16[2,128,256]{2,1,0:T(8,128)(2,1)}, bf16[2,128,256]{2,1,0:T(8,128)(2,1)S(1)}, u32[]{:S(2)}, u32[]{:S(2)}) collective-permute-start(bf16[2,128,256]{2,1,0:T(8,128)(2,1)} %bitcast.12), channel_id=1, source_target_pairs={{0,192},{64,0},{128,64},{192,128},{1,193},{65,1},{129,65},{193,129... | collective-permute-start | bytes 393224 | tf_op jit(solution)/shard_map/ppermute | solution.py:238
  9.0 16.9 %collective-permute-start = (bf16[256,512]{1,0:T(8,128)(2,1)S(1)}, bf16[256,512]{1,0:T(8,128)(2,1)S(1)}, u32[]{:S(2)}, u32[]{:S(2)}) collective-permute-start(bf16[256,512]{1,0:T(8,128)(2,1)S(1)} %get-tuple-element.17), channel_id=1, source_target_pairs={{0,8},{8,0},{1,9},{9,1},{2,10},{10,2},{3,11},{11,3},{4,12},{12,4},... | collective-permute-start | bytes 786440 | tf_op jit(solution)/shard_map/ppermute | solution.py:229
  9.7 6.8 %collective-permute-start.7 = (bf16[2,128,256]{2,1,0:T(8,128)(2,1)}, bf16[2,128,256]{2,1,0:T(8,128)(2,1)S(1)}, u32[]{:S(2)}, u32[]{:S(2)}) collective-permute-start(bf16[2,128,256]{2,1,0:T(8,128)(2,1)} %bitcast.13), channel_id=1, source_target_pairs={{0,128},{64,192},{128,0},{192,64},{1,129},{65,193},{129,1},{193,65... | collective-permute-start | bytes 393224 | tf_op jit(solution)/shard_map/ppermute | solution.py:238
  9.7 37.4 %copy-start.4 = (s32[1,24]{1,0:T(1,128)S(1)}, s32[1,24]{1,0:T(1,128)}, u32[]{:S(2)}) copy-start(s32[1,24]{1,0:T(1,128)} %tile_rows.1) | copy-start | bytes 292
  9.7 37.4 %copy-start.5 = (s32[1,24]{1,0:T(1,128)S(1)}, s32[1,24]{1,0:T(1,128)}, u32[]{:S(2)}) copy-start(s32[1,24]{1,0:T(1,128)} %tile_cols.1) | copy-start | bytes 292
  9.7 6.7 %collective-permute-start.8 = (bf16[2,128,256]{2,1,0:T(8,128)(2,1)S(1)}, bf16[2,128,256]{2,1,0:T(8,128)(2,1)S(1)}, u32[]{:S(2)}, u32[]{:S(2)}) collective-permute-start(bf16[2,128,256]{2,1,0:T(8,128)(2,1)S(1)} %bitcast.15), channel_id=1, source_target_pairs={{0,16},{16,32},{32,48},{48,0},{1,17},{17,33},{33,49},{49,1},{2,18}... | collective-permute-start | bytes 393224 | tf_op jit(solution)/shard_map/ppermute | solution.py:238
  12.8 4.1 %collective-permute-start.9 = (bf16[2,128,256]{2,1,0:T(8,128)(2,1)S(1)}, bf16[2,128,256]{2,1,0:T(8,128)(2,1)S(1)}, u32[]{:S(2)}, u32[]{:S(2)}) collective-permute-start(bf16[2,128,256]{2,1,0:T(8,128)(2,1)S(1)} %bitcast.16), channel_id=1, source_target_pairs={{0,48},{16,0},{32,16},{48,32},{1,49},{17,1},{33,17},{49,33},{2,50}... | collective-permute-start | bytes 393224 | tf_op jit(solution)/shard_map/ppermute | solution.py:238
  14.6 5.3 %collective-permute-start.10 = (bf16[2,128,256]{2,1,0:T(8,128)(2,1)S(1)}, bf16[2,128,256]{2,1,0:T(8,128)(2,1)S(1)}, u32[]{:S(2)}, u32[]{:S(2)}) collective-permute-start(bf16[2,128,256]{2,1,0:T(8,128)(2,1)S(1)} %bitcast.17), channel_id=1, source_target_pairs={{0,32},{16,48},{32,0},{48,16},{1,33},{17,49},{33,1},{49,17},{2,34}... | collective-permute-start | bytes 393224 | tf_op jit(solution)/shard_map/ppermute | solution.py:238
  23.2 42.7 %collective-permute-start.11 = (bf16[8,128,256]{2,1,0:T(8,128)(2,1)}, bf16[8,128,256]{2,1,0:T(8,128)(2,1)}, u32[]{:S(2)}, u32[]{:S(2)}) collective-permute-start(bf16[8,128,256]{2,1,0:T(8,128)(2,1)} %get-tuple-element.24.refs_0_), channel_id=1, source_target_pairs={{0,16},{16,32},{32,48},{48,0},{1,17},{17,33},{33,49},{49,1},{2,18}... | collective-permute-start | bytes 1572872 | tf_op jit(solution)/shard_map/ppermute | solution.py:238
  23.8 44.8 %collective-permute-start.12 = (bf16[8,128,256]{2,1,0:T(8,128)(2,1)}, bf16[8,128,256]{2,1,0:T(8,128)(2,1)}, u32[]{:S(2)}, u32[]{:S(2)}) collective-permute-start(bf16[8,128,256]{2,1,0:T(8,128)(2,1)} %get-tuple-element.24.refs_0_), channel_id=1, source_target_pairs={{0,48},{16,0},{32,16},{48,32},{1,49},{17,1},{33,17},{49,33},{2,50}... | collective-permute-start | bytes 1572872 | tf_op jit(solution)/shard_map/ppermute | solution.py:238
  26.8 12.2 %all-to-all-start = ((bf16[16,16,512]{2,1,0:T(8,128)(2,1)}), bf16[16,16,512]{2,1,0:T(8,128)(2,1)S(1)}, u32[]{:S(2)}, u32[]{:S(2)}) async-start(bf16[16,16,512]{2,1,0:T(8,128)(2,1)} %bitcast.1), calls=%async_computation | async-start | bytes 524288 | tf_op jit(solution)/shard_map/all_to_all | solution.py:233
  31.6 66.8 %collective-permute-start.3 = (bf16[24,128,128]{2,1,0:T(8,128)(2,1)}, bf16[24,128,128]{2,1,0:T(8,128)(2,1)}, u32[]{:S(2)}, u32[]{:S(2)}) collective-permute-start(bf16[24,128,128]{2,1,0:T(8,128)(2,1)} %bitcast.4.tiles), channel_id=1, source_target_pairs={{0,8},{8,0},{1,9},{9,1},{2,10},{10,2},{3,11},{11,3},{4,12},{12,4},... | collective-permute-start | bytes 2359304 | tf_op jit(solution)/shard_map/ppermute | solution.py:229
  34.8 43.5 %collective-permute-start.13 = (bf16[8,128,256]{2,1,0:T(8,128)(2,1)}, bf16[8,128,256]{2,1,0:T(8,128)(2,1)}, u32[]{:S(2)}, u32[]{:S(2)}) collective-permute-start(bf16[8,128,256]{2,1,0:T(8,128)(2,1)} %get-tuple-element.24.refs_0_), channel_id=1, source_target_pairs={{0,32},{16,48},{32,0},{48,16},{1,33},{17,49},{33,1},{49,17},{2,34}... | collective-permute-start | bytes 1572872 | tf_op jit(solution)/shard_map/ppermute | solution.py:238
  39.6 29.3 %all-to-all-start.1 = ((bf16[8,16,512]{2,1,0:T(8,128)(2,1)}), bf16[8,16,512]{2,1,0:T(8,128)(2,1)S(1)}, u32[]{:S(2)}, u32[]{:S(2)}) async-start(bf16[8,16,512]{2,1,0:T(8,128)(2,1)} %shard_map.114), calls=%async_computation.1 | async-start | bytes 262144 | tf_op jit(solution)/shard_map/all_to_all | solution.py:233
  47.2 21.7 %copy-start.3 = (f32[512]{0:T(512)S(1)}, f32[512]{0:T(512)}, u32[]{:S(2)}) copy-start(f32[512]{0:T(512)} %param.18) | copy-start | bytes 6148
  50.7 15.2 %collective-permute-start.2 = (s32[2,24]{1,0:T(2,128)S(1)}, s32[2,24]{1,0:T(2,128)S(1)}, u32[]{:S(2)}, u32[]{:S(2)}) collective-permute-start(s32[2,24]{1,0:T(2,128)S(1)} %get-tuple-element.21.idx_own.idx), channel_id=1, source_target_pairs={{0,8},{8,0},{1,9},{9,1},{2,10},{10,2},{3,11},{11,3},{4,12},{12,4},... | collective-permute-start | bytes 584 | tf_op jit(solution)/shard_map/ppermute | solution.py:229
  65.9 32.6 %collective-permute-start.14 = (bf16[8,128,256]{2,1,0:T(8,128)(2,1)}, bf16[8,128,256]{2,1,0:T(8,128)(2,1)}, u32[]{:S(2)}, u32[]{:S(2)}) collective-permute-start(bf16[8,128,256]{2,1,0:T(8,128)(2,1)} %get-tuple-element.25.refs_4_), channel_id=1, source_target_pairs={{0,64},{64,128},{128,192},{192,0},{1,65},{65,129},{129,193},{193,1... | collective-permute-start | bytes 1572872 | tf_op jit(solution)/shard_map/ppermute | solution.py:238
  65.9 32.6 %collective-permute-start.15 = (bf16[8,128,256]{2,1,0:T(8,128)(2,1)}, bf16[8,128,256]{2,1,0:T(8,128)(2,1)}, u32[]{:S(2)}, u32[]{:S(2)}) collective-permute-start(bf16[8,128,256]{2,1,0:T(8,128)(2,1)} %get-tuple-element.25.refs_4_), channel_id=1, source_target_pairs={{0,192},{64,0},{128,64},{192,128},{1,193},{65,1},{129,65},{193,129... | collective-permute-start | bytes 1572872 | tf_op jit(solution)/shard_map/ppermute | solution.py:238
  68.6 29.9 %collective-permute-start.16 = (bf16[8,128,256]{2,1,0:T(8,128)(2,1)}, bf16[8,128,256]{2,1,0:T(8,128)(2,1)}, u32[]{:S(2)}, u32[]{:S(2)}) collective-permute-start(bf16[8,128,256]{2,1,0:T(8,128)(2,1)} %get-tuple-element.25.refs_4_), channel_id=1, source_target_pairs={{0,128},{64,192},{128,0},{192,64},{1,129},{65,193},{129,1},{193,65... | collective-permute-start | bytes 1572872 | tf_op jit(solution)/shard_map/ppermute | solution.py:238
  71.1 25.3 %all-to-all-start.2 = ((bf16[16,16,512]{2,1,0:T(8,128)(2,1)}), bf16[16,16,512]{2,1,0:T(8,128)(2,1)S(1)}, u32[]{:S(2)}, u32[]{:S(2)}) async-start(bf16[16,16,512]{2,1,0:T(8,128)(2,1)} %shard_map.116), calls=%async_computation.2 | async-start | bytes 524288 | tf_op jit(solution)/shard_map/all_to_all | solution.py:233
  96.4 8.2 %collective-permute-start.1 = (bf16[256,512]{1,0:T(8,128)(2,1)S(1)}, bf16[256,512]{1,0:T(8,128)(2,1)S(1)}, u32[]{:S(2)}, u32[]{:S(2)}) collective-permute-start(bf16[256,512]{1,0:T(8,128)(2,1)S(1)} %bitcast.9), channel_id=1, source_target_pairs={{0,8},{8,0},{1,9},{9,1},{2,10},{10,2},{3,11},{11,3},{4,12},{12,4},... | collective-permute-start | bytes 786440 | tf_op jit(solution)/shard_map/ppermute | solution.py:229
  102.6 1.9 %collective-permute-start.17 = (bf16[256,256]{1,0:T(8,128)(2,1)S(1)}, bf16[256,256]{1,0:T(8,128)(2,1)S(1)}, u32[]{:S(2)}, u32[]{:S(2)}) collective-permute-start(bf16[256,256]{1,0:T(8,128)(2,1)S(1)} %get-tuple-element.27), channel_id=1, source_target_pairs={{0,8},{8,0},{1,9},{9,1},{2,10},{10,2},{3,11},{11,3},{4,12},{12,4},... | collective-permute-start | bytes 393224 | tf_op jit(solution)/shard_map/ppermute | solution.py:229
  (3 other events, 8.0 us)

commit v7 on v5

--- a/solution.py
+++ b/solution.py
@@ -83,27 +83,38 @@
 
 
 def join_kernel(*refs):
-    pieces, (low, high, sems) = refs[:-3], refs[-3:]
-    half = len(pieces) // 2
-    copies = []
-    for n, piece in enumerate(pieces):
-        out = low if n < half else high
-        size = piece.shape[0]
-        cp = pltpu.make_async_copy(piece, out.at[pl.ds((n % half) * size, size)], sems.at[n])
-        cp.start()
-        copies.append(cp)
-    for cp in copies:
-        cp.wait()
+    n = len(refs) - 4
+    pieces, outs, (held, sems) = refs[:n], refs[n : n + 2], refs[n + 2 :]
+    half = n // 2
+    size = pieces[0].shape[0]
+
+    def fetch(i):
+        return pltpu.make_async_copy(pieces[i], held.at[i], sems.at[0, i])
+
+    def store(i):
+        return pltpu.make_async_copy(held.at[i], outs[i // half].at[pl.ds((i % half) * size, size)], sems.at[1, i])
+
+    for i in range(n):
+        fetch(i).start()
+    for i in range(n):
+        fetch(i).wait()
+        store(i).start()
+    for i in range(n):
+        store(i).wait()
 
 
 def join(a, b):
-    shape = jax.ShapeDtypeStruct((len(a) * a[0].shape[0],) + a[0].shape[1:], a[0].dtype)
     pieces = a + b
+    shape = pltpu.HBM((len(a) * a[0].shape[0],) + a[0].shape[1:], a[0].dtype)
     return call(
         join_kernel,
         (shape, shape),
         [pl.BlockSpec(memory_space=pl.ANY)] * len(pieces),
-        scratch=[pltpu.SemaphoreType.DMA((len(pieces),))],
+        out=(hspec(), hspec()),
+        scratch=[
+            pltpu.VMEM((len(pieces),) + a[0].shape, a[0].dtype),
+            pltpu.SemaphoreType.DMA((2, len(pieces))),
+        ],
         flops=0,
     )(*pieces)
 
@@ -113,7 +124,7 @@
     out_ref[...] = jnp.broadcast_to(total.astype(BF16)[None], out_ref.shape)
 
 
-def chain_kernel(summ_ref, w_in_ref, w_ref, offset_ref, start_hbm, out_ref, side_ref, startt_ref, start_ref, sem):
+def chain_kernel(summ_ref, w_in_ref, w_ref, offset_ref, start_hbm, out_ref, side_ref, startt_ref, start_ref, wt_ref, sem):
     n_t, cols, width = summ_ref.shape
     x, y, core, last = place()
     col0 = core * (width // C) + (x * Y + y) * cols
@@ -126,15 +137,17 @@
         if g == 0:
             side = side - offset_ref[...]
         side_ref[g] = side.reshape(n_t, cols, width)
+    for g in range(3):
+        wt_ref[g] = w_ref[g].T
     fetch.wait()
     startt_ref[...] = start_ref[...].T
     state = startt_ref[pl.ds(pl.multiple_of(lax.rem(col0, BLOCK), cols), cols), :]
 
     def step(t, state):
         state_b = state.astype(BF16)
-        update = jax.nn.sigmoid(side_ref[0, t] + mm(state_b, w_ref[0], NT))
-        reset = jax.nn.sigmoid(side_ref[1, t] + mm(state_b, w_ref[1], NT))
-        cand = jnp.tanh(side_ref[2, t] + mm((reset * state).astype(BF16), w_ref[2], NT))
+        reset = jax.nn.sigmoid(side_ref[1, t] + mm(state_b, wt_ref[1], NN))
+        update = jax.nn.sigmoid(side_ref[0, t] + mm(state_b, wt_ref[0], NN))
+        cand = jnp.tanh(side_ref[2, t] + mm((reset * state).astype(BF16), wt_ref[2], NN))
         return (1.0 - update) * state + update * cand
 
     state = lax.fori_loop(0, last + 1, step, state)
@@ -155,8 +168,12 @@
     return jnp.where(step == 0, 0, jnp.where(step == 3, 1, step + 1))
 
 
-def agg_oth_kernel(cols_own, cols_oth, rows_oth, used_oth, tiles, feat, *refs):
-    pieces, (agg, rhs_own, blocks, rhs, lhs, sems) = refs[:-6], refs[-6:]
+def agg_oth_kernel(cols_own, cols_oth, rows_oth, used_oth, tiles_any, feat_any, *refs):
+    pieces, (agg, rhs_own, tiles, feat, blocks, rhs, lhs, sems) = refs[:-8], refs[-8:]
+    tile_copy = pltpu.make_async_copy(tiles_any, tiles, sems.at[len(pieces)])
+    tile_copy.start()
+    feat_copy = pltpu.make_async_copy(feat_any, feat, sems.at[len(pieces) + 1])
+    feat_copy.start()
     copies = []
     first = 0
     for n, piece in enumerate(pieces):
@@ -164,7 +181,9 @@
         cp.start()
         copies.append(cp)
         first += piece.shape[0]
+    tile_copy.wait()
     masked(rows_oth, used_oth, tiles, lhs)
+    feat_copy.wait()
     for cp in copies:
         cp.wait()
     x, y, core, _ = place()
@@ -263,6 +282,7 @@
     blocks_b = spread(feat_oth.reshape(four), "y")
     joined_a, joined_b = join(blocks_a, blocks_b)
     gathered = spread(joined_a, "y") + spread(joined_b, "x")
+    gathered = [in_hbm(piece) if piece is joined_a or piece is joined_b else piece for piece in gathered]
 
     rows_oth, cols_oth, used_oth = swap(tile_rows), swap(tile_cols), swap(tile_used)
     tiles_own = tile_vals[0]
@@ -272,12 +292,14 @@
     agg_give, rhs_own = call(
         agg_oth_kernel,
         (feat_half, jax.ShapeDtypeStruct((depth, half), BF16)),
-        [sspec()] * 4 + [vspec()] * 2 + [pl.BlockSpec(memory_space=pl.ANY)] * len(gathered),
+        [sspec()] * 4 + [pl.BlockSpec(memory_space=pl.ANY)] * (len(gathered) + 2),
         scratch=[
+            pltpu.VMEM(tiles_oth.shape, BF16),
+            pltpu.VMEM(feat_oth.shape, BF16),
             pltpu.VMEM((CHIPS * C * blocks_dev, BLOCK, half), BF16),
             pltpu.VMEM((depth, half), BF16),
             lhs,
-            pltpu.SemaphoreType.DMA((len(gathered),)),
+            pltpu.SemaphoreType.DMA((len(gathered) + 2,)),
         ],
         vmem_mib=16,
     )(tile_cols, cols_oth, rows_oth, used_oth, tiles_oth, feat_oth, *gathered)
@@ -294,6 +316,7 @@
             pltpu.VMEM((3, n_tm, cols, width), F32),
             pltpu.VMEM((BLOCK, width), F32),
             pltpu.VMEM((width, BLOCK), F32),
+            pltpu.VMEM(w_state.shape, BF16),
             pltpu.SemaphoreType.DMA(()),
         ],
         vmem_mib=8,

time: 108 us -> 106 us (0.981)
  local copies, waits for them, and re-layouts: 2.75 us -> 0.93 us
    unnamed x20 -> x16, local copies, waits for them, and re-layouts: 2.75 us -> 0.93 us
where the time goes in v7:
time: 106 us
  starting transfers between devices  46.6 us (44%)
  waiting for transfers between devices  40.7 us (38%)
  Pallas kernels  15.4 us (15%)
  between operations  1.45 us (1%)
    all_to_all x3, waiting for transfers between devices, trade(): return lax.all_to_all(x, axes, split_axis=0, concat_axis=0, tiled=True)  33.6 us
    all_to_all x3, starting transfers between devices, trade(): return lax.all_to_all(x, axes, split_axis=0, concat_axis=0, tiled=True)  19.3 us
    ppermute x12, starting transfers between devices, shift(): lax.ppermute(x, axis, [(i, (i + distance) % size) for i in range(size)])  17.1 us
    ppermute x8, starting transfers between devices, swap(): return lax.ppermute(x, 'c', [(0, 1), (1, 0)])  10.1 us
    pallas_call x1, Pallas kernels, layer(): call(agg_oth_kernel, (feat_half, jax.ShapeDtypeStruct((depth, half), BF16...  4.46 us
    ppermute x12, waiting for transfers between devices, shift(): lax.ppermute(x, axis, [(i, (i + distance) % size) for i in range(size)])  4.44 us
    pallas_call x1, Pallas kernels, layer(): call(chain_kernel, jax.ShapeDtypeStruct((CHIPS, cols, width), BF16), [vsp...  2.76 us
    ppermute x8, waiting for transfers between devices, swap(): return lax.ppermute(x, 'c', [(0, 1), (1, 0)])  2.65 us
  transfers between devices with their start and end apart: 23, of which 10 were waited for; matrix products, arithmetic and copies ran while one was open for 1% of the time, Pallas kernels for 11%

profile of v7, /device:TPU:1, one launch (start us, length us, event | category | flops | bytes accessed | tf_op | source)
XLA Modules:
  0.0 105.9 jit_solution(12800621446779405756)
XLA Ops:
  0.6 2.4 %shard_map.113 = (bf16[256,512]{1,0:T(8,128)(2,1)S(1)}, f32[256,512]{1,0:T(8,128)S(1)}, bf16[256,256]{1,0:T(8,128)(2,1)}, bf16[256,256]{1,0:T(8,128)(2,1)S(1)}) custom-call(bf16[256,512]{1,0:T(8,128)(2,1)} %bitcast.23, bf16[512,512]{1,0:T(8,128)(2,1)} %pool_hbm.1), custom_call_target="tpu_custom_call" | custom-call | flops 100000000 | bytes 1000000 | tf_op jit(solution)/shard_map/pallas_call | solution.py:259
  3.1 3.3 %collective-permute-start.6 = (bf16[256,256]{1,0:T(8,128)(2,1)S(1)}, bf16[256,256]{1,0:T(8,128)(2,1)S(1)}, u32[]{:S(2)}, u32[]{:S(2)}) collective-permute-start(bf16[256,256]{1,0:T(8,128)(2,1)S(1)} %get-tuple-element.15), channel_id=1, source_target_pairs={{0,8},{8,0},{1,9},{9,1},{2,10},{10,2},{3,11},{11,3},{4,12},{12,4},... | collective-permute-start | bytes 393224 | tf_op jit(solution)/shard_map/ppermute | solution.py:222
  6.4 1.0 collective-permute-start.9
  9.6 3.0 %collective-permute-start.12 = (bf16[2,128,256]{2,1,0:T(8,128)(2,1)S(1)}, bf16[2,128,256]{2,1,0:T(8,128)(2,1)S(1)}, u32[]{:S(2)}, u32[]{:S(2)}) collective-permute-start(bf16[2,128,256]{2,1,0:T(8,128)(2,1)S(1)} %bitcast.17), channel_id=1, source_target_pairs={{0,32},{16,48},{32,0},{48,16},{1,33},{17,49},{33,1},{49,17},{2,34}... | collective-permute-start | bytes 393224 | tf_op jit(solution)/shard_map/ppermute | solution.py:231
  14.2 1.3 %collective-permute-start.10 = (bf16[2,128,256]{2,1,0:T(8,128)(2,1)S(1)}, bf16[2,128,256]{2,1,0:T(8,128)(2,1)S(1)}, u32[]{:S(2)}, u32[]{:S(2)}) collective-permute-start(bf16[2,128,256]{2,1,0:T(8,128)(2,1)S(1)} %bitcast.19), channel_id=1, source_target_pairs={{0,16},{16,32},{32,48},{48,0},{1,17},{17,33},{33,49},{49,1},{2,18}... | collective-permute-start | bytes 393224 | tf_op jit(solution)/shard_map/ppermute | solution.py:231
  16.2 2.9 %collective-permute-done.11.refs_6_ = bf16[2,128,256]{2,1,0:T(8,128)(2,1)S(1)} collective-permute-done((bf16[2,128,256]{2,1,0:T(8,128)(2,1)S(1)}, bf16[2,128,256]{2,1,0:T(8,128)(2,1)S(1)}, u32[]{:S(2)}, u32[]{:S(2)}) %collective-permute-start.11) | collective-permute-done | bytes 131104 | tf_op jit(solution)/shard_map/ppermute | solution.py:231
  20.2 2.4 %shard_map.116 = (bf16[8,128,256]{2,1,0:T(8,128)(2,1)}, bf16[8,128,256]{2,1,0:T(8,128)(2,1)}) custom-call(bf16[2,128,256]{2,1,0:T(8,128)(2,1)S(1)} %bitcast.16, bf16[2,128,256]{2,1,0:T(8,128)(2,1)S(1)} %collective-permute-done.7.refs_1_, bf16[2,128,256]{2,1,0:T(8,128)(2,1)S(1)} %collective-permute-done.8.refs_2_, ...), custom_call_target="tpu_custom_call" | custom-call | bytes 1000000 | tf_op jit(solution)/shard_map/pallas_call | solution.py:109
  22.6 2.0 %collective-permute-start.15 = (bf16[8,128,256]{2,1,0:T(8,128)(2,1)}, bf16[8,128,256]{2,1,0:T(8,128)(2,1)}, u32[]{:S(2)}, u32[]{:S(2)}) collective-permute-start(bf16[8,128,256]{2,1,0:T(8,128)(2,1)} %get-tuple-element.16.refs_0_), channel_id=1, source_target_pairs={{0,32},{16,48},{32,0},{48,16},{1,33},{17,49},{33,1},{49,17},{2,34}... | collective-permute-start | bytes 1572872 | tf_op jit(solution)/shard_map/ppermute | solution.py:231
  24.6 1.8 %collective-permute-start.14 = (bf16[8,128,256]{2,1,0:T(8,128)(2,1)}, bf16[8,128,256]{2,1,0:T(8,128)(2,1)}, u32[]{:S(2)}, u32[]{:S(2)}) collective-permute-start(bf16[8,128,256]{2,1,0:T(8,128)(2,1)} %get-tuple-element.16.refs_0_), channel_id=1, source_target_pairs={{0,48},{16,0},{32,16},{48,32},{1,49},{17,1},{33,17},{49,33},{2,50}... | collective-permute-start | bytes 1572872 | tf_op jit(solution)/shard_map/ppermute | solution.py:231
  27.2 4.8 %all-to-all-start = ((bf16[16,16,512]{2,1,0:T(8,128)(2,1)}), bf16[16,16,512]{2,1,0:T(8,128)(2,1)S(1)}, u32[]{:S(2)}, u32[]{:S(2)}) async-start(bf16[16,16,512]{2,1,0:T(8,128)(2,1)} %bitcast.22), calls=%async_computation | async-start | bytes 524288 | tf_op jit(solution)/shard_map/all_to_all | solution.py:226
  32.0 2.3 %collective-permute-start.5 = (bf16[24,128,128]{2,1,0:T(8,128)(2,1)}, bf16[24,128,128]{2,1,0:T(8,128)(2,1)}, u32[]{:S(2)}, u32[]{:S(2)}) collective-permute-start(bf16[24,128,128]{2,1,0:T(8,128)(2,1)} %bitcast.11), channel_id=1, source_target_pairs={{0,8},{8,0},{1,9},{9,1},{2,10},{10,2},{3,11},{11,3},{4,12},{12,4},... | collective-permute-start | bytes 2359304 | tf_op jit(solution)/shard_map/ppermute | solution.py:222
  34.3 1.6 %collective-permute-start.13 = (bf16[8,128,256]{2,1,0:T(8,128)(2,1)}, bf16[8,128,256]{2,1,0:T(8,128)(2,1)}, u32[]{:S(2)}, u32[]{:S(2)}) collective-permute-start(bf16[8,128,256]{2,1,0:T(8,128)(2,1)} %get-tuple-element.16.refs_0_), channel_id=1, source_target_pairs={{0,16},{16,32},{32,48},{48,0},{1,17},{17,33},{33,49},{49,1},{2,18}... | collective-permute-start | bytes 1572872 | tf_op jit(solution)/shard_map/ppermute | solution.py:231
  35.9 15.3 %all-to-all-done.parts_ref = bf16[16,16,512]{2,1,0:T(8,128)(2,1)S(1)} async-done(((bf16[16,16,512]{2,1,0:T(8,128)(2,1)}), bf16[16,16,512]{2,1,0:T(8,128)(2,1)S(1)}, u32[]{:S(2)}, u32[]{:S(2)}) %all-to-all-start) | async-done | bytes 262176 | tf_op jit(solution)/shard_map/all_to_all | solution.py:226
  51.8 8.2 %all-to-all-start.1 = ((bf16[8,16,512]{2,1,0:T(8,128)(2,1)}), bf16[8,16,512]{2,1,0:T(8,128)(2,1)S(1)}, u32[]{:S(2)}, u32[]{:S(2)}) async-start(bf16[8,16,512]{2,1,0:T(8,128)(2,1)} %shard_map.114), calls=%async_computation.1 | async-start | bytes 262144 | tf_op jit(solution)/shard_map/all_to_all | solution.py:226
  60.0 1.8 %collective-permute-start.4 = (s32[1,1]{1,0:T(1,128)}, s32[1,1]{1,0:T(1,128)}, u32[]{:S(2)}, u32[]{:S(2)}) collective-permute-start(s32[1,1]{1,0:T(1,128)} %param.14), channel_id=1, source_target_pairs={{0,8},{8,0},{1,9},{9,1},{2,10},{10,2},{3,11},{11,3},{4,12},{12,4},... | collective-permute-start | bytes 20 | tf_op jit(solution)/shard_map/ppermute | solution.py:222
  65.1 1.1 %collective-permute-start.18 = (bf16[8,128,256]{2,1,0:T(8,128)(2,1)}, bf16[8,128,256]{2,1,0:T(8,128)(2,1)}, u32[]{:S(2)}, u32[]{:S(2)}) collective-permute-start(bf16[8,128,256]{2,1,0:T(8,128)(2,1)} %get-tuple-element.17.refs_4_), channel_id=1, source_target_pairs={{0,128},{64,192},{128,0},{192,64},{1,129},{65,193},{129,1},{193,65... | collective-permute-start | bytes 1572872 | tf_op jit(solution)/shard_map/ppermute | solution.py:231
  66.3 2.8 %collective-permute-start.17 = (bf16[8,128,256]{2,1,0:T(8,128)(2,1)}, bf16[8,128,256]{2,1,0:T(8,128)(2,1)}, u32[]{:S(2)}, u32[]{:S(2)}) collective-permute-start(bf16[8,128,256]{2,1,0:T(8,128)(2,1)} %get-tuple-element.17.refs_4_), channel_id=1, source_target_pairs={{0,192},{64,0},{128,64},{192,128},{1,193},{65,1},{129,65},{193,129... | collective-permute-start | bytes 1572872 | tf_op jit(solution)/shard_map/ppermute | solution.py:231
  69.1 2.8 %shard_map.115 = bf16[16,16,512]{2,1,0:T(8,128)(2,1)} custom-call(bf16[8,16,512]{2,1,0:T(8,128)(2,1)S(1)} %all-to-all-done.1.summ_ref, bf16[3,512,512]{2,1,0:T(8,128)(2,1)S(1)} %copy-done, bf16[3,512,512]{2,1,0:T(8,128)(2,1)S(1)} %copy-done.1, f32[1,512]{1,0:T(1,128)S(1)} %bitcast.21, f32[512,512]{1,0:T(8,128)} %start_hbm.1), custom_call_target="tpu_custom_call" | custom-call | flops 100000000 | bytes 1000000 | tf_op jit(solution)/shard_map/pallas_call | solution.py:311
  71.8 6.3 %all-to-all-start.2 = ((bf16[16,16,512]{2,1,0:T(8,128)(2,1)}), bf16[16,16,512]{2,1,0:T(8,128)(2,1)S(1)}, u32[]{:S(2)}, u32[]{:S(2)}) async-start(bf16[16,16,512]{2,1,0:T(8,128)(2,1)} %shard_map.115), calls=%async_computation.2 | async-start | bytes 524288 | tf_op jit(solution)/shard_map/all_to_all | solution.py:226
  78.2 18.4 %all-to-all-done.2 = bf16[16,16,512]{2,1,0:T(8,128)(2,1)S(1)} async-done(((bf16[16,16,512]{2,1,0:T(8,128)(2,1)}), bf16[16,16,512]{2,1,0:T(8,128)(2,1)S(1)}, u32[]{:S(2)}, u32[]{:S(2)}) %all-to-all-start.2) | async-done | bytes 262176 | tf_op jit(solution)/shard_map/all_to_all | solution.py:226
  96.6 1.3 %collective-permute-start.1 = (bf16[256,512]{1,0:T(8,128)(2,1)S(1)}, bf16[256,512]{1,0:T(8,128)(2,1)S(1)}, u32[]{:S(2)}, u32[]{:S(2)}) collective-permute-start(bf16[256,512]{1,0:T(8,128)(2,1)S(1)} %bitcast.9), channel_id=1, source_target_pairs={{0,8},{8,0},{1,9},{9,1},{2,10},{10,2},{3,11},{11,3},{4,12},{12,4},... | collective-permute-start | bytes 786440 | tf_op jit(solution)/shard_map/ppermute | solution.py:222
  97.9 4.5 %shard_map.117 = (bf16[256,256]{1,0:T(8,128)(2,1)S(1)}, bf16[3072,256]{1,0:T(8,128)(2,1)S(1)}) custom-call(s32[1,24]{1,0:T(1,128)S(1)} %copy-done.6, s32[1,24]{1,0:T(1,128)S(1)} %collective-permute-done.2.cols_oth, s32[1,24]{1,0:T(1,128)S(1)} %collective-permute-done.3.rows_oth, s32[1,1]{1,0:T(1,128)} %collective-permute-done.4.used_oth, ...), custom_call_target="tpu_custom_call" | custom-call | flops 100000000 | bytes 1000000 | tf_op jit(solution)/shard_map/pallas_call | solution.py:292
  103.2 1.2 %shard_map.118.agg_own = bf16[256,256]{1,0:T(8,128)(2,1)S(1)} custom-call(s32[1,24]{1,0:T(1,128)S(1)} %copy-done.7, s32[1,1]{1,0:T(1,128)S(6)} %copy.12.used, bf16[24,128,128]{2,1,0:T(8,128)(2,1)S(1)} %bitcast.12, bf16[256,256]{1,0:T(8,128)(2,1)S(1)} %copy-done.4, bf16[3072,256]{1,0:T(8,128)(2,1)S(1)} %get-tuple-element.18.rhs), custom_call_target="tpu_custom_call" | custom-call | flops 100000000 | bytes 1000000 | tf_op jit(solution)/shard_map/pallas_call | solution.py:307
  104.5 1.5 %shard_map.119 = (bf16[256,512]{1,0:T(8,128)(2,1)}, f32[512,512]{1,0:T(8,128)}) custom-call(bf16[256,512]{1,0:T(8,128)(2,1)S(1)} %bitcast.10, bf16[256,512]{1,0:T(8,128)(2,1)S(1)} %collective-permute-done.1.wt_oth, bf16[256,256]{1,0:T(8,128)(2,1)S(1)} %shard_map.118.agg_own, bf16[256,256]{1,0:T(8,128)(2,1)S(1)} %collective-permute-done.19.agg_oth), custom_call_target="tpu_custom_call" | custom-call | flops 100000000 | bytes 1000000 | tf_op jit(solution)/shard_map/pallas_call | solution.py:326
  (46 shorter events, 10.6 us)
Async XLA Ops:
  3.1 6.4 %collective-permute-start.6 = (bf16[256,256]{1,0:T(8,128)(2,1)S(1)}, bf16[256,256]{1,0:T(8,128)(2,1)S(1)}, u32[]{:S(2)}, u32[]{:S(2)}) collective-permute-start(bf16[256,256]{1,0:T(8,128)(2,1)S(1)} %get-tuple-element.15), channel_id=1, source_target_pairs={{0,8},{8,0},{1,9},{9,1},{2,10},{10,2},{3,11},{11,3},{4,12},{12,4},... | collective-permute-start | bytes 393224 | tf_op jit(solution)/shard_map/ppermute | solution.py:222
  6.4 6.7 %collective-permute-start.9 = (bf16[2,128,256]{2,1,0:T(8,128)(2,1)}, bf16[2,128,256]{2,1,0:T(8,128)(2,1)S(1)}, u32[]{:S(2)}, u32[]{:S(2)}) collective-permute-start(bf16[2,128,256]{2,1,0:T(8,128)(2,1)} %bitcast.13), channel_id=1, source_target_pairs={{0,128},{64,192},{128,0},{192,64},{1,129},{65,193},{129,1},{193,65... | collective-permute-start | bytes 393224 | tf_op jit(solution)/shard_map/ppermute | solution.py:231
  7.4 6.8 %collective-permute-start.8 = (bf16[2,128,256]{2,1,0:T(8,128)(2,1)}, bf16[2,128,256]{2,1,0:T(8,128)(2,1)S(1)}, u32[]{:S(2)}, u32[]{:S(2)}) collective-permute-start(bf16[2,128,256]{2,1,0:T(8,128)(2,1)} %bitcast.14), channel_id=1, source_target_pairs={{0,192},{64,0},{128,64},{192,128},{1,193},{65,1},{129,65},{193,129... | collective-permute-start | bytes 393224 | tf_op jit(solution)/shard_map/ppermute | solution.py:231
  8.3 60.8 %copy-start.5 = (f32[512]{0:T(512)S(1)}, f32[512]{0:T(512)}, u32[]{:S(2)}) copy-start(f32[512]{0:T(512)} %param.18) | copy-start | bytes 6148
  8.3 18.2 %collective-permute-start = (bf16[256,512]{1,0:T(8,128)(2,1)S(1)}, bf16[256,512]{1,0:T(8,128)(2,1)S(1)}, u32[]{:S(2)}, u32[]{:S(2)}) collective-permute-start(bf16[256,512]{1,0:T(8,128)(2,1)S(1)} %get-tuple-element.13), channel_id=1, source_target_pairs={{0,8},{8,0},{1,9},{9,1},{2,10},{10,2},{3,11},{11,3},{4,12},{12,4},... | collective-permute-start | bytes 786440 | tf_op jit(solution)/shard_map/ppermute | solution.py:222
  8.9 7.3 %collective-permute-start.7 = (bf16[2,128,256]{2,1,0:T(8,128)(2,1)}, bf16[2,128,256]{2,1,0:T(8,128)(2,1)S(1)}, u32[]{:S(2)}, u32[]{:S(2)}) collective-permute-start(bf16[2,128,256]{2,1,0:T(8,128)(2,1)} %bitcast.15), channel_id=1, source_target_pairs={{0,64},{64,128},{128,192},{192,0},{1,65},{65,129},{129,193},{193,1... | collective-permute-start | bytes 393224 | tf_op jit(solution)/shard_map/ppermute | solution.py:231
  9.6 6.6 %collective-permute-start.12 = (bf16[2,128,256]{2,1,0:T(8,128)(2,1)S(1)}, bf16[2,128,256]{2,1,0:T(8,128)(2,1)S(1)}, u32[]{:S(2)}, u32[]{:S(2)}) collective-permute-start(bf16[2,128,256]{2,1,0:T(8,128)(2,1)S(1)} %bitcast.17), channel_id=1, source_target_pairs={{0,32},{16,48},{32,0},{48,16},{1,33},{17,49},{33,1},{49,17},{2,34}... | collective-permute-start | bytes 393224 | tf_op jit(solution)/shard_map/ppermute | solution.py:231
  13.0 6.0 %collective-permute-start.11 = (bf16[2,128,256]{2,1,0:T(8,128)(2,1)S(1)}, bf16[2,128,256]{2,1,0:T(8,128)(2,1)S(1)}, u32[]{:S(2)}, u32[]{:S(2)}) collective-permute-start(bf16[2,128,256]{2,1,0:T(8,128)(2,1)S(1)} %bitcast.18), channel_id=1, source_target_pairs={{0,48},{16,0},{32,16},{48,32},{1,49},{17,1},{33,17},{49,33},{2,50}... | collective-permute-start | bytes 393224 | tf_op jit(solution)/shard_map/ppermute | solution.py:231
  14.2 5.1 %collective-permute-start.10 = (bf16[2,128,256]{2,1,0:T(8,128)(2,1)S(1)}, bf16[2,128,256]{2,1,0:T(8,128)(2,1)S(1)}, u32[]{:S(2)}, u32[]{:S(2)}) collective-permute-start(bf16[2,128,256]{2,1,0:T(8,128)(2,1)S(1)} %bitcast.19), channel_id=1, source_target_pairs={{0,16},{16,32},{32,48},{48,0},{1,17},{17,33},{33,49},{49,1},{2,18}... | collective-permute-start | bytes 393224 | tf_op jit(solution)/shard_map/ppermute | solution.py:231
  22.6 43.6 %collective-permute-start.15 = (bf16[8,128,256]{2,1,0:T(8,128)(2,1)}, bf16[8,128,256]{2,1,0:T(8,128)(2,1)}, u32[]{:S(2)}, u32[]{:S(2)}) collective-permute-start(bf16[8,128,256]{2,1,0:T(8,128)(2,1)} %get-tuple-element.16.refs_0_), channel_id=1, source_target_pairs={{0,32},{16,48},{32,0},{48,16},{1,33},{17,49},{33,1},{49,17},{2,34}... | collective-permute-start | bytes 1572872 | tf_op jit(solution)/shard_map/ppermute | solution.py:231
  24.6 44.4 %collective-permute-start.14 = (bf16[8,128,256]{2,1,0:T(8,128)(2,1)}, bf16[8,128,256]{2,1,0:T(8,128)(2,1)}, u32[]{:S(2)}, u32[]{:S(2)}) collective-permute-start(bf16[8,128,256]{2,1,0:T(8,128)(2,1)} %get-tuple-element.16.refs_0_), channel_id=1, source_target_pairs={{0,48},{16,0},{32,16},{48,32},{1,49},{17,1},{33,17},{49,33},{2,50}... | collective-permute-start | bytes 1572872 | tf_op jit(solution)/shard_map/ppermute | solution.py:231
  27.2 23.9 %all-to-all-start = ((bf16[16,16,512]{2,1,0:T(8,128)(2,1)}), bf16[16,16,512]{2,1,0:T(8,128)(2,1)S(1)}, u32[]{:S(2)}, u32[]{:S(2)}) async-start(bf16[16,16,512]{2,1,0:T(8,128)(2,1)} %bitcast.22), calls=%async_computation | async-start | bytes 524288 | tf_op jit(solution)/shard_map/all_to_all | solution.py:226
  32.0 65.8 %collective-permute-start.5 = (bf16[24,128,128]{2,1,0:T(8,128)(2,1)}, bf16[24,128,128]{2,1,0:T(8,128)(2,1)}, u32[]{:S(2)}, u32[]{:S(2)}) collective-permute-start(bf16[24,128,128]{2,1,0:T(8,128)(2,1)} %bitcast.11), channel_id=1, source_target_pairs={{0,8},{8,0},{1,9},{9,1},{2,10},{10,2},{3,11},{11,3},{4,12},{12,4},... | collective-permute-start | bytes 2359304 | tf_op jit(solution)/shard_map/ppermute | solution.py:222
  34.3 43.9 %collective-permute-start.13 = (bf16[8,128,256]{2,1,0:T(8,128)(2,1)}, bf16[8,128,256]{2,1,0:T(8,128)(2,1)}, u32[]{:S(2)}, u32[]{:S(2)}) collective-permute-start(bf16[8,128,256]{2,1,0:T(8,128)(2,1)} %get-tuple-element.16.refs_0_), channel_id=1, source_target_pairs={{0,16},{16,32},{32,48},{48,0},{1,17},{17,33},{33,49},{49,1},{2,18}... | collective-permute-start | bytes 1572872 | tf_op jit(solution)/shard_map/ppermute | solution.py:231
  51.8 17.2 %all-to-all-start.1 = ((bf16[8,16,512]{2,1,0:T(8,128)(2,1)}), bf16[8,16,512]{2,1,0:T(8,128)(2,1)S(1)}, u32[]{:S(2)}, u32[]{:S(2)}) async-start(bf16[8,16,512]{2,1,0:T(8,128)(2,1)} %shard_map.114), calls=%async_computation.1 | async-start | bytes 262144 | tf_op jit(solution)/shard_map/all_to_all | solution.py:226
  60.0 2.8 %collective-permute-start.4 = (s32[1,1]{1,0:T(1,128)}, s32[1,1]{1,0:T(1,128)}, u32[]{:S(2)}, u32[]{:S(2)}) collective-permute-start(s32[1,1]{1,0:T(1,128)} %param.14), channel_id=1, source_target_pairs={{0,8},{8,0},{1,9},{9,1},{2,10},{10,2},{3,11},{11,3},{4,12},{12,4},... | collective-permute-start | bytes 20 | tf_op jit(solution)/shard_map/ppermute | solution.py:222
  62.8 1.2 %collective-permute-start.3 = (s32[1,24]{1,0:T(1,128)S(1)}, s32[1,24]{1,0:T(1,128)S(1)}, u32[]{:S(2)}, u32[]{:S(2)}) collective-permute-start(s32[1,24]{1,0:T(1,128)S(1)} %copy-done.7), channel_id=1, source_target_pairs={{0,8},{8,0},{1,9},{9,1},{2,10},{10,2},{3,11},{11,3},{4,12},{12,4},... | collective-permute-start | bytes 296 | tf_op jit(solution)/shard_map/ppermute | solution.py:222
  64.0 1.2 %collective-permute-start.2 = (s32[1,24]{1,0:T(1,128)S(1)}, s32[1,24]{1,0:T(1,128)S(1)}, u32[]{:S(2)}, u32[]{:S(2)}) collective-permute-start(s32[1,24]{1,0:T(1,128)S(1)} %copy-done.6), channel_id=1, source_target_pairs={{0,8},{8,0},{1,9},{9,1},{2,10},{10,2},{3,11},{11,3},{4,12},{12,4},... | collective-permute-start | bytes 296 | tf_op jit(solution)/shard_map/ppermute | solution.py:222
  65.1 32.7 %collective-permute-start.18 = (bf16[8,128,256]{2,1,0:T(8,128)(2,1)}, bf16[8,128,256]{2,1,0:T(8,128)(2,1)}, u32[]{:S(2)}, u32[]{:S(2)}) collective-permute-start(bf16[8,128,256]{2,1,0:T(8,128)(2,1)} %get-tuple-element.17.refs_4_), channel_id=1, source_target_pairs={{0,128},{64,192},{128,0},{192,64},{1,129},{65,193},{129,1},{193,65... | collective-permute-start | bytes 1572872 | tf_op jit(solution)/shard_map/ppermute | solution.py:231
  66.3 31.6 %collective-permute-start.17 = (bf16[8,128,256]{2,1,0:T(8,128)(2,1)}, bf16[8,128,256]{2,1,0:T(8,128)(2,1)}, u32[]{:S(2)}, u32[]{:S(2)}) collective-permute-start(bf16[8,128,256]{2,1,0:T(8,128)(2,1)} %get-tuple-element.17.refs_4_), channel_id=1, source_target_pairs={{0,192},{64,0},{128,64},{192,128},{1,193},{65,1},{129,65},{193,129... | collective-permute-start | bytes 1572872 | tf_op jit(solution)/shard_map/ppermute | solution.py:231
  69.0 28.8 %collective-permute-start.16 = (bf16[8,128,256]{2,1,0:T(8,128)(2,1)}, bf16[8,128,256]{2,1,0:T(8,128)(2,1)}, u32[]{:S(2)}, u32[]{:S(2)}) collective-permute-start(bf16[8,128,256]{2,1,0:T(8,128)(2,1)} %get-tuple-element.17.refs_4_), channel_id=1, source_target_pairs={{0,64},{64,128},{128,192},{192,0},{1,65},{65,129},{129,193},{193,1... | collective-permute-start | bytes 1572872 | tf_op jit(solution)/shard_map/ppermute | solution.py:231
  71.8 24.7 %all-to-all-start.2 = ((bf16[16,16,512]{2,1,0:T(8,128)(2,1)}), bf16[16,16,512]{2,1,0:T(8,128)(2,1)S(1)}, u32[]{:S(2)}, u32[]{:S(2)}) async-start(bf16[16,16,512]{2,1,0:T(8,128)(2,1)} %shard_map.115), calls=%async_computation.2 | async-start | bytes 524288 | tf_op jit(solution)/shard_map/all_to_all | solution.py:226
  96.6 7.9 %collective-permute-start.1 = (bf16[256,512]{1,0:T(8,128)(2,1)S(1)}, bf16[256,512]{1,0:T(8,128)(2,1)S(1)}, u32[]{:S(2)}, u32[]{:S(2)}) collective-permute-start(bf16[256,512]{1,0:T(8,128)(2,1)S(1)} %bitcast.9), channel_id=1, source_target_pairs={{0,8},{8,0},{1,9},{9,1},{2,10},{10,2},{3,11},{11,3},{4,12},{12,4},... | collective-permute-start | bytes 786440 | tf_op jit(solution)/shard_map/ppermute | solution.py:222
  102.4 2.1 %collective-permute-start.19 = (bf16[256,256]{1,0:T(8,128)(2,1)S(1)}, bf16[256,256]{1,0:T(8,128)(2,1)S(1)}, u32[]{:S(2)}, u32[]{:S(2)}) collective-permute-start(bf16[256,256]{1,0:T(8,128)(2,1)S(1)} %get-tuple-element.19), channel_id=1, source_target_pairs={{0,8},{8,0},{1,9},{9,1},{2,10},{10,2},{3,11},{11,3},{4,12},{12,4},... | collective-permute-start | bytes 393224 | tf_op jit(solution)/shard_map/ppermute | solution.py:222
  (7 other events, 240.9 us)
